TPU v7x, 32 devices: a whole 2x2x4 slice. The times are simulated.
32 devices in a mesh: dp: 8 (over z, x), tensor: 4 (over y, core).
Axes of the slice: x: 2, y: 2, z: 4, core: 2. Of those that a mesh axis runs over, the one named last changes fastest.
Arguments:
- layer_in: bfloat16 [16384, 1024], P(('dp', 'tensor')), may hold values from -6 to 6
- cotangent: bfloat16 [16384, 1024], P(('dp', 'tensor')), may hold values from -6 to 6
- lengths: int32 [8], P('dp'), may hold values from 256 to 2048, as said below
- languages: int32 [8], P('dp'), may hold values from 0 to 45
- lang_weight: float32 [46], replicated, may hold values from 0.3 to 3
- ln1_gain: float32 [1024], replicated, may hold values from 0.5 to 1.5
- ln1_bias: float32 [1024], replicated, may hold values from -2.5 to 2.5
- w_qkv: bfloat16 [1024, 3072], P(None, 'tensor'), may hold values from -0.1875 to 0.1875
- b_qv: float32 [2048], P('tensor'), may hold values from -2.5 to 2.5
- w_out: bfloat16 [1024, 1024], P('tensor'), may hold values from -1.5 to 1.5
- b_out: float32 [1024], replicated, may hold values from -2.5 to 2.5
- ln2_gain: float32 [1024], replicated, may hold values from 0.5 to 1.5
- ln2_bias: float32 [1024], replicated, may hold values from -2.5 to 2.5
- w_up: bfloat16 [1024, 4096], P(None, 'tensor'), may hold values from -0.1875 to 0.1875
- b_up: float32 [4096], P('tensor'), may hold values from -2.5 to 2.5
- w_down: bfloat16 [4096, 1024], P('tensor'), may hold values from -0.09375 to 0.09375
- b_down: float32 [1024], replicated, may hold values from -2.5 to 2.5
Outputs:
- output: bfloat16 [16384, 1024], P(('dp', 'tensor'))
- grad_x: bfloat16 [16384, 1024], P(('dp', 'tensor'))
- g_ln1_gain: float32 [1024], replicated
- g_ln1_bias: float32 [1024], replicated
- g_w_qkv: float32 [1024, 3072], P(None, 'tensor')
- g_b_qv: float32 [2048], P('tensor')
- g_w_out: float32 [1024, 1024], P('tensor')
- g_b_out: float32 [1024], replicated
- g_ln2_gain: float32 [1024], replicated
- g_ln2_bias: float32 [1024], replicated
- g_w_up: float32 [1024, 4096], P(None, 'tensor')
- g_b_up: float32 [4096], P('tensor')
- g_w_down: float32 [4096, 1024], P('tensor')
- g_b_down: float32 [1024], replicated
Inputs may be any that keep to these rules, and one draw needn't show every extreme that they name: `lengths`: rows of languages 0 to 7 have all 2048 tokens; some row has 2048 tokens and some row 256.
All inputs are finite; a program needn't handle non-finite values.
Results may differ from a plain program's by a relative error of at most 0.019.
Values may be sent and summed in bfloat16 or wider, within the bound.
No kernel may reach another device: no remote copies, remote signals or barrier semaphores. Data moves between devices by JAX's collectives and lax.ppermute only.
A program may use at most 192 MiB of HBM per device.

v0:
```python
import jax
import jax.numpy as jnp
from jax import lax
from jax.sharding import PartitionSpec as P

HEADS = 16
HD = 64


eps = 1e-05
block_most = 512


def layer_norm(values, gain, bias):
    centre = jnp.mean(values, axis=-1, keepdims=True)
    shifted = values - centre
    spread = jnp.mean(shifted * shifted, axis=-1, keepdims=True)
    factor = lax.rsqrt(spread + eps)
    unit_rows = shifted * factor
    return (unit_rows * gain + bias, unit_rows, factor)


def norm_back(grad_rows, unit_rows, factor, gain):
    scaled = grad_rows * gain
    inner = jnp.mean(scaled * unit_rows, axis=-1, keepdims=True)
    return factor * (scaled - jnp.mean(scaled, axis=-1, keepdims=True) - unit_rows * inner)


def cross_rows(left, right):
    return lax.dot_general(
        left, right, (((0,), (0,)), ((), ())), preferred_element_type=jnp.float32
    )


def times_trans(left, right):
    return lax.dot_general(
        left, right, (((1,), (1,)), ((), ())), preferred_element_type=jnp.float32
    )


def block_rows():
    return block_most


def qkv_bias(pairs):
    return jnp.stack([pairs[:, 0], jnp.zeros_like(pairs[:, 0]), pairs[:, 1]], axis=1)


def masked_scores(query_block, keys, start, length, slopes):
    query_pos = start + jnp.arange(query_block.shape[1], dtype=jnp.int32)
    key_pos = jnp.arange(keys.shape[1], dtype=jnp.int32)
    scores = jnp.einsum(
        "hqe,hke->hqk", query_block, keys, preferred_element_type=jnp.float32
    ) * keys.shape[2] ** (-0.5)
    offsets = (key_pos[None, :] - query_pos[:, None]).astype(jnp.float32)
    scores = scores + slopes[:, None, None] * offsets[None]
    allowed = (key_pos[None, :] <= query_pos[:, None]) & (key_pos[None, :] < length)
    return jnp.where(allowed[None], scores, -jnp.inf)


def attend_forward(query, keys, values, length, slopes):
    span = query.shape[1]
    block = block_rows()

    def forward_block(start):
        query_block = lax.dynamic_slice_in_dim(query, start, block, 1)
        scores = masked_scores(query_block, keys, start, length, slopes)
        highest = jnp.max(scores, axis=-1, keepdims=True)
        expos = jnp.exp(scores - highest)
        denom = jnp.sum(expos, axis=-1, keepdims=True)
        probs_b = (expos / denom).astype(jnp.bfloat16)
        result = jnp.einsum("hqk,hke->hqe", probs_b, values, preferred_element_type=jnp.float32)
        return (result, (highest + jnp.log(denom))[..., 0])

    starts = jnp.arange(span // block, dtype=jnp.int32) * block
    results, log_total = lax.map(forward_block, starts)
    heads_count = query.shape[0]
    return (
        results.transpose(1, 0, 2, 3).reshape(query.shape),
        log_total.transpose(1, 0, 2).reshape(heads_count, span),
    )


def attend_backward(query, keys, values, grad_heads, log_total, length, slopes):
    span = query.shape[1]
    block = block_rows()
    scale = keys.shape[2] ** (-0.5)

    def backward_block(carry, start):
        grad_keys, grad_values = carry
        query_block = lax.dynamic_slice_in_dim(query, start, block, 1)
        grad_block = lax.dynamic_slice_in_dim(grad_heads, start, block, 1)
        log_block = lax.dynamic_slice_in_dim(log_total, start, block, 1)
        scores = masked_scores(query_block, keys, start, length, slopes)
        probs = jnp.exp(scores - log_block[..., None])
        grad_probs = jnp.einsum(
            "hqe,hke->hqk", grad_block, values, preferred_element_type=jnp.float32
        )
        grad_scores = (
            probs * (grad_probs - jnp.sum(probs * grad_probs, axis=-1, keepdims=True))
        ).astype(jnp.bfloat16)
        grad_query = (
            jnp.einsum("hqk,hke->hqe", grad_scores, keys, preferred_element_type=jnp.float32)
            * scale
        )
        grad_keys = (
            grad_keys
            + jnp.einsum(
                "hqk,hqe->hke", grad_scores, query_block, preferred_element_type=jnp.float32
            )
            * scale
        )
        grad_values = grad_values + jnp.einsum(
            "hqk,hqe->hke",
            probs.astype(jnp.bfloat16),
            grad_block,
            preferred_element_type=jnp.float32,
        )
        return ((grad_keys, grad_values), grad_query)

    starts = jnp.arange(span // block, dtype=jnp.int32) * block
    empty = jnp.zeros(keys.shape, jnp.float32)
    (grad_keys, grad_values), grad_query = lax.scan(backward_block, (empty, empty), starts)
    return (grad_query.transpose(1, 0, 2, 3).reshape(query.shape), grad_keys, grad_values)


def body(
    layer_in,
    cotangent,
    lengths,
    languages,
    lang_weight,
    ln1_gain,
    ln1_bias,
    w_qkv,
    b_qv,
    w_out,
    b_out,
    ln2_gain,
    ln2_bias,
    w_up,
    b_up,
    w_down,
    b_down,
):
    groups = lax.axis_size("tensor")
    place = lax.axis_index("tensor")
    own_rows = layer_in.shape[0]
    all_rows = own_rows * groups
    seq_count = lengths.shape[0]
    seq_len = all_rows // seq_count
    head_dim = HD
    local_heads = w_out.shape[0] // head_dim
    head_ids = (place * local_heads + jnp.arange(local_heads, dtype=jnp.int32)).astype(jnp.float32)
    slopes = jnp.exp2(-8.0 * (head_ids + 1.0) / HEADS)
    in_float = layer_in.astype(jnp.float32)
    normed1, unit1, factor1 = layer_norm(in_float, ln1_gain, ln1_bias)
    normed1_b = normed1.astype(jnp.bfloat16)
    mixed = jnp.dot(
        lax.all_gather(normed1_b, "tensor", axis=0, tiled=True),
        w_qkv,
        preferred_element_type=jnp.float32,
    )
    bias_three = qkv_bias(b_qv.reshape(local_heads, 2, head_dim))
    mixed_b = (mixed.reshape(all_rows, local_heads, 3, head_dim) + bias_three[None]).astype(
        jnp.bfloat16
    )
    per_seq = mixed_b.reshape(seq_count, seq_len, local_heads, 3, head_dim).transpose(0, 3, 2, 1, 4)

    def forward_seq(item):
        parts, length = item
        return attend_forward(parts[0], parts[1], parts[2], length, slopes)

    heads_out, log_total = lax.map(forward_seq, (per_seq, lengths))
    heads_b = (
        heads_out.astype(jnp.bfloat16)
        .transpose(0, 2, 1, 3)
        .reshape(all_rows, local_heads * head_dim)
    )
    attn_sum = lax.psum_scatter(
        jnp.dot(heads_b, w_out, preferred_element_type=jnp.float32).astype(jnp.bfloat16),
        "tensor",
        scatter_dimension=0,
        tiled=True,
    ).astype(jnp.float32)
    middle = in_float + attn_sum + b_out
    normed2, unit2, factor2 = layer_norm(middle, ln2_gain, ln2_bias)
    normed2_b = normed2.astype(jnp.bfloat16)
    pre_act = (
        jnp.dot(
            lax.all_gather(normed2_b, "tensor", axis=0, tiled=True),
            w_up,
            preferred_element_type=jnp.float32,
        )
        + b_up
    )
    gelu_out, gelu_pull = jax.vjp(lambda inputs: jax.nn.gelu(inputs, approximate=True), pre_act)
    active_b = gelu_out.astype(jnp.bfloat16)
    output = (
        middle
        + lax.psum_scatter(
            jnp.dot(active_b, w_down, preferred_element_type=jnp.float32).astype(jnp.bfloat16),
            "tensor",
            scatter_dimension=0,
            tiled=True,
        ).astype(jnp.float32)
        + b_down
    )
    row_ids = place * own_rows + jnp.arange(own_rows, dtype=jnp.int32)
    seq_ids = row_ids // seq_len
    positions = row_ids - seq_ids * seq_len
    seq_hit = seq_ids[:, None] == jnp.arange(seq_count, dtype=jnp.int32)[None, :]
    row_length = jnp.sum(jnp.where(seq_hit, lengths[None, :], 0), axis=1)
    row_lang = jnp.sum(jnp.where(seq_hit, languages[None, :], 0), axis=1)
    lang_hit = row_lang[:, None] == jnp.arange(lang_weight.shape[0], dtype=jnp.int32)[None, :]
    row_weight = jnp.sum(jnp.where(lang_hit, lang_weight[None, :], 0.0), axis=1)
    live = jnp.where(positions < row_length, row_weight, 0.0)
    grad_top = cotangent.astype(jnp.float32) * live[:, None]
    g_b_down = jnp.sum(grad_top, axis=0)
    grad_full = lax.all_gather(grad_top.astype(jnp.bfloat16), "tensor", axis=0, tiled=True)
    g_w_down = cross_rows(active_b, grad_full)
    grad_active = times_trans(grad_full, w_down)
    grad_pre_b = gelu_pull(grad_active)[0].astype(jnp.bfloat16)
    g_b_up = jnp.sum(grad_pre_b.astype(jnp.float32), axis=0)
    rows_here = grad_pre_b
    g_w_up = cross_rows(lax.all_gather(normed2_b, "tensor", axis=0, tiled=True), rows_here)
    grad_norm2 = lax.psum_scatter(
        times_trans(grad_pre_b, w_up).astype(jnp.bfloat16),
        "tensor",
        scatter_dimension=0,
        tiled=True,
    ).astype(jnp.float32)
    g_ln2_gain = jnp.sum(grad_norm2 * unit2, axis=0)
    g_ln2_bias = jnp.sum(grad_norm2, axis=0)
    grad_middle = grad_top + norm_back(grad_norm2, unit2, factor2, ln2_gain)
    g_b_out = jnp.sum(grad_middle, axis=0)
    grad_mid_b = grad_middle.astype(jnp.bfloat16)
    grad_mid_full = lax.all_gather(grad_mid_b, "tensor", axis=0, tiled=True)
    g_w_out = cross_rows(heads_b, grad_mid_full)
    grad_heads_b = times_trans(grad_mid_full, w_out).astype(jnp.bfloat16)
    grad_seq = grad_heads_b.reshape(seq_count, seq_len, local_heads, head_dim).transpose(0, 2, 1, 3)

    def backward_seq(item):
        parts, grad_part, log_part, length = item
        return attend_backward(parts[0], parts[1], parts[2], grad_part, log_part, length, slopes)

    grad_query, grad_key, grad_value = lax.map(
        backward_seq, (per_seq, grad_seq, log_total, lengths)
    )
    grad_parts = jnp.stack([grad_query, grad_key, grad_value], axis=1)
    grad_mixed_b = (
        grad_parts.transpose(0, 3, 2, 1, 4)
        .reshape(all_rows, local_heads * 3 * head_dim)
        .astype(jnp.bfloat16)
    )
    column_sums = jnp.sum(grad_mixed_b.astype(jnp.float32), axis=0).reshape(
        local_heads, 3, head_dim
    )
    g_b_qv = jnp.stack([column_sums[:, 0], column_sums[:, 2]], axis=1).reshape(-1)
    rows_here = grad_mixed_b
    g_w_qkv = cross_rows(lax.all_gather(normed1_b, "tensor", axis=0, tiled=True), rows_here)
    grad_norm1 = lax.psum_scatter(
        times_trans(grad_mixed_b, w_qkv).astype(jnp.bfloat16),
        "tensor",
        scatter_dimension=0,
        tiled=True,
    ).astype(jnp.float32)
    g_ln1_gain = jnp.sum(grad_norm1 * unit1, axis=0)
    g_ln1_bias = jnp.sum(grad_norm1, axis=0)
    grad_input = grad_middle + norm_back(grad_norm1, unit1, factor1, ln1_gain)
    weights = (
        lax.psum(g_w_qkv.astype(jnp.bfloat16), "dp").astype(jnp.float32),
        lax.psum(g_b_qv.astype(jnp.bfloat16), "dp").astype(jnp.float32),
        lax.psum(g_w_out.astype(jnp.bfloat16), "dp").astype(jnp.float32),
        lax.psum(g_w_up.astype(jnp.bfloat16), "dp").astype(jnp.float32),
        lax.psum(g_b_up.astype(jnp.bfloat16), "dp").astype(jnp.float32),
        lax.psum(g_w_down.astype(jnp.bfloat16), "dp").astype(jnp.float32),
    )
    shared = lax.psum(
        (g_ln1_gain, g_ln1_bias, g_b_out, g_ln2_gain, g_ln2_bias, g_b_down), ("dp", "tensor")
    )
    return (
        output.astype(jnp.bfloat16),
        grad_input.astype(jnp.bfloat16),
        shared[0],
        shared[1],
        weights[0],
        weights[1],
        weights[2],
        shared[2],
        shared[3],
        shared[4],
        weights[3],
        weights[4],
        weights[5],
        shared[5],
    )


def solution(mesh):
    in_specs = (
        P(("dp", "tensor"), None),
        P(("dp", "tensor"), None),
        P("dp"),
        P("dp"),
        P(),
        P(),
        P(),
        P(None, "tensor"),
        P("tensor"),
        P("tensor", None),
        P(),
        P(),
        P(),
        P(None, "tensor"),
        P("tensor"),
        P("tensor", None),
        P(),
    )
    out_specs = (
        P(("dp", "tensor"), None),
        P(("dp", "tensor"), None),
        P(),
        P(),
        P(None, "tensor"),
        P("tensor"),
        P("tensor", None),
        P(),
        P(),
        P(),
        P(None, "tensor"),
        P("tensor"),
        P("tensor", None),
        P(),
    )
    return jax.shard_map(body, mesh=mesh, in_specs=in_specs, out_specs=out_specs, check_vma=False)
```

profile of v0, /device:TPU:0, one launch (start us, length us, event | category | flops | bytes accessed | tf_op | source)
XLA Modules:
  0.0 1035.9 jit_solution(2467794752946454012)
XLA Ops:
  14.1 37.0 %all-gather.5.cloned.1.call-done = bf16[2048,1024]{1,0:T(8,128)(2,1)} async-done(((bf16[512,1024]{1,0:T(8,128)(2,1)}), bf16[2048,1024]{1,0:T(8,128)(2,1)}) %all-gather.5.cloned.1.call-update) | async-done | bytes 4194320 | tf_op jit(solution)/shard_map/all_gather | solution.py:160
  51.1 5.8 fusion.82
  60.2 106.7 %while.48 = (s32[]{:T(128)}, bf16[4,4,512,64]{2,3,1,0:T(8,128)(2,1)}, f32[4,4,512]{2,1,0:T(4,128)S(1)}, s32[4]{0:T(128)S(1)}, s32[]{:T(128)}, /*index=5*/bf16[4,...) while((s32[]{:T(128)}, ...), condition=%wide.region_5.6_spmd.clone, body=%wide.region_2.5_spmd.clone.sunk | while | flops 1153434112 | bytes 99428696 | solution.py:76
  65.4 6.9 fusion.136
  72.4 5.8 fusion.137
  78.2 8.8 fusion.138
  92.1 6.9 fusion.136
  104.9 8.8 fusion.138
  118.8 6.9 fusion.136
  125.7 5.8 fusion.137
  131.5 8.8 fusion.138
  145.4 6.9 fusion.136
  152.3 5.8 fusion.137
  158.1 8.8 fusion.138
  177.4 44.6 %reduce-scatter.5.cloned.1.call-done = bf16[512,1024]{1,0:T(8,128)(2,1)} async-done(((bf16[2048,1024]{1,0:T(8,128)(2,1)}), bf16[512,1024]{1,0:T(8,128)(2,1)}) %reduce-scatter.5.cloned.1.call-update) | async-done | bytes 1048592 | tf_op jit(solution)/shard_map/reduce_scatter | solution.py:180
  231.2 30.6 %all-gather.7.cloned.1.call-done = bf16[2048,1024]{1,0:T(8,128)(2,1)} async-done(((bf16[512,1024]{1,0:T(8,128)(2,1)}), bf16[2048,1024]{1,0:T(8,128)(2,1)}) %all-gather.7.cloned.1.call-update) | async-done | bytes 4194320 | tf_op jit(solution)/shard_map/all_gather | solution.py:191
  261.8 11.4 %fusion.83 = f32[2048,1024]{1,0:T(8,128)} fusion(bf16[2048,1024]{1,0:T(8,128)(2,1)} %all-gather.7.cloned.1.call-done, bf16[1024,1024]{1,0:T(8,128)(2,1)} %param.34), kind=kOutput, calls=%fused_computation.151 | convolution fusion | flops 4294967296 | bytes 14680064 | tf_op jit(solution)/shard_map/dot_general | solution.py:190
  273.2 25.2 %all-gather.9.cloned.1.call-done = bf16[2048,1024]{1,0:T(8,128)(2,1)} async-done(((bf16[512,1024]{1,0:T(8,128)(2,1)}), bf16[2048,1024]{1,0:T(8,128)(2,1)}) %all-gather.9.cloned.1.call-update) | async-done | bytes 4194320 | tf_op jit(solution)/shard_map/all_gather | solution.py:220
  298.4 13.8 %fusion.76 = (bf16[1024]{0:T(1024)(128)(2,1)}, bf16[2048,1024]{1,0:T(8,128)(2,1)S(1)}) fusion(f32[2048,1024]{1,0:T(8,128)} %fusion.83, f32[1024]{0:T(1024)S(1)} %copy-done.50, bf16[2048,1024]{1,0:T(8,128)(2,1)} %all-gather.9.cloned.1.call-done, bf16[1024,1024]{1,0:T(8,128)(2,1)S(1)} %copy-done), kind=kOutput, calls=%fused_computation.146 | convolution fusion | flops 4341103616 | bytes 18880512 | tf_op jit(solution)/shard_map/dot_general | solution.py:36
  314.1 6.2 convolution_convert_fusion.2
  320.4 11.2 %convolution_convert_fusion.3 = bf16[2048,1024]{1,0:T(8,128)(2,1)} fusion(bf16[1024,1024]{1,0:T(8,128)(2,1)S(1)} %copy-done, f32[2048,1024]{1,0:T(8,128)} %fusion.83, f32[1024]{0:T(1024)S(1)} %copy-done.50), kind=kOutput, calls=%fused_computation.65 | convolution fusion | flops 4318035968 | bytes 14684160 | tf_op jit(solution)/shard_map/dot_general | solution.py:202
  331.7 33.4 %reduce-scatter.9.cloned.1.call-done = bf16[512,1024]{1,0:T(8,128)(2,1)} async-done(((bf16[2048,1024]{1,0:T(8,128)(2,1)}), bf16[512,1024]{1,0:T(8,128)(2,1)}) %reduce-scatter.9.cloned.1.call-update) | async-done | bytes 1048592 | tf_op jit(solution)/shard_map/reduce_scatter | solution.py:227
  368.1 44.5 %reduce-scatter.7.cloned.1.call-done = bf16[512,1024]{1,0:T(8,128)(2,1)} async-done(((bf16[2048,1024]{1,0:T(8,128)(2,1)}), bf16[512,1024]{1,0:T(8,128)(2,1)}) %reduce-scatter.7.cloned.1.call-update) | async-done | bytes 1048592 | tf_op jit(solution)/shard_map/reduce_scatter | solution.py:201
  419.5 9.5 convolution_convert_fusion.6
  429.1 11.0 %convolution_convert_fusion.5 = bf16[1024,1024]{1,0:T(8,128)(2,1)} fusion(bf16[2048,1024]{1,0:T(8,128)(2,1)S(1)} %copy-done.47, f32[2048,1024]{1,0:T(8,128)} %fusion.83, f32[1024]{0:T(1024)S(1)} %copy-done.50), kind=kOutput, calls=%fused_computation.109 | convolution fusion | flops 4316987392 | bytes 14684160 | tf_op jit(solution)/shard_map/dot_general | solution.py:30
  440.1 14.0 %all-gather.11.cloned.1.call-done = bf16[2048,1024]{1,0:T(8,128)(2,1)} async-done(((bf16[512,1024]{1,0:T(8,128)(2,1)}), bf16[2048,1024]{1,0:T(8,128)(2,1)}) %all-gather.11.cloned.1.call-update) | async-done | bytes 4194320 | tf_op jit(solution)/shard_map/all_gather | solution.py:238
  459.6 244.7 %while.49 = (s32[]{:T(128)}, f32[4,2048,64]{1,2,0:T(8,128)}, f32[4,2048,64]{1,2,0:T(8,128)}, bf16[4,4,512,64]{2,3,1,0:T(8,128)(2,1)}, s32[4]{0:T(128)S(1)}, /*in...) while((s32[]{:T(128)}, f32[4,2048,64]{1,2,0:T(8,128)}, ...), condition=%wide.region_16.17_spmd.clone, body=%wide.region_14.16_spmd.clone.sunk | while | flops 2737439232 | bytes 296274944 | solution.py:123
  464.9 9.3 fusion.148
  474.2 14.5 %multiply_reduce_fusion.3 = (f32[4,512]{1,0:T(4,128)S(1)}, f32[4,512,2048]{2,1,0:T(8,128)}) fusion(f32[4,512,2048]{2,1,0:T(8,128)} %fusion.148, f32[4,512]{1,0:T(4,128)S(1)} %constant_dynamic-slice_fusion.2, f32[512,2048]{1,0:T(8,128)S(1)} %subtract_convert_fusion.5, f32[4]{0:T(128)S(1)} %multiply_exponential_fusion.5, ...), kind=kOutput, calls=%fused_computation.23.clone.1 | convolution fusion | flops 566228992 | bytes 40124932 | tf_op jit(solution)/shard_map/while/body/eval_jaxpr/while/body/eval_jaxpr/hqe,hke->hqk/dot_general | solution.py:52
  488.6 15.0 %multiply_convert_fusion.5 = bf16[4,512,2048]{2,1,0:T(8,128)(2,1)} fusion(f32[4,512,2048]{2,1,0:T(8,128)} %get-tuple-element.456, f32[4,512,2048]{2,1,0:T(8,128)} %fusion.148, f32[4,512]{1,0:T(4,128)S(1)} %get-tuple-element.457), kind=kLoop, calls=%fused_computation.22.clone.1 | loop fusion | flops 12582912 | bytes 41951232 | tf_op jit(solution)/shard_map/while/body/eval_jaxpr/while/body/eval_jaxpr/convert_element_type | solution.py:101
  510.8 6.8 fusion.152
  526.0 9.3 fusion.148
  535.2 14.5 %multiply_reduce_fusion.3 = (f32[4,512]{1,0:T(4,128)S(1)}, f32[4,512,2048]{2,1,0:T(8,128)}) fusion(f32[4,512,2048]{2,1,0:T(8,128)} %fusion.148, f32[4,512]{1,0:T(4,128)S(1)} %constant_dynamic-slice_fusion.2, f32[512,2048]{1,0:T(8,128)S(1)} %subtract_convert_fusion.5, f32[4]{0:T(128)S(1)} %multiply_exponential_fusion.5, ...), kind=kOutput, calls=%fused_computation.23.clone.1 | convolution fusion | flops 566228992 | bytes 40124932 | tf_op jit(solution)/shard_map/while/body/eval_jaxpr/while/body/eval_jaxpr/hqe,hke->hqk/dot_general | solution.py:52
  549.7 15.0 %multiply_convert_fusion.5 = bf16[4,512,2048]{2,1,0:T(8,128)(2,1)} fusion(f32[4,512,2048]{2,1,0:T(8,128)} %get-tuple-element.456, f32[4,512,2048]{2,1,0:T(8,128)} %fusion.148, f32[4,512]{1,0:T(4,128)S(1)} %get-tuple-element.457), kind=kLoop, calls=%fused_computation.22.clone.1 | loop fusion | flops 12582912 | bytes 41951232 | tf_op jit(solution)/shard_map/while/body/eval_jaxpr/while/body/eval_jaxpr/convert_element_type | solution.py:101
  571.8 6.8 fusion.152
  587.0 9.3 fusion.148
  596.3 14.5 %multiply_reduce_fusion.3 = (f32[4,512]{1,0:T(4,128)S(1)}, f32[4,512,2048]{2,1,0:T(8,128)}) fusion(f32[4,512,2048]{2,1,0:T(8,128)} %fusion.148, f32[4,512]{1,0:T(4,128)S(1)} %constant_dynamic-slice_fusion.2, f32[512,2048]{1,0:T(8,128)S(1)} %subtract_convert_fusion.5, f32[4]{0:T(128)S(1)} %multiply_exponential_fusion.5, ...), kind=kOutput, calls=%fused_computation.23.clone.1 | convolution fusion | flops 566228992 | bytes 40124932 | tf_op jit(solution)/shard_map/while/body/eval_jaxpr/while/body/eval_jaxpr/hqe,hke->hqk/dot_general | solution.py:52
  610.8 15.0 %multiply_convert_fusion.5 = bf16[4,512,2048]{2,1,0:T(8,128)(2,1)} fusion(f32[4,512,2048]{2,1,0:T(8,128)} %get-tuple-element.456, f32[4,512,2048]{2,1,0:T(8,128)} %fusion.148, f32[4,512]{1,0:T(4,128)S(1)} %get-tuple-element.457), kind=kLoop, calls=%fused_computation.22.clone.1 | loop fusion | flops 12582912 | bytes 41951232 | tf_op jit(solution)/shard_map/while/body/eval_jaxpr/while/body/eval_jaxpr/convert_element_type | solution.py:101
  632.9 6.8 fusion.152
  648.1 9.3 fusion.148
  657.4 14.5 %multiply_reduce_fusion.3 = (f32[4,512]{1,0:T(4,128)S(1)}, f32[4,512,2048]{2,1,0:T(8,128)}) fusion(f32[4,512,2048]{2,1,0:T(8,128)} %fusion.148, f32[4,512]{1,0:T(4,128)S(1)} %constant_dynamic-slice_fusion.2, f32[512,2048]{1,0:T(8,128)S(1)} %subtract_convert_fusion.5, f32[4]{0:T(128)S(1)} %multiply_exponential_fusion.5, ...), kind=kOutput, calls=%fused_computation.23.clone.1 | convolution fusion | flops 566228992 | bytes 40124932 | tf_op jit(solution)/shard_map/while/body/eval_jaxpr/while/body/eval_jaxpr/hqe,hke->hqk/dot_general | solution.py:52
  671.8 15.0 %multiply_convert_fusion.5 = bf16[4,512,2048]{2,1,0:T(8,128)(2,1)} fusion(f32[4,512,2048]{2,1,0:T(8,128)} %get-tuple-element.456, f32[4,512,2048]{2,1,0:T(8,128)} %fusion.148, f32[4,512]{1,0:T(4,128)S(1)} %get-tuple-element.457), kind=kLoop, calls=%fused_computation.22.clone.1 | loop fusion | flops 12582912 | bytes 41951232 | tf_op jit(solution)/shard_map/while/body/eval_jaxpr/while/body/eval_jaxpr/convert_element_type | solution.py:101
  693.9 6.8 fusion.152
  723.3 7.0 convolution_convert_fusion.1
  731.0 22.5 %all-reduce.1 = (bf16[512]{0:T(512)(128)(2,1)S(1)}, bf16[1024]{0:T(1024)(128)(2,1)S(1)}) all-reduce(bf16[512]{0:T(512)(128)(2,1)S(1)} %convert_element_type.190, bf16[1024]{0:T(1024)(128)(2,1)S(1)} %copy-done.43), channel_id=1, replica_groups=mesh['dp'=8,'tensor'=4] {'dp'}, use_global_device_ids=true, to_apply=%region_26.27 | all-reduce | flops 1536 | bytes 6144 | tf_op jit(solution)/shard_map/psum | solution.py:273
  754.7 182.3 %all-reduce.5.cloned.1.call-done = (bf16[1024,768]{1,0:T(8,128)(2,1)}, bf16[256,1024]{1,0:T(8,128)(2,1)}, bf16[1024,1024]{1,0:T(8,128)(2,1)}, bf16[1024,1024]{1,0:T(8,128)(2,1)}) async-done(((bf16[1024,768]{1,0:T(8,128)(2,1)}, bf16[256,1024]{1,0:T(8,128)(2,1)}, bf16[1024,1024]{1,0:T(8,128)(2,1)}, bf16[1024,1024]{1,0:T(8,128)(2,1)}), (bf16[1024,768]{1,0:T(8,128)(2,1)}, bf16[256,1024]{1,0:T(8,128)(2,1)}, ...) | async-done | bytes 6291472 | tf_op jit(solution)/shard_map/psum | solution.py:272
  947.9 35.0 %reduce-scatter.11.cloned.1.call-done = bf16[512,1024]{1,0:T(8,128)(2,1)} async-done(((bf16[2048,1024]{1,0:T(8,128)(2,1)}), bf16[512,1024]{1,0:T(8,128)(2,1)}) %reduce-scatter.11.cloned.1.call-update) | async-done | bytes 1048592 | tf_op jit(solution)/shard_map/reduce_scatter | solution.py:262
  985.3 40.0 %all-reduce = (f32[1024]{0:T(1024)}, f32[1024]{0:T(1024)}, f32[1024]{0:T(1024)}, f32[1024]{0:T(1024)}, f32[1024]{0:T(1024)}, /*index=5*/f32[1024]{0:T(1024)}) all-reduce(f32[1024]{0:T(1024)S(1)} %get-tuple-element.241, f32[1024]{0:T(1024)S(1)} %get-tuple-element.246, ...), channel_id=1, replica_groups=mesh['dp'=8,'tensor'=4] {'dp','tensor'}, use_global_device_ids=true, to_apply=%region_21.22 | all-reduce | flops 6144 | bytes 49152 | tf_op jit(solution)/shard_map/psum | solution.py:279
  (314 shorter events, 155.2 us)
Async XLA Ops:
  7.2 291.2 %copy-start = (bf16[1024,1024]{1,0:T(8,128)(2,1)S(1)}, bf16[1024,1024]{1,0:T(8,128)(2,1)}, u32[]{:S(2)}) copy-start(bf16[1024,1024]{1,0:T(8,128)(2,1)} %param.36) | copy-start | bytes 6291460
  7.2 43.9 %all-gather.5.cloned.1.call-start = ((), (), s32[]{:S(2)}) async-start(), calls=%async_computation.4 | async-start | bytes 5242880 | tf_op jit(solution)/shard_map/all_gather | solution.py:160
  13.8 208.2 %reduce-scatter.5.cloned.1.call-start = ((), (), s32[]{:S(2)}) async-start(), calls=%async_computation.5 | async-start | bytes 5242880 | tf_op jit(solution)/shard_map/reduce_scatter | solution.py:180
  177.3 44.7 %copy-start.8 = (bf16[512,1024]{1,0:T(8,128)(2,1)S(1)}, bf16[512,1024]{1,0:T(8,128)(2,1)}, u32[]{:S(2)}) copy-start(bf16[512,1024]{1,0:T(8,128)(2,1)} %param.21) | copy-start | bytes 3145732
  177.3 44.7 %copy-start.29 = (f32[1024]{0:T(1024)S(1)}, f32[1024]{0:T(1024)}, u32[]{:S(2)}) copy-start(f32[1024]{0:T(1024)} %param.31) | copy-start | bytes 12292
  177.3 48.2 %copy-start.32 = (f32[1024]{0:T(1024)S(1)}, f32[1024]{0:T(1024)}, u32[]{:S(2)}) copy-start(f32[1024]{0:T(1024)} %param.32) | copy-start | bytes 12292
  177.3 48.2 %copy-start.41 = (f32[1024]{0:T(1024)S(1)}, f32[1024]{0:T(1024)}, u32[]{:S(2)}) copy-start(f32[1024]{0:T(1024)} %param.33) | copy-start | bytes 12292
  177.3 51.2 %copy-start.44 = (f32[46]{0:T(128)S(1)}, f32[46]{0:T(128)}, u32[]{:S(2)}) copy-start(f32[46]{0:T(128)} %param.25) | copy-start | bytes 556
  177.3 84.4 %all-gather.7.cloned.1.call-start = ((), (), s32[]{:S(2)}) async-start(), calls=%async_computation.6 | async-start | bytes 5242880 | tf_op jit(solution)/shard_map/all_gather | solution.py:191
  227.2 71.2 %all-gather.9.cloned.1.call-start = ((), (), s32[]{:S(2)}) async-start(), calls=%async_computation.8 | async-start | bytes 5242880 | tf_op jit(solution)/shard_map/all_gather | solution.py:220
  231.1 67.3 %copy-start.50 = (f32[1024]{0:T(1024)S(1)}, f32[1024]{0:T(1024)}, u32[]{:S(2)}) copy-start(f32[1024]{0:T(1024)} %param.35) | copy-start | bytes 12292
  231.1 134.0 %reduce-scatter.9.cloned.1.call-start = ((), (), s32[]{:S(2)}) async-start(), calls=%async_computation.9 | async-start | bytes 5242880 | tf_op jit(solution)/shard_map/reduce_scatter | solution.py:227
  298.4 15.8 %copy-start.48 = (bf16[1024,1024]{1,0:T(8,128)(2,1)S(1)}, bf16[1024,1024]{1,0:T(8,128)(2,1)}, u32[]{:S(2)}) copy-start(bf16[1024,1024]{1,0:T(8,128)(2,1)} %param.34) | copy-start | bytes 6291460
  320.4 92.2 %reduce-scatter.7.cloned.1.call-start = ((), (), s32[]{:S(2)}) async-start(), calls=%async_computation.7 | async-start | bytes 5242880 | tf_op jit(solution)/shard_map/reduce_scatter | solution.py:201
  331.6 33.5 %copy-start.17 = (bf16[512,1024]{1,0:T(8,128)(2,1)S(1)}, bf16[512,1024]{1,0:T(8,128)(2,1)}, u32[]{:S(2)}) copy-start(bf16[512,1024]{1,0:T(8,128)(2,1)} %reduce-scatter.5.cloned.1.call-done) | copy-start | bytes 3145732
  331.6 81.0 %copy-start.22 = (bf16[512,1024]{1,0:T(8,128)(2,1)S(1)}, bf16[512,1024]{1,0:T(8,128)(2,1)}, u32[]{:S(2)}) copy-start(bf16[512,1024]{1,0:T(8,128)(2,1)} %param.22) | copy-start | bytes 3145732
  331.6 81.0 %copy-start.40 = (f32[1024]{0:T(1024)S(1)}, f32[1024]{0:T(1024)}, u32[]{:S(2)}) copy-start(f32[1024]{0:T(1024)} %param.37) | copy-start | bytes 12292
  331.7 122.5 %all-gather.11.cloned.1.call-start = ((), (), s32[]{:S(2)}) async-start(), calls=%async_computation.10 | async-start | bytes 5242880 | tf_op jit(solution)/shard_map/all_gather | solution.py:238
  419.5 517.5 %all-reduce.5.cloned.1.call-start = ((), (), s32[]{:S(2)}) async-start(), calls=%async_computation.12 | async-start | bytes 12582912 | tf_op jit(solution)/shard_map/psum | solution.py:272
  419.5 9.5 copy-start.47
  429.0 25.1 %copy-start.28 = (bf16[256,1024]{1,0:T(8,128)(2,1)S(1)}, bf16[256,1024]{1,0:T(8,128)(2,1)}, u32[]{:S(2)}) copy-start(bf16[256,1024]{1,0:T(8,128)(2,1)} %param.30) | copy-start | bytes 1572868
  440.1 19.6 %copy-start.6 = (bf16[4,2048,64]{1,2,0:T(8,128)(2,1)S(1)}, bf16[4,2048,64]{1,2,0:T(8,128)(2,1)}, u32[]{:S(2)}) copy-start(bf16[4,2048,64]{1,2,0:T(8,128)(2,1)} %get-tuple-element.555) | copy-start | bytes 3145732
  440.1 19.6 %copy-start.15 = (bf16[4,2048,64]{1,2,0:T(8,128)(2,1)S(1)}, bf16[4,2048,64]{1,2,0:T(8,128)(2,1)}, u32[]{:S(2)}) copy-start(bf16[4,2048,64]{1,2,0:T(8,128)(2,1)} %get-tuple-element.556) | copy-start | bytes 3145732
  464.9 9.3 copy-start.19
  488.6 18.4 %copy-start.2 = (f32[4,512,2048]{2,1,0:T(8,128)S(1)}, f32[4,512,2048]{2,1,0:T(8,128)}, u32[]{:S(2)}) copy-start(f32[4,512,2048]{2,1,0:T(8,128)} %get-tuple-element.456) | copy-start | bytes 50331652 | tf_op jit(solution)/shard_map/while/body/eval_jaxpr/while
  488.6 19.0 %copy-start.13 = (f32[4,2048,64]{1,2,0:T(8,128)S(1)}, f32[4,2048,64]{1,2,0:T(8,128)}, u32[]{:S(2)}) copy-start(f32[4,2048,64]{1,2,0:T(8,128)} %get-tuple-element.511) | copy-start | bytes 6291460 | tf_op jit(solution)/shard_map/while/body/eval_jaxpr/while
  507.7 10.0 copy-start.10
  526.0 9.3 copy-start.19
  549.7 18.4 %copy-start.2 = (f32[4,512,2048]{2,1,0:T(8,128)S(1)}, f32[4,512,2048]{2,1,0:T(8,128)}, u32[]{:S(2)}) copy-start(f32[4,512,2048]{2,1,0:T(8,128)} %get-tuple-element.456) | copy-start | bytes 50331652 | tf_op jit(solution)/shard_map/while/body/eval_jaxpr/while
  549.7 19.0 %copy-start.13 = (f32[4,2048,64]{1,2,0:T(8,128)S(1)}, f32[4,2048,64]{1,2,0:T(8,128)}, u32[]{:S(2)}) copy-start(f32[4,2048,64]{1,2,0:T(8,128)} %get-tuple-element.511) | copy-start | bytes 6291460 | tf_op jit(solution)/shard_map/while/body/eval_jaxpr/while
  568.7 10.0 copy-start.10
  587.0 9.3 copy-start.19
  610.8 18.4 %copy-start.2 = (f32[4,512,2048]{2,1,0:T(8,128)S(1)}, f32[4,512,2048]{2,1,0:T(8,128)}, u32[]{:S(2)}) copy-start(f32[4,512,2048]{2,1,0:T(8,128)} %get-tuple-element.456) | copy-start | bytes 50331652 | tf_op jit(solution)/shard_map/while/body/eval_jaxpr/while
  610.8 19.0 %copy-start.13 = (f32[4,2048,64]{1,2,0:T(8,128)S(1)}, f32[4,2048,64]{1,2,0:T(8,128)}, u32[]{:S(2)}) copy-start(f32[4,2048,64]{1,2,0:T(8,128)} %get-tuple-element.511) | copy-start | bytes 6291460 | tf_op jit(solution)/shard_map/while/body/eval_jaxpr/while
  629.8 10.0 copy-start.10
  671.8 18.4 %copy-start.2 = (f32[4,512,2048]{2,1,0:T(8,128)S(1)}, f32[4,512,2048]{2,1,0:T(8,128)}, u32[]{:S(2)}) copy-start(f32[4,512,2048]{2,1,0:T(8,128)} %get-tuple-element.456) | copy-start | bytes 50331652 | tf_op jit(solution)/shard_map/while/body/eval_jaxpr/while
  671.8 19.0 %copy-start.13 = (f32[4,2048,64]{1,2,0:T(8,128)S(1)}, f32[4,2048,64]{1,2,0:T(8,128)}, u32[]{:S(2)}) copy-start(f32[4,2048,64]{1,2,0:T(8,128)} %get-tuple-element.511) | copy-start | bytes 6291460 | tf_op jit(solution)/shard_map/while/body/eval_jaxpr/while
  690.8 9.9 copy-start.10
  721.9 261.0 %reduce-scatter.11.cloned.1.call-start = ((), (), s32[]{:S(2)}) async-start(), calls=%async_computation.11 | async-start | bytes 5242880 | tf_op jit(solution)/shard_map/reduce_scatter | solution.py:262
  945.0 38.0 %copy-start.9 = (bf16[512,1024]{1,0:T(8,128)(2,1)S(1)}, bf16[512,1024]{1,0:T(8,128)(2,1)}, u32[]{:S(2)}) copy-start(bf16[512,1024]{1,0:T(8,128)(2,1)} %param.21) | copy-start | bytes 3145732
  945.0 38.0 %copy-start.31 = (f32[512]{0:T(512)S(1)}, f32[512]{0:T(512)}, u32[]{:S(2)}) copy-start(f32[512]{0:T(512)} %copy-done.30) | copy-start | bytes 6148
  945.0 38.0 %copy-start.33 = (f32[1024]{0:T(1024)S(1)}, f32[1024]{0:T(1024)}, u32[]{:S(2)}) copy-start(f32[1024]{0:T(1024)} %param.26) | copy-start | bytes 12292
  945.0 38.0 %copy-start.35 = (f32[512]{0:T(512)S(1)}, f32[512]{0:T(512)}, u32[]{:S(2)}) copy-start(f32[512]{0:T(512)} %copy-done.34) | copy-start | bytes 6148
  945.0 40.2 %copy-start.36 = (f32[1024]{0:T(1024)S(1)}, f32[1024]{0:T(1024)}, u32[]{:S(2)}) copy-start(f32[1024]{0:T(1024)} %get-tuple-element.303) | copy-start | bytes 12292
  945.0 40.2 %copy-start.37 = (f32[1024]{0:T(1024)S(1)}, f32[1024]{0:T(1024)}, u32[]{:S(2)}) copy-start(f32[1024]{0:T(1024)} %get-tuple-element.315) | copy-start | bytes 12292
  945.0 40.2 %copy-start.38 = (f32[1024]{0:T(1024)S(1)}, f32[1024]{0:T(1024)}, u32[]{:S(2)}) copy-start(f32[1024]{0:T(1024)} %get-tuple-element.239) | copy-start | bytes 12292
  945.0 40.2 %copy-start.39 = (f32[1024]{0:T(1024)S(1)}, f32[1024]{0:T(1024)}, u32[]{:S(2)}) copy-start(f32[1024]{0:T(1024)} %get-tuple-element.245) | copy-start | bytes 12292
  945.1 83.8 %copy-start.1 = (bf16[1024,1024]{1,0:T(8,128)(2,1)S(1)}, bf16[1024,1024]{1,0:T(8,128)(2,1)}, u32[]{:S(2)}) copy-start(bf16[1024,1024]{1,0:T(8,128)(2,1)} %param.36) | copy-start | bytes 6291460
  (49 other events, 197.8 us)
Sparse Core Ops, SparseCore 0:
  13.9 37.1 all-gather.4
  177.4 44.4 reduce-scatter.4
  227.3 34.4 all-gather.6
  263.8 34.4 all-gather.8
  320.5 44.5 reduce-scatter.8
  368.0 44.5 reduce-scatter.6
  419.6 34.4 all-gather.10
  722.0 214.8 all-reduce.4
  939.4 43.4 reduce-scatter.10
where the time goes:
time: 1040 us
  waiting for transfers between devices  447 us (43%)
  matrix products  297 us (29%)
  other arithmetic  145 us (14%)
  blocking collectives  62.5 us (6%)
  local copies, waits for them, and re-layouts  51.4 us (5%)
  loops' own time  17.1 us (2%)
  between operations  16 us (2%)
    psum x1, waiting for transfers between devices, body(): lax.psum(g_w_qkv.astype(jnp.bfloat16), 'dp').astype(jnp.float32)  182 us
    dot_general x8, matrix products, masked_scores(): jnp.einsum('hqe,hke->hqk', query_block, keys, preferred_element_type=jnp....  85.5 us
    convert_element_type x4, other arithmetic, backward_block(): grad_scores = (probs * (grad_probs - jnp.sum(probs * grad_probs, axis=-1,...  60 us
    reduce_scatter x1, waiting for transfers between devices, body(): lax.psum_scatter(jnp.dot(heads_b, w_out, preferred_element_type=jnp.float...  44.6 us
    reduce_scatter x1, waiting for transfers between devices, body(): lax.psum_scatter(jnp.dot(active_b, w_down, preferred_element_type=jnp.flo...  44.5 us
    psum x1, blocking collectives, body(): lax.psum((g_ln1_gain, g_ln1_bias, g_b_out, g_ln2_gain, g_ln2_bias, g_b_do...  40 us
    dot_general x4, matrix products, backward_block(): jnp.einsum('hqe,hke->hqk', grad_block, values, preferred_element_type=jnp...  37.1 us
    all_gather x1, waiting for transfers between devices, body(): lax.all_gather(normed1_b, 'tensor', axis=0, tiled=True)  37 us
  transfers between devices with their start and end apart: 9, of which 9 were waited for; matrix products, arithmetic and copies ran while one was open for 7% of the time, Pallas kernels for 0%

commit v1 on v0

--- a/solution.py
+++ b/solution.py
@@ -1,14 +1,204 @@
+import functools
 import jax
 import jax.numpy as jnp
 from jax import lax
 from jax.sharding import PartitionSpec as P
+from jax.experimental import pallas as pl
+from jax.experimental.pallas import tpu as pltpu
 
 HEADS = 16
 HD = 64
+LANES = 128
+F32 = jnp.float32
+BF16 = jnp.bfloat16
+
+
+def split3(x):
+    hi = x.astype(BF16)
+    rest = x - hi.astype(F32)
+    mid = rest.astype(BF16)
+    low = (rest - mid.astype(F32)).astype(BF16)
+    return hi.astype(F32), mid.astype(F32), low.astype(F32)
+
+
+def nt(a, b):
+    return lax.dot_general(a, b, (((1,), (1,)), ((), ())), preferred_element_type=F32)
+
+
+def nn(a, b):
+    return jnp.dot(a, b, preferred_element_type=F32)
+
+
+def at_lanes(lane, base, pairs):
+    out = base
+    for where, value in pairs:
+        out = jnp.where(lane == where, value, out)
+    return out
+
+
+def key_side(span, length):
+    pos = lax.broadcasted_iota(jnp.int32, (span, LANES), 0)
+    lane = lax.broadcasted_iota(jnp.int32, (span, LANES), 1)
+    low = (pos & 255).astype(F32)
+    high = (pos - (pos & 255)).astype(F32)
+    is_high = (lane == 64) | (lane == 66) | (lane == 68)
+    is_low = (lane == 65) | (lane == 67) | (lane == 69)
+    gone = jnp.where(pos < length, 0.0, -1e30)
+    out = jnp.where(is_high, high, jnp.where(is_low, low, 0.0))
+    out = jnp.where(lane == 70, gone, out)
+    return jnp.where((lane >= 71) & (lane <= 73), 1.0, out)
+
+
+def slope_side(lane, slope_parts):
+    s1, s2, s3 = slope_parts
+    out = jnp.where(lane < 66, s1, jnp.where(lane < 68, s2, s3))
+    out = jnp.where(lane == 70, 1.0, out)
+    return jnp.where((lane >= 64) & (lane <= 70), out, 0.0)
+
+
+def wide(x):
+    return jnp.concatenate([x, jnp.zeros_like(x)], axis=1)
+
+
+def fwd_kernel(bq, length_ref, slope_ref, mixed_ref, heads_ref, qa_ref, ka_ref, va_ref, o_ref):
+    span = mixed_ref.shape[0]
+    heads = heads_ref.shape[1] // HD
+    lane = lax.broadcasted_iota(jnp.int32, (1, LANES), 1)
+    keys = key_side(span, length_ref[0])
+    for h in range(heads):
+        base = h * 3 * HD
+        q = mixed_ref[:, base : base + HD].astype(F32) * (HD ** -0.5)
+        k = mixed_ref[:, base + HD : base + 2 * HD].astype(F32)
+        v = mixed_ref[:, base + 2 * HD : base + 3 * HD].astype(F32)
+        parts = [slope_ref[h, n] for n in range(3)]
+        qa_ref[h] = (wide(q) + slope_side(lane, parts)).astype(BF16)
+        ka_ref[h] = (wide(k) + keys).astype(BF16)
+        va_ref[h] = (wide(v) + jnp.where((lane >= 64) & (lane <= 66), 1.0, 0.0)).astype(BF16)
+
+    def one_head(h, carry):
+        for i in range(span // bq):
+            rows = slice(i * bq, (i + 1) * bq)
+            ext = (i + 1) * bq
+            q = qa_ref[h, rows, :]
+            s = nt(q, ka_ref[h, :ext, :])
+            tq = lax.broadcasted_iota(jnp.int32, (bq, bq), 0)
+            tk = lax.broadcasted_iota(jnp.int32, (bq, bq), 1)
+            diag = jnp.where(tk <= tq, s[:, i * bq :], -3e38)
+            s = jnp.concatenate([s[:, : i * bq], diag], axis=1) if i else diag
+            m = jnp.max(s, axis=1, keepdims=True)
+            p = jnp.exp(s - m).astype(BF16)
+            o = nn(p, va_ref[h, :ext, :])
+            total = o[:, HD : HD + 1]
+            out = o / total
+            lse = -(m + jnp.log(total))
+            l1, l2, l3 = split3(lse)
+            o_ref[h, rows, :] = out.astype(BF16)
+            qa_ref[h, rows, :] = at_lanes(lane, q.astype(F32), ((71, l1), (72, l2), (73, l3))).astype(BF16)
+        return carry
+
+    lax.fori_loop(0, heads, one_head, 0)
+    heads_ref[...] = jnp.concatenate([o_ref[h][:, :HD] for h in range(heads)], axis=1)
+
+
+def attend_forward(mixed, length, slope_parts, bq=256):
+    span = mixed.shape[0]
+    heads = mixed.shape[1] // (3 * HD)
+    vm = pl.BlockSpec(memory_space=pltpu.VMEM)
+    sm = pl.BlockSpec(memory_space=pltpu.SMEM)
+    aug = jax.ShapeDtypeStruct((heads, span, LANES), BF16)
+    return pl.pallas_call(
+        functools.partial(fwd_kernel, bq),
+        out_shape=(jax.ShapeDtypeStruct((span, heads * HD), BF16), aug, aug, aug),
+        in_specs=[sm, sm, vm],
+        out_specs=(vm, vm, vm, vm),
+        scratch_shapes=[pltpu.VMEM((heads, span, LANES), BF16)],
+        compiler_params=pltpu.CompilerParams(vmem_limit_bytes=60 << 20),
+        cost_estimate=pl.CostEstimate(
+            flops=4 * heads * span * span * LANES // 2, transcendentals=heads * span * span // 2,
+            bytes_accessed=heads * span * LANES * 10,
+        ),
+        name="attend_forward",
+    )(length, slope_parts, mixed)
+
+
+def bwd_kernel(bk, bq, qa_ref, ka_ref, va_ref, heads_ref, grad_ref, out_ref, da_ref, dqt_ref, dk_ref, dv_ref):
+    heads, span, _ = qa_ref.shape
+    lane = lax.broadcasted_iota(jnp.int32, (1, LANES), 1)
+    for h in range(heads):
+        o = heads_ref[:, h * HD : (h + 1) * HD].astype(F32)
+        g = grad_ref[:, h * HD : (h + 1) * HD].astype(F32)
+        d1, d2, d3 = split3(-jnp.sum(o * g, axis=1, keepdims=True))
+        da_ref[h] = at_lanes(lane, wide(g), ((64, d1), (65, d2), (66, d3))).astype(BF16)
+
+    def one_head(h, carry):
+        for j in range(span // bk):
+            cols = slice(j * bk, (j + 1) * bk)
+            k = ka_ref[h, cols, :]
+            v = va_ref[h, cols, :]
+            kt = k[:, :HD].T
+            start = j * bk
+            dk = jnp.zeros((bk, LANES), F32)
+            dv = jnp.zeros((bk, LANES), F32)
+            while start < span:
+                stop = min(span, (start // bq + 1) * bq)
+                q = qa_ref[h, start:stop, :]
+                d = da_ref[h, start:stop, :]
+                p = jnp.exp(nt(k, q))
+                if start == j * bk:
+                    tk = lax.broadcasted_iota(jnp.int32, (bk, stop - start), 0)
+                    tq = lax.broadcasted_iota(jnp.int32, (bk, stop - start), 1)
+                    p = jnp.where(tk <= tq, p, 0.0)
+                dp = nt(v, d)
+                ds = (p * dp).astype(BF16)
+                dv = dv + nn(p.astype(BF16), d)
+                dk = dk + nn(ds, q)
+                part = nn(kt, ds)
+                if j == 0:
+                    dqt_ref[h, :, start:stop] = part
+                else:
+                    dqt_ref[h, :, start:stop] += part
+                start = stop
+            dk_ref[h, cols, :] = dk
+            dv_ref[h, cols, :] = dv
+        return carry
+
+    lax.fori_loop(0, heads, one_head, 0)
+    pieces = []
+    for h in range(heads):
+        pieces += [dqt_ref[h].T * (HD ** -0.5), dk_ref[h][:, :HD], dv_ref[h][:, :HD]]
+    out_ref[...] = jnp.concatenate(pieces, axis=1).astype(BF16)
+
+
+def attend_backward(qa, ka, va, heads_b, grad_heads, bk=256, bq=1024):
+    heads, span, _ = qa.shape
+    vm = pl.BlockSpec(memory_space=pltpu.VMEM)
+    return pl.pallas_call(
+        functools.partial(bwd_kernel, bk, bq),
+        out_shape=jax.ShapeDtypeStruct((span, heads * 3 * HD), BF16),
+        in_specs=[vm] * 5,
+        out_specs=vm,
+        scratch_shapes=[
+            pltpu.VMEM((heads, span, LANES), BF16),
+            pltpu.VMEM((heads, HD, span), F32),
+            pltpu.VMEM((heads, span, LANES), F32),
+            pltpu.VMEM((heads, span, LANES), F32),
+        ],
+        compiler_params=pltpu.CompilerParams(vmem_limit_bytes=60 << 20),
+        cost_estimate=pl.CostEstimate(
+            flops=10 * heads * span * span * LANES // 2, transcendentals=heads * span * span // 2,
+            bytes_accessed=heads * span * LANES * 12,
+        ),
+        name="attend_backward",
+    )(qa, ka, va, heads_b, grad_heads)
+
+
+def slope_table(first, count, total):
+    ids = (first + jnp.arange(count, dtype=jnp.int32)).astype(F32)
+    slopes = jnp.exp2(-8.0 * (ids + 1.0) / total)
+    return jnp.stack(split3(slopes), axis=1)
 
 
 eps = 1e-05
-block_most = 512
 
 
 def layer_norm(values, gain, bias):
@@ -38,90 +228,8 @@
     )
 
 
-def block_rows():
-    return block_most
-
-
 def qkv_bias(pairs):
     return jnp.stack([pairs[:, 0], jnp.zeros_like(pairs[:, 0]), pairs[:, 1]], axis=1)
-
-
-def masked_scores(query_block, keys, start, length, slopes):
-    query_pos = start + jnp.arange(query_block.shape[1], dtype=jnp.int32)
-    key_pos = jnp.arange(keys.shape[1], dtype=jnp.int32)
-    scores = jnp.einsum(
-        "hqe,hke->hqk", query_block, keys, preferred_element_type=jnp.float32
-    ) * keys.shape[2] ** (-0.5)
-    offsets = (key_pos[None, :] - query_pos[:, None]).astype(jnp.float32)
-    scores = scores + slopes[:, None, None] * offsets[None]
-    allowed = (key_pos[None, :] <= query_pos[:, None]) & (key_pos[None, :] < length)
-    return jnp.where(allowed[None], scores, -jnp.inf)
-
-
-def attend_forward(query, keys, values, length, slopes):
-    span = query.shape[1]
-    block = block_rows()
-
-    def forward_block(start):
-        query_block = lax.dynamic_slice_in_dim(query, start, block, 1)
-        scores = masked_scores(query_block, keys, start, length, slopes)
-        highest = jnp.max(scores, axis=-1, keepdims=True)
-        expos = jnp.exp(scores - highest)
-        denom = jnp.sum(expos, axis=-1, keepdims=True)
-        probs_b = (expos / denom).astype(jnp.bfloat16)
-        result = jnp.einsum("hqk,hke->hqe", probs_b, values, preferred_element_type=jnp.float32)
-        return (result, (highest + jnp.log(denom))[..., 0])
-
-    starts = jnp.arange(span // block, dtype=jnp.int32) * block
-    results, log_total = lax.map(forward_block, starts)
-    heads_count = query.shape[0]
-    return (
-        results.transpose(1, 0, 2, 3).reshape(query.shape),
-        log_total.transpose(1, 0, 2).reshape(heads_count, span),
-    )
-
-
-def attend_backward(query, keys, values, grad_heads, log_total, length, slopes):
-    span = query.shape[1]
-    block = block_rows()
-    scale = keys.shape[2] ** (-0.5)
-
-    def backward_block(carry, start):
-        grad_keys, grad_values = carry
-        query_block = lax.dynamic_slice_in_dim(query, start, block, 1)
-        grad_block = lax.dynamic_slice_in_dim(grad_heads, start, block, 1)
-        log_block = lax.dynamic_slice_in_dim(log_total, start, block, 1)
-        scores = masked_scores(query_block, keys, start, length, slopes)
-        probs = jnp.exp(scores - log_block[..., None])
-        grad_probs = jnp.einsum(
-            "hqe,hke->hqk", grad_block, values, preferred_element_type=jnp.float32
-        )
-        grad_scores = (
-            probs * (grad_probs - jnp.sum(probs * grad_probs, axis=-1, keepdims=True))
-        ).astype(jnp.bfloat16)
-        grad_query = (
-            jnp.einsum("hqk,hke->hqe", grad_scores, keys, preferred_element_type=jnp.float32)
-            * scale
-        )
-        grad_keys = (
-            grad_keys
-            + jnp.einsum(
-                "hqk,hqe->hke", grad_scores, query_block, preferred_element_type=jnp.float32
-            )
-            * scale
-        )
-        grad_values = grad_values + jnp.einsum(
-            "hqk,hqe->hke",
-            probs.astype(jnp.bfloat16),
-            grad_block,
-            preferred_element_type=jnp.float32,
-        )
-        return ((grad_keys, grad_values), grad_query)
-
-    starts = jnp.arange(span // block, dtype=jnp.int32) * block
-    empty = jnp.zeros(keys.shape, jnp.float32)
-    (grad_keys, grad_values), grad_query = lax.scan(backward_block, (empty, empty), starts)
-    return (grad_query.transpose(1, 0, 2, 3).reshape(query.shape), grad_keys, grad_values)
 
 
 def body(
@@ -151,8 +259,6 @@
     seq_len = all_rows // seq_count
     head_dim = HD
     local_heads = w_out.shape[0] // head_dim
-    head_ids = (place * local_heads + jnp.arange(local_heads, dtype=jnp.int32)).astype(jnp.float32)
-    slopes = jnp.exp2(-8.0 * (head_ids + 1.0) / HEADS)
     in_float = layer_in.astype(jnp.float32)
     normed1, unit1, factor1 = layer_norm(in_float, ln1_gain, ln1_bias)
     normed1_b = normed1.astype(jnp.bfloat16)
@@ -162,21 +268,9 @@
         preferred_element_type=jnp.float32,
     )
     bias_three = qkv_bias(b_qv.reshape(local_heads, 2, head_dim))
-    mixed_b = (mixed.reshape(all_rows, local_heads, 3, head_dim) + bias_three[None]).astype(
-        jnp.bfloat16
-    )
-    per_seq = mixed_b.reshape(seq_count, seq_len, local_heads, 3, head_dim).transpose(0, 3, 2, 1, 4)
-
-    def forward_seq(item):
-        parts, length = item
-        return attend_forward(parts[0], parts[1], parts[2], length, slopes)
-
-    heads_out, log_total = lax.map(forward_seq, (per_seq, lengths))
-    heads_b = (
-        heads_out.astype(jnp.bfloat16)
-        .transpose(0, 2, 1, 3)
-        .reshape(all_rows, local_heads * head_dim)
-    )
+    mixed_b = (mixed + bias_three.reshape(1, -1)).astype(jnp.bfloat16)
+    slope_parts = slope_table(place * local_heads, local_heads, HEADS)
+    heads_b, query_aug, key_aug, value_aug = attend_forward(mixed_b, lengths, slope_parts)
     attn_sum = lax.psum_scatter(
         jnp.dot(heads_b, w_out, preferred_element_type=jnp.float32).astype(jnp.bfloat16),
         "tensor",
@@ -238,21 +332,7 @@
     grad_mid_full = lax.all_gather(grad_mid_b, "tensor", axis=0, tiled=True)
     g_w_out = cross_rows(heads_b, grad_mid_full)
     grad_heads_b = times_trans(grad_mid_full, w_out).astype(jnp.bfloat16)
-    grad_seq = grad_heads_b.reshape(seq_count, seq_len, local_heads, head_dim).transpose(0, 2, 1, 3)
-
-    def backward_seq(item):
-        parts, grad_part, log_part, length = item
-        return attend_backward(parts[0], parts[1], parts[2], grad_part, log_part, length, slopes)
-
-    grad_query, grad_key, grad_value = lax.map(
-        backward_seq, (per_seq, grad_seq, log_total, lengths)
-    )
-    grad_parts = jnp.stack([grad_query, grad_key, grad_value], axis=1)
-    grad_mixed_b = (
-        grad_parts.transpose(0, 3, 2, 1, 4)
-        .reshape(all_rows, local_heads * 3 * head_dim)
-        .astype(jnp.bfloat16)
-    )
+    grad_mixed_b = attend_backward(query_aug, key_aug, value_aug, heads_b, grad_heads_b)
     column_sums = jnp.sum(grad_mixed_b.astype(jnp.float32), axis=0).reshape(
         local_heads, 3, head_dim
     )

time: 1040 us -> 734 us (0.71)
  matrix products: 297 us -> 94.8 us
  other arithmetic: 145 us -> 38.3 us
  Pallas kernels: 0 us -> 61.3 us
  local copies, waits for them, and re-layouts: 51.4 us -> 5.58 us
  loops' own time: 17.1 us -> 0 us
    dot_general x28 -> x0, matrix products: 205 us -> none  [the longest x8 85.5 us: masked_scores(): jnp.einsum('hqe,hke->hqk', query_block, keys, preferred_element_type=jnp....]
    convert_element_type x12 -> x2, other arithmetic: 62.7 us -> 0.02 us  [split3(): return (hi.astype(F32), mid.astype(F32), low.astype(F32))]
    pallas_call x0 -> x2, Pallas kernels: none -> 61.3 us  [the longest x1 36.1 us: attend_backward(): pl.pallas_call(functools.partial(bwd_kernel, bk, bq), out_shape=jax.Shape...]
    reduce_sum x4 -> x0, other arithmetic: 23.3 us -> none  [forward_block(): denom = jnp.sum(expos, axis=-1, keepdims=True)]
    while x96 -> x0, local copies, waits for them, and re-layouts: 21.4 us -> none
    another operation x2 -> x0, loops' own time: 17.1 us -> none  [the longest x1 8.74 us: attend_backward(): lax.scan(backward_block, (empty, empty), starts)]
  transfers between devices with their start and end apart: 9 -> 9, of which waited for: 9 -> 9; matrix products, arithmetic and copies ran while one was open for 7% -> 10% of each run, Pallas kernels for 0% -> 0%
where the time goes in v1:
time: 734 us; the launch traced here: 724 us
  waiting for transfers between devices  444 us (60%)
  matrix products  94.8 us (13%)
  blocking collectives  62.6 us (9%)
  Pallas kernels  61.3 us (8%)
  other arithmetic  38.3 us (5%)
  between operations  15.9 us (2%)
    psum x1, waiting for transfers between devices, body(): lax.psum(g_w_qkv.astype(jnp.bfloat16), 'dp').astype(jnp.float32)  180 us
    reduce_scatter x1, waiting for transfers between devices, body(): lax.psum_scatter(jnp.dot(active_b, w_down, preferred_element_type=jnp.flo...  45 us
    reduce_scatter x1, waiting for transfers between devices, body(): lax.psum_scatter(jnp.dot(heads_b, w_out, preferred_element_type=jnp.float...  44.5 us
    psum x1, blocking collectives, body(): lax.psum((g_ln1_gain, g_ln1_bias, g_b_out, g_ln2_gain, g_ln2_bias, g_b_do...  40 us
    pallas_call x1, Pallas kernels, attend_backward(): pl.pallas_call(functools.partial(bwd_kernel, bk, bq), out_shape=jax.Shape...  36.1 us
    reduce_scatter x1, waiting for transfers between devices, body(): lax.psum_scatter(times_trans(grad_mixed_b, w_qkv).astype(jnp.bfloat16), '...  35.7 us
    all_gather x1, waiting for transfers between devices, body(): lax.all_gather(normed1_b, 'tensor', axis=0, tiled=True)  35.6 us
    reduce_scatter x1, waiting for transfers between devices, body(): lax.psum_scatter(times_trans(grad_pre_b, w_up).astype(jnp.bfloat16), 'ten...  33 us
  transfers between devices with their start and end apart: 9, of which 9 were waited for; matrix products, arithmetic and copies ran while one was open for 10% of the time, Pallas kernels for 0%

profile of v1, /device:TPU:0, one launch (start us, length us, event | category | flops | bytes accessed | tf_op | source)
XLA Modules:
  0.0 724.3 jit_solution(7503839936509655855)
XLA Ops:
  7.3 1.6 convert_reduce_fusion.2
  8.9 1.6 fusion.23
  10.6 1.4 fusion.18
  13.1 0.7 pad_maximum_fusion.1.slope_ref
  13.7 35.6 %all-gather.5.cloned.1.call-done = bf16[2048,1024]{1,0:T(8,128)(2,1)} async-done(((bf16[512,1024]{1,0:T(8,128)(2,1)}), bf16[2048,1024]{1,0:T(8,128)(2,1)}) %all-gather.5.cloned.1.call-update) | async-done | bytes 4194320 | tf_op jit(solution)/shard_map/all_gather | solution.py:266
  49.4 7.8 %add_convert_fusion.mixed_ref = bf16[2048,768]{1,0:T(8,128)(2,1)} fusion(bf16[2048,1024]{1,0:T(8,128)(2,1)} %all-gather.5.cloned.1.call-done, bf16[1024,768]{1,0:T(8,128)(2,1)} %param.24, f32[768]{0:T(1024)S(1)} %add.191), kind=kOutput, calls=%fused_computation.10 | convolution fusion | flops 3224371200 | bytes 8915968 | tf_op jit(solution)/shard_map/dot_general | solution.py:265
  57.2 25.2 %attend_forward.1 = (bf16[2048,256]{1,0:T(8,128)(2,1)}, bf16[4,2048,128]{2,1,0:T(8,128)(2,1)}, bf16[4,2048,128]{2,1,0:T(8,128)(2,1)}, bf16[4,2048,128]{2,1,0:T(8,128)(2,1)}) custom-call(s32[1]{0:T(128)} %copy.35.length_ref, f32[4,3]{1,0:T(4,128)} %pad_maximum_fusion.1.slope_ref, bf16[2048,768]{1,0:T(8,128)(2,1)} %add_convert_fusion.mixed_ref), custom_call_target="tpu_custom_call" | custom-call | flops 4294967296 | bytes 10485760 | tf_op jit(solution)/shard_map/attend_forward/pallas_call | solution.py:109
  82.3 4.5 convolution_convert_fusion
  87.2 44.5 %reduce-scatter.5.cloned.1.call-done = bf16[512,1024]{1,0:T(8,128)(2,1)} async-done(((bf16[2048,1024]{1,0:T(8,128)(2,1)}), bf16[512,1024]{1,0:T(8,128)(2,1)}) %reduce-scatter.5.cloned.1.call-update) | async-done | bytes 1048592 | tf_op jit(solution)/shard_map/reduce_scatter | solution.py:274
  131.6 1.7 fusion.34
  134.0 1.6 add_convert_fusion.2
  136.4 2.4 fusion.33
  139.0 31.3 %all-gather.7.cloned.1.call-done = bf16[2048,1024]{1,0:T(8,128)(2,1)} async-done(((bf16[512,1024]{1,0:T(8,128)(2,1)}), bf16[2048,1024]{1,0:T(8,128)(2,1)}) %all-gather.7.cloned.1.call-update) | async-done | bytes 4194320 | tf_op jit(solution)/shard_map/all_gather | solution.py:285
  170.2 11.4 %fusion.49 = f32[2048,1024]{1,0:T(8,128)} fusion(bf16[2048,1024]{1,0:T(8,128)(2,1)} %all-gather.7.cloned.1.call-done, bf16[1024,1024]{1,0:T(8,128)(2,1)} %param.30), kind=kOutput, calls=%fused_computation.99 | convolution fusion | flops 4294967296 | bytes 14680064 | tf_op jit(solution)/shard_map/dot_general | solution.py:284
  181.6 25.2 %all-gather.9.cloned.1.call-done = bf16[2048,1024]{1,0:T(8,128)(2,1)} async-done(((bf16[512,1024]{1,0:T(8,128)(2,1)}), bf16[2048,1024]{1,0:T(8,128)(2,1)}) %all-gather.9.cloned.1.call-update) | async-done | bytes 4194320 | tf_op jit(solution)/shard_map/all_gather | solution.py:314
  206.8 12.8 %fusion.43 = (bf16[1024]{0:T(1024)(128)(2,1)S(1)}, bf16[2048,1024]{1,0:T(8,128)(2,1)S(1)}) fusion(f32[2048,1024]{1,0:T(8,128)} %fusion.49, f32[1024]{0:T(1024)S(1)} %copy-done.26, bf16[2048,1024]{1,0:T(8,128)(2,1)} %all-gather.9.cloned.1.call-done, bf16[1024,1024]{1,0:T(8,128)(2,1)S(1)} %copy-done), kind=kOutput, calls=%fused_computation.95 | convolution fusion | flops 4341103616 | bytes 18880512 | tf_op jit(solution)/shard_map/dot_general | solution.py:226
  219.6 2.0 copy-done.27
  221.6 6.2 convolution_convert_fusion.2
  228.3 11.2 %convolution_convert_fusion.3 = bf16[2048,1024]{1,0:T(8,128)(2,1)} fusion(bf16[1024,1024]{1,0:T(8,128)(2,1)S(1)} %copy-done, f32[2048,1024]{1,0:T(8,128)} %fusion.49, f32[1024]{0:T(1024)S(1)} %copy-done.26), kind=kOutput, calls=%fused_computation.14 | convolution fusion | flops 4318035968 | bytes 14684160 | tf_op jit(solution)/shard_map/dot_general | solution.py:296
  239.5 33.0 %reduce-scatter.9.cloned.1.call-done = bf16[512,1024]{1,0:T(8,128)(2,1)} async-done(((bf16[2048,1024]{1,0:T(8,128)(2,1)}), bf16[512,1024]{1,0:T(8,128)(2,1)}) %reduce-scatter.9.cloned.1.call-update) | async-done | bytes 1048592 | tf_op jit(solution)/shard_map/reduce_scatter | solution.py:321
  272.5 2.5 fusion.30
  275.0 45.0 %reduce-scatter.7.cloned.1.call-done = bf16[512,1024]{1,0:T(8,128)(2,1)} async-done(((bf16[2048,1024]{1,0:T(8,128)(2,1)}), bf16[512,1024]{1,0:T(8,128)(2,1)}) %reduce-scatter.7.cloned.1.call-update) | async-done | bytes 1048592 | tf_op jit(solution)/shard_map/reduce_scatter | solution.py:295
  320.0 3.6 fusion.45
  323.6 1.4 copy-done.5
  325.0 1.1 convert_element_type.225
  326.4 9.5 %convolution_convert_fusion.6 = bf16[1024,1024]{1,0:T(8,128)(2,1)} fusion(bf16[2048,1024]{1,0:T(8,128)(2,1)} %all-gather.7.cloned.1.call-done, bf16[2048,1024]{1,0:T(8,128)(2,1)} %copy-done.27), kind=kOutput, calls=%fused_computation.58 | convolution fusion | flops 4296015872 | bytes 10485760 | tf_op jit(solution)/shard_map/dot_general | solution.py:220
  335.9 10.9 %convolution_convert_fusion.5 = bf16[1024,1024]{1,0:T(8,128)(2,1)} fusion(bf16[2048,1024]{1,0:T(8,128)(2,1)S(1)} %copy-done.23, f32[2048,1024]{1,0:T(8,128)} %fusion.49, f32[1024]{0:T(1024)S(1)} %copy-done.26), kind=kOutput, calls=%fused_computation.57 | convolution fusion | flops 4316987392 | bytes 14684160 | tf_op jit(solution)/shard_map/dot_general | solution.py:220
  346.8 14.0 %all-gather.11.cloned.1.call-done = bf16[2048,1024]{1,0:T(8,128)(2,1)} async-done(((bf16[512,1024]{1,0:T(8,128)(2,1)}), bf16[2048,1024]{1,0:T(8,128)(2,1)}) %all-gather.11.cloned.1.call-update) | async-done | bytes 4194320 | tf_op jit(solution)/shard_map/all_gather | solution.py:332
  360.8 4.5 convolution_convert_fusion.4.grad_ref
  365.2 36.1 %attend_backward.1 = bf16[2048,768]{1,0:T(8,128)(2,1)} custom-call(bf16[4,2048,128]{2,1,0:T(8,128)(2,1)} %get-tuple-element.19.qa_ref, bf16[4,2048,128]{2,1,0:T(8,128)(2,1)} %get-tuple-element.20.ka_ref, bf16[4,2048,128]{2,1,0:T(8,128)(2,1)} %get-tuple-element.21.va_ref, bf16[2048,256]{1,0:T(8,128)(2,1)} %get-tuple-element.18.heads_ref, ...), custom_call_target="tpu_custom_call" | custom-call | flops 10737418240 | bytes 12582912 | tf_op jit(solution)/shard_map/attend_backward/pallas_call | solution.py:175
  401.4 4.4 convolution_convert_fusion.8
  405.8 4.7 convolution_convert_fusion.7
  410.8 1.1 copy-done.25
  411.9 7.0 convolution_convert_fusion.1
  418.9 2.4 reduce.1
  421.5 22.6 %all-reduce.1 = (bf16[512]{0:T(512)(128)(2,1)S(1)}, bf16[1024]{0:T(1024)(128)(2,1)S(1)}) all-reduce(bf16[512]{0:T(512)(128)(2,1)S(1)} %convert_element_type.233, bf16[1024]{0:T(1024)(128)(2,1)S(1)} %get-tuple-element.42), channel_id=1, replica_groups=mesh['dp'=8,'tensor'=4] {'dp'}, use_global_device_ids=true, to_apply=%region_19.20 | all-reduce | flops 1536 | bytes 6144 | tf_op jit(solution)/shard_map/psum | solution.py:353
  444.1 0.6 convert_element_type.234
  444.7 0.6 convert_element_type.239
  445.3 180.1 %all-reduce.5.cloned.1.call-done = (bf16[1024,768]{1,0:T(8,128)(2,1)}, bf16[256,1024]{1,0:T(8,128)(2,1)}, bf16[1024,1024]{1,0:T(8,128)(2,1)}, bf16[1024,1024]{1,0:T(8,128)(2,1)}) async-done(((bf16[1024,768]{1,0:T(8,128)(2,1)}, bf16[256,1024]{1,0:T(8,128)(2,1)}, bf16[1024,1024]{1,0:T(8,128)(2,1)}, bf16[1024,1024]{1,0:T(8,128)(2,1)}), (bf16[1024,768]{1,0:T(8,128)(2,1)}, bf16[256,1024]{1,0:T(8,128)(2,1)}, ...) | async-done | bytes 6291472 | tf_op jit(solution)/shard_map/psum | solution.py:352
  625.4 2.2 convert_element_type.236
  627.6 1.9 convert_element_type.231
  629.5 0.6 copy-done.10
  630.2 2.7 convert_element_type.238
  632.9 2.8 convert_element_type.241
  635.7 35.7 %reduce-scatter.11.cloned.1.call-done = bf16[512,1024]{1,0:T(8,128)(2,1)} async-done(((bf16[2048,1024]{1,0:T(8,128)(2,1)}), bf16[512,1024]{1,0:T(8,128)(2,1)}) %reduce-scatter.11.cloned.1.call-update) | async-done | bytes 1048592 | tf_op jit(solution)/shard_map/reduce_scatter | solution.py:342
  671.4 2.2 fusion.31
  673.7 40.0 %all-reduce = (f32[1024]{0:T(1024)}, f32[1024]{0:T(1024)}, f32[1024]{0:T(1024)}, f32[1024]{0:T(1024)}, f32[1024]{0:T(1024)}, /*index=5*/f32[1024]{0:T(1024)}) all-reduce(f32[1024]{0:T(1024)S(1)} %get-tuple-element.24, f32[1024]{0:T(1024)S(1)} %get-tuple-element.29, ...), channel_id=1, replica_groups=mesh['dp'=8,'tensor'=4] {'dp','tensor'}, use_global_device_ids=true, to_apply=%region_14.15 | all-reduce | flops 6144 | bytes 49152 | tf_op jit(solution)/shard_map/psum | solution.py:359
  713.7 3.6 fusion.22
  (93 shorter events, 3.0 us)
Async XLA Ops:
  7.2 199.6 %copy-start = (bf16[1024,1024]{1,0:T(8,128)(2,1)S(1)}, bf16[1024,1024]{1,0:T(8,128)(2,1)}, u32[]{:S(2)}) copy-start(bf16[1024,1024]{1,0:T(8,128)(2,1)} %param.32) | copy-start | bytes 6291460
  7.2 3.3 copy-start.2
  7.2 3.3 copy-start.16
  7.2 3.3 copy-start.18
  7.2 42.1 %all-gather.5.cloned.1.call-start = ((), (), s32[]{:S(2)}) async-start(), calls=%async_computation.4 | async-start | bytes 5242880 | tf_op jit(solution)/shard_map/all_gather | solution.py:266
  8.9 3.8 copy-start.20
  12.0 119.6 %reduce-scatter.5.cloned.1.call-start = ((), (), s32[]{:S(2)}) async-start(), calls=%async_computation.5 | async-start | bytes 5242880 | tf_op jit(solution)/shard_map/reduce_scatter | solution.py:274
  57.2 25.2 %copy-start.12 = (bf16[256,1024]{1,0:T(8,128)(2,1)S(1)}, bf16[256,1024]{1,0:T(8,128)(2,1)}, u32[]{:S(2)}) copy-start(bf16[256,1024]{1,0:T(8,128)(2,1)} %param.26) | copy-start | bytes 1572868
  86.8 44.8 %copy-start.14 = (f32[1024]{0:T(1024)S(1)}, f32[1024]{0:T(1024)}, u32[]{:S(2)}) copy-start(f32[1024]{0:T(1024)} %param.27) | copy-start | bytes 12292
  86.9 47.1 %copy-start.15 = (f32[1024]{0:T(1024)S(1)}, f32[1024]{0:T(1024)}, u32[]{:S(2)}) copy-start(f32[1024]{0:T(1024)} %param.28) | copy-start | bytes 12292
  86.9 47.1 %copy-start.19 = (f32[1024]{0:T(1024)S(1)}, f32[1024]{0:T(1024)}, u32[]{:S(2)}) copy-start(f32[1024]{0:T(1024)} %param.29) | copy-start | bytes 12292
  86.9 83.3 %all-gather.7.cloned.1.call-start = ((), (), s32[]{:S(2)}) async-start(), calls=%async_computation.6 | async-start | bytes 5242880 | tf_op jit(solution)/shard_map/all_gather | solution.py:285
  131.6 1.7 copy-start.3
  134.0 2.3 copy-start.21
  135.6 71.2 %all-gather.9.cloned.1.call-start = ((), (), s32[]{:S(2)}) async-start(), calls=%async_computation.8 | async-start | bytes 5242880 | tf_op jit(solution)/shard_map/all_gather | solution.py:314
  138.9 67.9 %copy-start.26 = (f32[1024]{0:T(1024)S(1)}, f32[1024]{0:T(1024)}, u32[]{:S(2)}) copy-start(f32[1024]{0:T(1024)} %param.31) | copy-start | bytes 12292
  138.9 133.6 %reduce-scatter.9.cloned.1.call-start = ((), (), s32[]{:S(2)}) async-start(), calls=%async_computation.9 | async-start | bytes 5242880 | tf_op jit(solution)/shard_map/reduce_scatter | solution.py:321
  206.8 14.7 %copy-start.24 = (bf16[1024,1024]{1,0:T(8,128)(2,1)S(1)}, bf16[1024,1024]{1,0:T(8,128)(2,1)}, u32[]{:S(2)}) copy-start(bf16[1024,1024]{1,0:T(8,128)(2,1)} %param.30) | copy-start | bytes 6291460
  219.6 2.0 copy-start.27
  227.8 92.2 %reduce-scatter.7.cloned.1.call-start = ((), (), s32[]{:S(2)}) async-start(), calls=%async_computation.7 | async-start | bytes 5242880 | tf_op jit(solution)/shard_map/reduce_scatter | solution.py:295
  239.4 33.0 %copy-start.4 = (bf16[512,1024]{1,0:T(8,128)(2,1)S(1)}, bf16[512,1024]{1,0:T(8,128)(2,1)}, u32[]{:S(2)}) copy-start(bf16[512,1024]{1,0:T(8,128)(2,1)} %reduce-scatter.5.cloned.1.call-done) | copy-start | bytes 3145732
  239.5 80.5 %copy-start.17 = (f32[1024]{0:T(1024)S(1)}, f32[1024]{0:T(1024)}, u32[]{:S(2)}) copy-start(f32[1024]{0:T(1024)} %param.33) | copy-start | bytes 12292
  239.5 121.3 %all-gather.11.cloned.1.call-start = ((), (), s32[]{:S(2)}) async-start(), calls=%async_computation.10 | async-start | bytes 5242880 | tf_op jit(solution)/shard_map/all_gather | solution.py:332
  272.5 47.5 %copy-start.6 = (bf16[512,1024]{1,0:T(8,128)(2,1)S(1)}, bf16[512,1024]{1,0:T(8,128)(2,1)}, u32[]{:S(2)}) copy-start(bf16[512,1024]{1,0:T(8,128)(2,1)} %reduce-scatter.9.cloned.1.call-done) | copy-start | bytes 3145732
  323.6 1.4 copy-start.5
  326.2 299.2 %all-reduce.5.cloned.1.call-start = ((), (), s32[]{:S(2)}) async-start(), calls=%async_computation.12 | async-start | bytes 12582912 | tf_op jit(solution)/shard_map/psum | solution.py:352
  326.4 9.5 %copy-start.23 = (bf16[2048,1024]{1,0:T(8,128)(2,1)S(1)}, bf16[2048,1024]{1,0:T(8,128)(2,1)}, u32[]{:S(2)}) copy-start(bf16[2048,1024]{1,0:T(8,128)(2,1)} %all-gather.9.cloned.1.call-done) | copy-start | bytes 12582916
  335.9 24.9 %copy-start.13 = (bf16[256,1024]{1,0:T(8,128)(2,1)S(1)}, bf16[256,1024]{1,0:T(8,128)(2,1)}, u32[]{:S(2)}) copy-start(bf16[256,1024]{1,0:T(8,128)(2,1)} %param.26) | copy-start | bytes 1572868
  365.2 36.1 %copy-start.8 = (bf16[2048,256]{1,0:T(8,128)(2,1)S(1)}, bf16[2048,256]{1,0:T(8,128)(2,1)}, u32[]{:S(2)}) copy-start(bf16[2048,256]{1,0:T(8,128)(2,1)} %get-tuple-element.18.heads_ref) | copy-start | bytes 3145732
  401.4 4.4 copy-start.7
  401.4 4.4 copy-start.22
  410.5 1.4 copy-start.25
  410.5 260.9 %reduce-scatter.11.cloned.1.call-start = ((), (), s32[]{:S(2)}) async-start(), calls=%async_computation.11 | async-start | bytes 5242880 | tf_op jit(solution)/shard_map/reduce_scatter | solution.py:342
  625.4 2.2 copy-start.11
  627.6 2.5 copy-start.10
  630.2 2.7 copy-start.9
  673.7 43.6 %copy-start.1 = (bf16[1024,1024]{1,0:T(8,128)(2,1)S(1)}, bf16[1024,1024]{1,0:T(8,128)(2,1)}, u32[]{:S(2)}) copy-start(bf16[1024,1024]{1,0:T(8,128)(2,1)} %param.32) | copy-start | bytes 6291460
Sparse Core Ops, SparseCore 0:
  12.1 37.2 all-gather.4
  87.0 44.6 reduce-scatter.4
  135.7 34.4 all-gather.6
  172.3 34.4 all-gather.8
  227.9 44.5 reduce-scatter.8
  275.4 44.5 reduce-scatter.6
  326.3 34.4 all-gather.10
  410.6 214.6 all-reduce.4
  627.9 43.4 reduce-scatter.10

commit v2 on v1

v2 whole, which is shorter than its diff:
```python
import functools
import jax
import jax.numpy as jnp
from jax import lax
from jax.sharding import PartitionSpec as P
from jax.experimental import pallas as pl
from jax.experimental.pallas import tpu as pltpu

HEADS = 16
HD = 64
LANES = 128
F32 = jnp.float32
BF16 = jnp.bfloat16


def split3(x):
    hi = x.astype(BF16)
    rest = x - hi.astype(F32)
    mid = rest.astype(BF16)
    low = (rest - mid.astype(F32)).astype(BF16)
    return hi.astype(F32), mid.astype(F32), low.astype(F32)


def nt(a, b):
    return lax.dot_general(a, b, (((1,), (1,)), ((), ())), preferred_element_type=F32)


def nn(a, b):
    return jnp.dot(a, b, preferred_element_type=F32)


def at_lanes(lane, base, pairs):
    out = base
    for where, value in pairs:
        out = jnp.where(lane == where, value, out)
    return out


def key_side(span, first, length):
    pos = first + lax.broadcasted_iota(jnp.int32, (span, LANES), 0)
    lane = lax.broadcasted_iota(jnp.int32, (span, LANES), 1)
    low = (pos & 255).astype(F32)
    high = (pos - (pos & 255)).astype(F32)
    is_high = (lane == 64) | (lane == 66) | (lane == 68)
    is_low = (lane == 65) | (lane == 67) | (lane == 69)
    gone = jnp.where(pos < length, 0.0, -1e30)
    out = jnp.where(is_high, high, jnp.where(is_low, low, 0.0))
    out = jnp.where(lane == 70, gone, out)
    return jnp.where((lane >= 71) & (lane <= 73), 1.0, out)


def slope_side(lane, slope_parts):
    s1, s2, s3 = slope_parts
    out = jnp.where(lane < 66, s1, jnp.where(lane < 68, s2, s3))
    out = jnp.where(lane == 70, 1.0, out)
    return jnp.where((lane >= 64) & (lane <= 70), out, 0.0)


def wide(x):
    return jnp.concatenate([x, jnp.zeros_like(x)], axis=1)


def fwd_kernel(count, bq, place_ref, length_ref, slope_ref, *refs):
    mixed_refs, heads_refs = refs[:count], refs[count : 2 * count]
    qa_ref, ka_ref, va_ref, o_ref = refs[2 * count :]
    own = mixed_refs[0].shape[0]
    heads, span, _ = qa_ref.shape
    lane = lax.broadcasted_iota(jnp.int32, (1, LANES), 1)
    ones = jnp.where((lane >= 64) & (lane <= 66), 1.0, 0.0)
    for j in range(count):
        first = pl.multiple_of((place_ref[0] ^ j) * own, own)
        keys = key_side(own, first, length_ref[0])
        for h in range(heads):
            base = h * 3 * HD
            q = mixed_refs[j][:, base : base + HD].astype(F32) * (HD ** -0.5)
            k = mixed_refs[j][:, base + HD : base + 2 * HD].astype(F32)
            v = mixed_refs[j][:, base + 2 * HD : base + 3 * HD].astype(F32)
            parts = [slope_ref[h, n] for n in range(3)]
            rows = pl.ds(first, own)
            qa_ref[h, rows, :] = (wide(q) + slope_side(lane, parts)).astype(BF16)
            ka_ref[h, rows, :] = (wide(k) + keys).astype(BF16)
            va_ref[h, rows, :] = (wide(v) + ones).astype(BF16)

    def one_head(h, carry):
        for i in range(span // bq):
            rows = slice(i * bq, (i + 1) * bq)
            ext = (i + 1) * bq
            q = qa_ref[h, rows, :]
            s = nt(q, ka_ref[h, :ext, :])
            tq = lax.broadcasted_iota(jnp.int32, (bq, bq), 0)
            tk = lax.broadcasted_iota(jnp.int32, (bq, bq), 1)
            diag = jnp.where(tk <= tq, s[:, i * bq :], -3e38)
            s = jnp.concatenate([s[:, : i * bq], diag], axis=1) if i else diag
            m = jnp.max(s, axis=1, keepdims=True)
            p = jnp.exp(s - m).astype(BF16)
            o = nn(p, va_ref[h, :ext, :])
            total = o[:, HD : HD + 1]
            out = o / total
            l1, l2, l3 = split3(-(m + jnp.log(total)))
            o_ref[h, rows, :] = out.astype(BF16)
            logs = at_lanes(lane, q.astype(F32), ((71, l1), (72, l2), (73, l3)))
            qa_ref[h, rows, :] = logs.astype(BF16)
        return carry

    lax.fori_loop(0, heads, one_head, 0)
    for j in range(count):
        rows = pl.ds(pl.multiple_of((place_ref[0] ^ j) * own, own), own)
        heads_refs[j][...] = jnp.concatenate([o_ref[h, rows, :][:, :HD] for h in range(heads)], axis=1)


def attend_forward(mixed, place, length, slope_parts, bq=256):
    count = len(mixed)
    own = mixed[0].shape[0]
    span = own * count
    heads = mixed[0].shape[1] // (3 * HD)
    vm = pl.BlockSpec(memory_space=pltpu.VMEM)
    sm = pl.BlockSpec(memory_space=pltpu.SMEM)
    aug = jax.ShapeDtypeStruct((heads, span, LANES), BF16)
    res = pl.pallas_call(
        functools.partial(fwd_kernel, count, bq),
        out_shape=(jax.ShapeDtypeStruct((own, heads * HD), BF16),) * count + (aug, aug, aug),
        in_specs=[sm, sm, sm] + [vm] * count,
        out_specs=(vm,) * (count + 3),
        scratch_shapes=[pltpu.VMEM((heads, span, LANES), BF16)],
        compiler_params=pltpu.CompilerParams(vmem_limit_bytes=60 << 20),
        cost_estimate=pl.CostEstimate(
            flops=4 * heads * span * span * LANES // 2, transcendentals=heads * span * span // 2,
            bytes_accessed=heads * span * LANES * 10,
        ),
        name="attend_forward",
    )(place, length, slope_parts, *mixed)
    return res[:count], res[count:]


def bwd_kernel(count, bk, bq, place_ref, qa_ref, ka_ref, va_ref, *refs):
    heads_refs, grad_refs, out_refs = refs[:count], refs[count : 2 * count], refs[2 * count : 3 * count]
    da_ref, dqt_ref, dk_ref, dv_ref = refs[3 * count :]
    own = heads_refs[0].shape[0]
    heads, span, _ = qa_ref.shape
    lane = lax.broadcasted_iota(jnp.int32, (1, LANES), 1)
    for j in range(count):
        rows = pl.ds(pl.multiple_of((place_ref[0] ^ j) * own, own), own)
        for h in range(heads):
            o = heads_refs[j][:, h * HD : (h + 1) * HD].astype(F32)
            g = grad_refs[j][:, h * HD : (h + 1) * HD].astype(F32)
            d1, d2, d3 = split3(-jnp.sum(o * g, axis=1, keepdims=True))
            da_ref[h, rows, :] = at_lanes(lane, wide(g), ((64, d1), (65, d2), (66, d3))).astype(BF16)

    def one_head(h, carry):
        for j in range(span // bk):
            cols = slice(j * bk, (j + 1) * bk)
            k = ka_ref[h, cols, :]
            v = va_ref[h, cols, :]
            kt = k[:, :HD].T
            start = j * bk
            dk = jnp.zeros((bk, LANES), F32)
            dv = jnp.zeros((bk, LANES), F32)
            while start < span:
                stop = min(span, (start // bq + 1) * bq)
                q = qa_ref[h, start:stop, :]
                d = da_ref[h, start:stop, :]
                p = jnp.exp(nt(k, q))
                if start == j * bk:
                    tk = lax.broadcasted_iota(jnp.int32, (bk, stop - start), 0)
                    tq = lax.broadcasted_iota(jnp.int32, (bk, stop - start), 1)
                    p = jnp.where(tk <= tq, p, 0.0)
                dp = nt(v, d)
                ds = (p * dp).astype(BF16)
                dv = dv + nn(p.astype(BF16), d)
                dk = dk + nn(ds, q)
                part = nn(kt, ds)
                if j == 0:
                    dqt_ref[h, :, start:stop] = part
                else:
                    dqt_ref[h, :, start:stop] += part
                start = stop
            dk_ref[h, cols, :] = dk
            dv_ref[h, cols, :] = dv
        return carry

    lax.fori_loop(0, heads, one_head, 0)
    for j in range(count):
        first = pl.multiple_of((place_ref[0] ^ j) * own, own)
        rows = pl.ds(first, own)
        pieces = []
        for h in range(heads):
            pieces += [dqt_ref[h, :, rows].T * (HD ** -0.5), dk_ref[h, rows, :HD], dv_ref[h, rows, :HD]]
        out_refs[j][...] = jnp.concatenate(pieces, axis=1).astype(BF16)


def attend_backward(saved, heads_b, grad_heads, place, bk=256, bq=2048):
    heads, span, _ = saved[0].shape
    count = len(heads_b)
    own = span // count
    vm = pl.BlockSpec(memory_space=pltpu.VMEM)
    sm = pl.BlockSpec(memory_space=pltpu.SMEM)
    return pl.pallas_call(
        functools.partial(bwd_kernel, count, bk, bq),
        out_shape=(jax.ShapeDtypeStruct((own, heads * 3 * HD), BF16),) * count,
        in_specs=[sm] + [vm] * (3 + 2 * count),
        out_specs=(vm,) * count,
        scratch_shapes=[
            pltpu.VMEM((heads, span, LANES), BF16),
            pltpu.VMEM((heads, HD, span), F32),
            pltpu.VMEM((heads, span, LANES), F32),
            pltpu.VMEM((heads, span, LANES), F32),
        ],
        compiler_params=pltpu.CompilerParams(vmem_limit_bytes=60 << 20),
        cost_estimate=pl.CostEstimate(
            flops=10 * heads * span * span * LANES // 2, transcendentals=heads * span * span // 2,
            bytes_accessed=heads * span * LANES * 12,
        ),
        name="attend_backward",
    )(place, *saved, *heads_b, *grad_heads)


def slope_table(first, count, total):
    ids = (first + jnp.arange(count, dtype=jnp.int32)).astype(F32)
    slopes = jnp.exp2(-8.0 * (ids + 1.0) / total)
    return jnp.stack(split3(slopes), axis=1)


eps = 1e-05


def layer_norm(values, gain, bias):
    centre = jnp.mean(values, axis=-1, keepdims=True)
    shifted = values - centre
    spread = jnp.mean(shifted * shifted, axis=-1, keepdims=True)
    factor = lax.rsqrt(spread + eps)
    unit_rows = shifted * factor
    return (unit_rows * gain + bias, unit_rows, factor)


def norm_back(grad_rows, unit_rows, factor, gain):
    scaled = grad_rows * gain
    inner = jnp.mean(scaled * unit_rows, axis=-1, keepdims=True)
    return factor * (scaled - jnp.mean(scaled, axis=-1, keepdims=True) - unit_rows * inner)


def tn(a, b):
    return lax.dot_general(a, b, (((0,), (0,)), ((), ())), preferred_element_type=F32)


def swap(x, axis, bit):
    return lax.ppermute(x, axis, [(i, i ^ bit) for i in range(lax.axis_size(axis))])


def bits_of(axis):
    return [1 << n for n in range(lax.axis_size(axis).bit_length() - 1)]


def gather_blocks(x, axis):
    blocks = {0: x}
    for bit in bits_of(axis)[1:]:
        blocks.update({j ^ bit: swap(b, axis, bit) for j, b in list(blocks.items())})
    blocks.update({j ^ 1: swap(b, axis, 1) for j, b in list(blocks.items())})
    return [blocks[j] for j in range(len(blocks))]


def sum_blocks(parts, axis):
    parts = dict(enumerate(parts))
    for bit in bits_of(axis):
        kept = {}
        for j in sorted(parts, reverse=True):
            if not j & bit:
                kept[j] = parts[j].astype(F32) + swap(parts[j | bit].astype(BF16), axis, bit).astype(F32)
        parts = kept
    return parts[0]


def total_of(x, axis):
    for bit in bits_of(axis):
        x = x + swap(x, axis, bit)
    return x


def body(
    layer_in,
    cotangent,
    lengths,
    languages,
    lang_weight,
    ln1_gain,
    ln1_bias,
    w_qkv,
    b_qv,
    w_out,
    b_out,
    ln2_gain,
    ln2_bias,
    w_up,
    b_up,
    w_down,
    b_down,
):
    groups = lax.axis_size("tensor")
    place = lax.axis_index("tensor")
    place_one = place.astype(jnp.int32).reshape(1)
    own_rows = layer_in.shape[0]
    local_heads = w_out.shape[0] // HD

    in_float = layer_in.astype(F32)
    normed1, unit1, factor1 = layer_norm(in_float, ln1_gain, ln1_bias)
    n1 = gather_blocks(normed1.astype(BF16), "tensor")

    positions = place * own_rows + jnp.arange(own_rows, dtype=jnp.int32)
    weight = jnp.sum(jnp.where(jnp.arange(lang_weight.shape[0]) == languages[0], lang_weight, 0.0))
    live = jnp.where(positions < lengths[0], weight, 0.0)
    grad_top = cotangent.astype(F32) * live[:, None]
    g_b_down = jnp.sum(grad_top, axis=0)

    pairs = b_qv.reshape(local_heads, 2, HD)
    bias_three = jnp.stack([pairs[:, 0], jnp.zeros_like(pairs[:, 0]), pairs[:, 1]], axis=1).reshape(1, -1)
    mixed = [(nn(x, w_qkv) + bias_three).astype(BF16) for x in n1]
    slope_parts = slope_table(place * local_heads, local_heads, HEADS)
    heads_b, saved = attend_forward(mixed, place_one, lengths, slope_parts)

    top_gate, mixed_gate = lax.optimization_barrier((grad_top.astype(BF16), mixed[-1]))
    top = gather_blocks(top_gate, "tensor")

    attn_sum = sum_blocks([nn(x, w_out).astype(BF16) for x in heads_b], "tensor")
    middle = in_float + attn_sum + b_out
    normed2, unit2, factor2 = layer_norm(middle, ln2_gain, ln2_bias)
    n2 = gather_blocks(normed2.astype(BF16), "tensor")

    active, grad_pre = [], []
    for j in range(groups):
        pre = nn(n2[j], w_up) + b_up
        out, pull = jax.vjp(lambda v: jax.nn.gelu(v, approximate=True), pre)
        active.append(out.astype(BF16))
        grad_pre.append(pull(nt(top[j], w_down))[0].astype(BF16))
    grad_norm2 = sum_blocks([nt(x, w_up).astype(BF16) for x in grad_pre], "tensor")
    mlp_sum = sum_blocks([nn(x, w_down).astype(BF16) for x in active], "tensor")
    output = middle + mlp_sum + b_down

    def weight_grad(lefts, rights):
        return tn(jnp.concatenate(lefts, axis=0), jnp.concatenate(rights, axis=0))

    g_w_down = weight_grad(active, top)
    g_w_up = weight_grad(n2, grad_pre)
    g_b_up = sum(jnp.sum(x.astype(F32), axis=0) for x in grad_pre)

    g_ln2_gain = jnp.sum(grad_norm2 * unit2, axis=0)
    g_ln2_bias = jnp.sum(grad_norm2, axis=0)
    grad_middle = grad_top + norm_back(grad_norm2, unit2, factor2, ln2_gain)
    g_b_out = jnp.sum(grad_middle, axis=0)
    gm = gather_blocks(grad_middle.astype(BF16), "tensor")
    grad_heads = [nt(x, w_out).astype(BF16) for x in gm]
    grad_mixed = attend_backward(saved, heads_b, grad_heads, place_one)
    g_w_out = weight_grad(heads_b, gm)
    column_sums = sum(jnp.sum(x.astype(F32), axis=0) for x in grad_mixed).reshape(local_heads, 3, HD)
    g_b_qv = jnp.stack([column_sums[:, 0], column_sums[:, 2]], axis=1).reshape(-1)
    g_w_qkv = weight_grad(n1, grad_mixed)
    grad_norm1 = sum_blocks([nt(x, w_qkv).astype(BF16) for x in grad_mixed], "tensor")
    g_ln1_gain = jnp.sum(grad_norm1 * unit1, axis=0)
    g_ln1_bias = jnp.sum(grad_norm1, axis=0)
    grad_input = grad_middle + norm_back(grad_norm1, unit1, factor1, ln1_gain)

    up, down = lax.psum((g_w_up.astype(BF16), g_w_down.astype(BF16)), "dp")
    w_rest, up, down = lax.optimization_barrier(((g_w_qkv.astype(BF16), g_w_out.astype(BF16)), up, down))
    qkv, out = lax.psum(w_rest, "dp")

    width = ln1_gain.shape[0]
    early = total_of(jnp.concatenate([g_b_down, g_b_out, g_ln2_gain, g_ln2_bias]), "tensor")
    early = total_of(jnp.concatenate([early, g_b_up]), "dp")
    late = total_of(jnp.concatenate([g_ln1_gain, g_ln1_bias]), "tensor")
    late = total_of(jnp.concatenate([late, g_b_qv]), "dp")
    shared = [early[n * width : (n + 1) * width] for n in range(4)]
    g_b_up = early[4 * width :]
    return (
        output.astype(BF16),
        grad_input.astype(BF16),
        late[:width],
        late[width : 2 * width],
        qkv.astype(F32),
        late[2 * width :],
        out.astype(F32),
        shared[1],
        shared[2],
        shared[3],
        up.astype(F32),
        g_b_up,
        down.astype(F32),
        shared[0],
    )


def solution(mesh):
    rows, columns, flat = P("tensor", None), P(None, "tensor"), P("tensor")
    tokens = P(("dp", "tensor"), None)
    in_specs = (tokens, tokens, P("dp"), P("dp"), P(), P(), P(), columns, flat, rows, P(), P(), P(), columns, flat, rows, P())
    out_specs = (tokens, tokens, P(), P(), columns, flat, rows, P(), P(), P(), columns, flat, rows, P())
    return jax.shard_map(body, mesh=mesh, in_specs=in_specs, out_specs=out_specs, check_vma=False)
```

time: 734 us -> 553 us (0.75)
  waiting for transfers between devices: 444 us -> 308 us
  blocking collectives: 62.6 us -> 0 us
  starting transfers between devices: 1.41 us -> 24.6 us
  other arithmetic: 38.3 us -> 29.3 us
  matrix products: 94.8 us -> 103 us
    reduce_scatter x4 -> x0, waiting for transfers between devices: 158 us -> none  [the longest x1 45 us: body(): lax.psum_scatter(jnp.dot(active_b, w_down, preferred_element_type=jnp.flo...]
    ppermute x0 -> x34, waiting for transfers between devices: none -> 145 us  [swap(): lax.ppermute(x, axis, [(i, i ^ bit) for i in range(lax.axis_size(axis))])]
    all_gather x4 -> x0, waiting for transfers between devices: 106 us -> none  [the longest x1 35.6 us: body(): lax.all_gather(normed1_b, 'tensor', axis=0, tiled=True)]
    psum x2 -> x0, blocking collectives: 62.6 us -> none  [the longest x1 40 us: body(): lax.psum((g_ln1_gain, g_ln1_bias, g_b_out, g_ln2_gain, g_ln2_bias, g_b_do...]
    ppermute x0 -> x34, starting transfers between devices: none -> 24.3 us  [swap(): lax.ppermute(x, axis, [(i, i ^ bit) for i in range(lax.axis_size(axis))])]
    psum x1 -> x2, waiting for transfers between devices: 180 us -> 164 us  [the longest x1 85.3 us: body(): up, down = lax.psum((g_w_up.astype(BF16), g_w_down.astype(BF16)), 'dp')]
    dot_general x12 -> x36, matrix products: 94.8 us -> 103 us  [the longest x16 41.2 us: nt(): lax.dot_general(a, b, (((1,), (1,)), ((), ())), preferred_element_type=F32)]
    convert_element_type x11 -> x9, other arithmetic: 21 us -> 19.3 us  [the longest x1 4.66 us: body(): up.astype(F32)]
  transfers between devices with their start and end apart: 9 -> 36, of which waited for: 9 -> 14; matrix products, arithmetic and copies ran while one was open for 10% -> 20% of each run, Pallas kernels for 0% -> 6%
where the time goes in v2:
time: 553 us; the launch traced here: 545 us
  waiting for transfers between devices  308 us (56%)
  matrix products  103 us (19%)
  Pallas kernels  60.3 us (11%)
  other arithmetic  29.3 us (5%)
  starting transfers between devices  24.6 us (4%)
  between operations  16.5 us (3%)
    ppermute x34, waiting for transfers between devices, swap(): lax.ppermute(x, axis, [(i, i ^ bit) for i in range(lax.axis_size(axis))])  145 us
    psum x1, waiting for transfers between devices, body(): up, down = lax.psum((g_w_up.astype(BF16), g_w_down.astype(BF16)), 'dp')  85.3 us
    psum x1, waiting for transfers between devices, body(): qkv, out = lax.psum(w_rest, 'dp')  78.4 us
    dot_general x16, matrix products, nt(): lax.dot_general(a, b, (((1,), (1,)), ((), ())), preferred_element_type=F32)  41.2 us
    dot_general x16, matrix products, nn(): return jnp.dot(a, b, preferred_element_type=F32)  36.9 us
    pallas_call x1, Pallas kernels, attend_backward(): pl.pallas_call(functools.partial(bwd_kernel, count, bk, bq), out_shape=(j...  34.1 us
    pallas_call x1, Pallas kernels, attend_forward(): pl.pallas_call(functools.partial(fwd_kernel, count, bq), out_shape=(jax.S...  26.2 us
    dot_general x4, matrix products, tn(): lax.dot_general(a, b, (((0,), (0,)), ((), ())), preferred_element_type=F32)  24.4 us
  transfers between devices with their start and end apart: 36, of which 14 were waited for; matrix products, arithmetic and copies ran while one was open for 20% of the time, Pallas kernels for 6%

profile of v2, /device:TPU:0, one launch (start us, length us, event | category | flops | bytes accessed | tf_op | source)
XLA Modules:
  0.0 544.7 jit_solution(9937777660963951340)
XLA Ops:
  12.0 3.0 collective-permute-start.1
  15.9 22.5 %collective-permute-done.1 = bf16[512,1024]{1,0:T(8,128)(2,1)} collective-permute-done((bf16[512,1024]{1,0:T(8,128)(2,1)}, bf16[512,1024]{1,0:T(8,128)(2,1)}, u32[]{:S(2)}, u32[]{:S(2)}) %collective-permute-start.1) | collective-permute-done | bytes 1048608 | tf_op jit(solution)/shard_map/ppermute | solution.py:246
  39.1 3.7 add_convert_fusion.9.refs_0_
  42.8 3.1 add_convert_fusion.7.refs_2_
  45.9 3.1 add_convert_fusion.8.refs_1_
  49.0 1.9 add_convert_fusion.6.refs_3_
  50.9 26.2 %attend_forward.1 = (bf16[512,256]{1,0:T(8,128)(2,1)}, bf16[512,256]{1,0:T(8,128)(2,1)}, bf16[512,256]{1,0:T(8,128)(2,1)}, bf16[512,256]{1,0:T(8,128)(2,1)}, bf1...) custom-call(s32[1]{0:T(128)} %bitcast.place_ref, s32[1]{0:T(128)} %copy.35.length_ref, ...), custom_call_target="tpu_custom_call" | custom-call | flops 4294967296 | bytes 10485760 | tf_op jit(solution)/shard_map/attend_forward/pallas_call | solution.py:119
  77.1 2.4 convolution_convert_fusion.12
  83.4 1.8 collective-permute-start.14
  85.8 1.9 add_convert_fusion.5
  90.1 19.4 %collective-permute-done.14 = bf16[512,1024]{1,0:T(8,128)(2,1)S(1)} collective-permute-done((bf16[512,1024]{1,0:T(8,128)(2,1)S(1)}, bf16[512,1024]{1,0:T(8,128)(2,1)S(1)}, u32[]{:S(2)}, u32[]{:S(2)}) %collective-permute-start.14) | collective-permute-done | bytes 1048608 | tf_op jit(solution)/shard_map/ppermute | solution.py:246
  109.5 21.5 %collective-permute-done.5 = bf16[512,1024]{1,0:T(8,128)(2,1)S(1)} collective-permute-done((bf16[512,1024]{1,0:T(8,128)(2,1)S(1)}, bf16[512,1024]{1,0:T(8,128)(2,1)S(1)}, u32[]{:S(2)}, u32[]{:S(2)}) %collective-permute-start.5) | collective-permute-done | bytes 1048608 | tf_op jit(solution)/shard_map/ppermute | solution.py:246
  132.8 1.8 collective-permute-start.8
  135.9 2.6 fusion.155
  139.8 17.3 %collective-permute-done.8 = bf16[512,1024]{1,0:T(8,128)(2,1)S(1)} collective-permute-done((bf16[512,1024]{1,0:T(8,128)(2,1)S(1)}, bf16[512,1024]{1,0:T(8,128)(2,1)S(1)}, u32[]{:S(2)}, u32[]{:S(2)}) %collective-permute-start.8) | collective-permute-done | bytes 1048608 | tf_op jit(solution)/shard_map/ppermute | solution.py:246
  157.1 2.6 fusion.157
  162.3 11.1 %convert_reduce_fusion.4 = (f32[1024]{0:T(1024)S(1)}, bf16[512,1024]{1,0:T(8,128)(2,1)}, bf16[512,1024]{1,0:T(8,128)(2,1)}, bf16[512,1024]{1,0:T(8,128)(2,1)}, f...) fusion(f32[512,1024]{1,0:T(8,128)S(1)} %fusion.154, ...), kind=kOutput, calls=%fused_computation.111 | convolution fusion | flops 1126166528 | bytes 26234880 | tf_op jit(solution)/shard_map/dot_general | solution.py:29
  173.4 2.9 convolution_convert_fusion.4
  181.4 1.8 collective-permute-start.17
  187.5 20.0 %collective-permute-done.17 = bf16[512,1024]{1,0:T(8,128)(2,1)S(1)} collective-permute-done((bf16[512,1024]{1,0:T(8,128)(2,1)S(1)}, bf16[512,1024]{1,0:T(8,128)(2,1)S(1)}, u32[]{:S(2)}, u32[]{:S(2)}) %collective-permute-start.17) | collective-permute-done | bytes 1048608 | tf_op jit(solution)/shard_map/ppermute | solution.py:246
  207.5 2.1 multiply_reduce_fusion
  209.7 19.4 %collective-permute-done.11 = bf16[512,1024]{1,0:T(8,128)(2,1)S(1)} collective-permute-done((bf16[512,1024]{1,0:T(8,128)(2,1)S(1)}, bf16[512,1024]{1,0:T(8,128)(2,1)S(1)}, u32[]{:S(2)}, u32[]{:S(2)}) %collective-permute-start.11) | collective-permute-done | bytes 1048608 | tf_op jit(solution)/shard_map/ppermute | solution.py:246
  229.1 3.0 fusion.140
  237.1 1.8 collective-permute-start.31
  238.9 6.1 %fusion.99 = bf16[1024,1024]{1,0:T(8,128)(2,1)} fusion(bf16[512,1024]{1,0:T(8,128)(2,1)S(1)} %collective-permute-done.15, bf16[512,1024]{1,0:T(8,128)(2,1)S(1)} %collective-permute-done.14, bf16[512,1024]{1,0:T(8,128)(2,1)S(1)} %collective-permute-done.12, bf16[512,1024]{1,0:T(8,128)(2,1)S(1)} %fusion.98, bf16[512,1024]{1,0:T(8,128)(2,1)S(1)} %copy-done.43, ...), kind=kOutput, calls=%fused_computation.132 | convolution fusion | flops 4329570304 | bytes 10485760 | tf_op jit(solution)/shard_map/dot_general | solution.py:242
  246.6 14.8 %collective-permute-done.19 = bf16[512,1024]{1,0:T(8,128)(2,1)} collective-permute-done((bf16[512,1024]{1,0:T(8,128)(2,1)}, bf16[512,1024]{1,0:T(8,128)(2,1)}, u32[]{:S(2)}, u32[]{:S(2)}) %collective-permute-start.19) | collective-permute-done | bytes 1048608 | tf_op jit(solution)/shard_map/ppermute | solution.py:246
  261.5 7.4 %fusion.104 = bf16[1024,1024]{1,0:T(8,128)(2,1)} fusion(bf16[512,1024]{1,0:T(8,128)(2,1)} %get-tuple-element.93, bf16[512,1024]{1,0:T(8,128)(2,1)S(1)} %copy-done.38, bf16[512,1024]{1,0:T(8,128)(2,1)S(1)} %copy-done.49, bf16[512,1024]{1,0:T(8,128)(2,1)S(1)} %copy-done.45, bf16[512,1024]{1,0:T(8,128)(2,1)S(1)} %collective-permute-done.9, ...), kind=kOutput, calls=%fused_computation.133 | convolution fusion | flops 4329570304 | bytes 10485760 | tf_op jit(solution)/shard_map/dot_general | solution.py:242
  269.2 2.7 collective-permute-start.33
  271.9 2.5 convolution_convert_fusion.19.refs_4_
  275.0 2.7 convolution_convert_fusion.17.refs_6_
  277.7 2.4 convolution_convert_fusion.18.refs_5_
  280.1 2.4 convolution_convert_fusion.16.refs_7_
  282.5 34.1 %attend_backward.1 = (bf16[512,768]{1,0:T(8,128)(2,1)}, bf16[512,768]{1,0:T(8,128)(2,1)}, bf16[512,768]{1,0:T(8,128)(2,1)}, bf16[512,768]{1,0:T(8,128)(2,1)}) custom-call(s32[1]{0:T(128)} %bitcast.place_ref, bf16[4,2048,128]{2,1,0:T(8,128)(2,1)} %get-tuple-element.35.qa_ref, bf16[4,2048,128]{2,1,0:T(8,128)(2,1)} %get-tuple-element.36.ka_ref, ...), custom_call_target="tpu_custom_call" | custom-call | flops 10737418240 | bytes 12582912 | tf_op jit(solution)/shard_map/attend_backward/pallas_call | solution.py:197
  316.7 3.8 convolution_convert_fusion
  321.9 3.7 convolution_convert_fusion.2
  325.9 4.4 fusion.114
  330.3 3.4 add_convert_fusion
  334.3 6.5 %fusion.109 = bf16[1024,768]{1,0:T(8,128)(2,1)} fusion(bf16[512,768]{1,0:T(8,128)(2,1)S(1)} %copy-done.17, bf16[512,768]{1,0:T(8,128)(2,1)S(1)} %copy-done.15, bf16[512,768]{1,0:T(8,128)(2,1)S(1)} %copy-done.13, bf16[512,768]{1,0:T(8,128)(2,1)S(1)} %copy-done.11, bf16[512,1024]{1,0:T(8,128)(2,1)S(1)} %copy-done.35, ...), kind=kOutput, calls=%fused_computation.136 | convolution fusion | flops 3251372032 | bytes 8912896 | tf_op jit(solution)/shard_map/dot_general | solution.py:242
  340.9 85.3 %all-reduce.7.cloned.1.call-done = (bf16[1024,1024]{1,0:T(8,128)(2,1)}, bf16[1024,1024]{1,0:T(8,128)(2,1)}) async-done(((bf16[1024,1024]{1,0:T(8,128)(2,1)}, bf16[1024,1024]{1,0:T(8,128)(2,1)}), (bf16[1024,1024]{1,0:T(8,128)(2,1)}, bf16[1024,1024]{1,0:T(8,128)(2,1)})) %all-reduce.7.cloned.1.call-update) | async-done | bytes 4194320 | tf_op jit(solution)/shard_map/psum | solution.py:360
  426.2 4.8 fusion.66
  433.8 4.7 convert_element_type.429
  438.5 2.5 convert_element_type.430
  442.3 2.4 collective-permute-done.26
  444.8 4.3 collective-permute-done.27
  450.1 3.6 fusion.65
  453.6 78.4 %all-reduce.5.cloned.1.call-done = (bf16[1024,768]{1,0:T(8,128)(2,1)}, bf16[256,1024]{1,0:T(8,128)(2,1)}) async-done(((bf16[1024,768]{1,0:T(8,128)(2,1)}, bf16[256,1024]{1,0:T(8,128)(2,1)}), (bf16[1024,768]{1,0:T(8,128)(2,1)}, bf16[256,1024]{1,0:T(8,128)(2,1)})) %all-reduce.5.cloned.1.call-update) | async-done | bytes 2097168 | tf_op jit(solution)/shard_map/psum | solution.py:362
  532.0 2.2 convert_element_type.424
  534.3 1.9 convert_element_type.423
  (223 shorter events, 44.3 us)
Async XLA Ops:
  7.2 131.4 %copy-start = (bf16[1024,1024]{1,0:T(8,128)(2,1)S(1)}, bf16[1024,1024]{1,0:T(8,128)(2,1)}, u32[]{:S(2)}) copy-start(bf16[1024,1024]{1,0:T(8,128)(2,1)} %param.30) | copy-start | bytes 6291460
  7.2 7.7 %copy-start.30 = (f32[512]{0:T(512)S(1)}, f32[512]{0:T(512)}, u32[]{:S(2)}) copy-start(f32[512]{0:T(512)} %param.25) | copy-start | bytes 6148
  7.2 418.9 %all-reduce.7.cloned.1.call-start = ((), (), s32[]{:S(2)}) async-start(), calls=%async_computation.1 | async-start | bytes 8388608 | tf_op jit(solution)/shard_map/psum | solution.py:360
  12.0 26.4 %collective-permute-start.1 = (bf16[512,1024]{1,0:T(8,128)(2,1)}, bf16[512,1024]{1,0:T(8,128)(2,1)}, u32[]{:S(2)}, u32[]{:S(2)}) collective-permute-start(bf16[512,1024]{1,0:T(8,128)(2,1)} %fusion.60), channel_id=1, source_target_pairs={{0,2},{1,3},{2,0},{3,1},{4,6},{5,7},{6,4},{7,5},{8,10},{9,11},{10,... | collective-permute-start | bytes 3145736 | tf_op jit(solution)/shard_map/ppermute | solution.py:246
  14.9 30.9 %collective-permute-start = (bf16[512,1024]{1,0:T(8,128)(2,1)}, bf16[512,1024]{1,0:T(8,128)(2,1)}, u32[]{:S(2)}, u32[]{:S(2)}) collective-permute-start(bf16[512,1024]{1,0:T(8,128)(2,1)} %fusion.60), channel_id=1, source_target_pairs={{0,1},{1,0},{2,3},{3,2},{4,5},{5,4},{6,7},{7,6},{8,9},{9,8},{10,11... | collective-permute-start | bytes 3145736 | tf_op jit(solution)/shard_map/ppermute | solution.py:246
  38.4 10.6 %collective-permute-start.2 = (bf16[512,1024]{1,0:T(8,128)(2,1)}, bf16[512,1024]{1,0:T(8,128)(2,1)S(1)}, u32[]{:S(2)}, u32[]{:S(2)}) collective-permute-start(bf16[512,1024]{1,0:T(8,128)(2,1)} %collective-permute-done.1), channel_id=1, source_target_pairs={{0,1},{1,0},{2,3},{3,2},{4,5},{5,4},{6,7},{7,6},{8,9},{9,8},{10,11... | collective-permute-start | bytes 3145736 | tf_op jit(solution)/shard_map/ppermute | solution.py:246
  50.9 26.2 %copy-start.3 = (bf16[256,1024]{1,0:T(8,128)(2,1)S(1)}, bf16[256,1024]{1,0:T(8,128)(2,1)}, u32[]{:S(2)}) copy-start(bf16[256,1024]{1,0:T(8,128)(2,1)} %param.26) | copy-start | bytes 1572868
  50.9 29.8 %copy-start.37 = (f32[46]{0:T(128)S(1)}, f32[46]{0:T(128)}, u32[]{:S(2)}) copy-start(f32[46]{0:T(128)} %param.21) | copy-start | bytes 556
  79.4 6.3 %collective-permute-start.4 = (bf16[512,1024]{1,0:T(8,128)(2,1)}, bf16[512,1024]{1,0:T(8,128)(2,1)}, u32[]{:S(2)}, u32[]{:S(2)}) collective-permute-start(bf16[512,1024]{1,0:T(8,128)(2,1)} %convolution_convert_fusion.12), channel_id=1, source_target_pairs={{0,1},{1,0},{2,3},{3,2},{4,5},{5,4},{6,7},{7,6},{8,9},{9,8},{10,11... | collective-permute-start | bytes 3145736 | tf_op jit(solution)/shard_map/ppermute | solution.py:246
  83.4 26.1 %collective-permute-start.14 = (bf16[512,1024]{1,0:T(8,128)(2,1)S(1)}, bf16[512,1024]{1,0:T(8,128)(2,1)S(1)}, u32[]{:S(2)}, u32[]{:S(2)}) collective-permute-start(bf16[512,1024]{1,0:T(8,128)(2,1)S(1)} %fusion.98), channel_id=1, source_target_pairs={{0,2},{1,3},{2,0},{3,1},{4,6},{5,7},{6,4},{7,5},{8,10},{9,11},{10,... | collective-permute-start | bytes 3145736 | tf_op jit(solution)/shard_map/ppermute | solution.py:246
  85.7 23.8 %collective-permute-start.3 = (bf16[512,1024]{1,0:T(8,128)(2,1)S(1)}, bf16[512,1024]{1,0:T(8,128)(2,1)S(1)}, u32[]{:S(2)}, u32[]{:S(2)}) collective-permute-start(bf16[512,1024]{1,0:T(8,128)(2,1)S(1)} %convolution_convert_fusion.14), channel_id=1, source_target_pairs={{0,1},{1,0},{2,3},{3,2},{4,5},{5,4},{6,7},{7,6},{8,9},{9,8},{10,11... | collective-permute-start | bytes 3145736 | tf_op jit(solution)/shard_map/ppermute | solution.py:246
  87.7 43.3 %collective-permute-start.5 = (bf16[512,1024]{1,0:T(8,128)(2,1)S(1)}, bf16[512,1024]{1,0:T(8,128)(2,1)S(1)}, u32[]{:S(2)}, u32[]{:S(2)}) collective-permute-start(bf16[512,1024]{1,0:T(8,128)(2,1)S(1)} %add_convert_fusion.5), channel_id=1, source_target_pairs={{0,2},{1,3},{2,0},{3,1},{4,6},{5,7},{6,4},{7,5},{8,10},{9,11},{10,... | collective-permute-start | bytes 3145736 | tf_op jit(solution)/shard_map/ppermute | solution.py:246
  88.0 47.9 %collective-permute-start.12 = (bf16[512,1024]{1,0:T(8,128)(2,1)S(1)}, bf16[512,1024]{1,0:T(8,128)(2,1)S(1)}, u32[]{:S(2)}, u32[]{:S(2)}) collective-permute-start(bf16[512,1024]{1,0:T(8,128)(2,1)S(1)} %fusion.98), channel_id=1, source_target_pairs={{0,1},{1,0},{2,3},{3,2},{4,5},{5,4},{6,7},{7,6},{8,9},{9,8},{10,11... | collective-permute-start | bytes 3145736 | tf_op jit(solution)/shard_map/ppermute | solution.py:246
  88.8 42.3 %copy-start.27 = (f32[1024]{0:T(1024)S(1)}, f32[1024]{0:T(1024)}, u32[]{:S(2)}) copy-start(f32[1024]{0:T(1024)} %param.27) | copy-start | bytes 12292
  109.5 47.6 %collective-permute-start.15 = (bf16[512,1024]{1,0:T(8,128)(2,1)S(1)}, bf16[512,1024]{1,0:T(8,128)(2,1)S(1)}, u32[]{:S(2)}, u32[]{:S(2)}) collective-permute-start(bf16[512,1024]{1,0:T(8,128)(2,1)S(1)} %collective-permute-done.14), channel_id=1, source_target_pairs={{0,1},{1,0},{2,3},{3,2},{4,5},{5,4},{6,7},{7,6},{8,9},{9,8},{10,11... | collective-permute-start | bytes 3145736 | tf_op jit(solution)/shard_map/ppermute | solution.py:246
  132.8 24.3 %collective-permute-start.8 = (bf16[512,1024]{1,0:T(8,128)(2,1)S(1)}, bf16[512,1024]{1,0:T(8,128)(2,1)S(1)}, u32[]{:S(2)}, u32[]{:S(2)}) collective-permute-start(bf16[512,1024]{1,0:T(8,128)(2,1)S(1)} %add_convert_fusion.4), channel_id=1, source_target_pairs={{0,2},{1,3},{2,0},{3,1},{4,6},{5,7},{6,4},{7,5},{8,10},{9,11},{10,... | collective-permute-start | bytes 3145736 | tf_op jit(solution)/shard_map/ppermute | solution.py:246
  138.6 22.4 %collective-permute-start.6 = (bf16[512,1024]{1,0:T(8,128)(2,1)S(1)}, bf16[512,1024]{1,0:T(8,128)(2,1)S(1)}, u32[]{:S(2)}, u32[]{:S(2)}) collective-permute-start(bf16[512,1024]{1,0:T(8,128)(2,1)S(1)} %add_convert_fusion.4), channel_id=1, source_target_pairs={{0,1},{1,0},{2,3},{3,2},{4,5},{5,4},{6,7},{7,6},{8,9},{9,8},{10,11... | collective-permute-start | bytes 3145736 | tf_op jit(solution)/shard_map/ppermute | solution.py:246
  157.1 5.2 collective-permute-start.9
  176.3 3.8 collective-permute-start.16
  178.2 7.7 %collective-permute-start.10 = (bf16[512,1024]{1,0:T(8,128)(2,1)S(1)}, bf16[512,1024]{1,0:T(8,128)(2,1)S(1)}, u32[]{:S(2)}, u32[]{:S(2)}) collective-permute-start(bf16[512,1024]{1,0:T(8,128)(2,1)S(1)} %convolution_convert_fusion.8), channel_id=1, source_target_pairs={{0,1},{1,0},{2,3},{3,2},{4,5},{5,4},{6,7},{7,6},{8,9},{9,8},{10,11... | collective-permute-start | bytes 3145736 | tf_op jit(solution)/shard_map/ppermute | solution.py:246
  179.6 8.0 %collective-permute-start.13 = (bf16[512,1024]{1,0:T(8,128)(2,1)S(1)}, bf16[512,1024]{1,0:T(8,128)(2,1)S(1)}, u32[]{:S(2)}, u32[]{:S(2)}) collective-permute-start(bf16[512,1024]{1,0:T(8,128)(2,1)S(1)} %convolution_convert_fusion.6), channel_id=1, source_target_pairs={{0,1},{1,0},{2,3},{3,2},{4,5},{5,4},{6,7},{7,6},{8,9},{9,8},{10,11... | collective-permute-start | bytes 3145736 | tf_op jit(solution)/shard_map/ppermute | solution.py:246
  181.4 26.1 %collective-permute-start.17 = (bf16[512,1024]{1,0:T(8,128)(2,1)S(1)}, bf16[512,1024]{1,0:T(8,128)(2,1)S(1)}, u32[]{:S(2)}, u32[]{:S(2)}) collective-permute-start(bf16[512,1024]{1,0:T(8,128)(2,1)S(1)} %add_convert_fusion.1), channel_id=1, source_target_pairs={{0,2},{1,3},{2,0},{3,1},{4,6},{5,7},{6,4},{7,5},{8,10},{9,11},{10,... | collective-permute-start | bytes 3145736 | tf_op jit(solution)/shard_map/ppermute | solution.py:246
  184.5 25.1 %collective-permute-start.7 = (bf16[512,1024]{1,0:T(8,128)(2,1)S(1)}, bf16[512,1024]{1,0:T(8,128)(2,1)S(1)}, u32[]{:S(2)}, u32[]{:S(2)}) collective-permute-start(bf16[512,1024]{1,0:T(8,128)(2,1)S(1)} %convolution_convert_fusion.10), channel_id=1, source_target_pairs={{0,1},{1,0},{2,3},{3,2},{4,5},{5,4},{6,7},{7,6},{8,9},{9,8},{10,11... | collective-permute-start | bytes 3145736 | tf_op jit(solution)/shard_map/ppermute | solution.py:246
  185.9 21.6 %copy-start.44 = (bf16[512,1024]{1,0:T(8,128)(2,1)S(1)}, bf16[512,1024]{1,0:T(8,128)(2,1)}, u32[]{:S(2)}) copy-start(bf16[512,1024]{1,0:T(8,128)(2,1)} %get-tuple-element.63) | copy-start | bytes 3145732
  187.2 41.9 %collective-permute-start.11 = (bf16[512,1024]{1,0:T(8,128)(2,1)S(1)}, bf16[512,1024]{1,0:T(8,128)(2,1)S(1)}, u32[]{:S(2)}, u32[]{:S(2)}) collective-permute-start(bf16[512,1024]{1,0:T(8,128)(2,1)S(1)} %add_convert_fusion.3), channel_id=1, source_target_pairs={{0,2},{1,3},{2,0},{3,1},{4,6},{5,7},{6,4},{7,5},{8,10},{9,11},{10,... | collective-permute-start | bytes 3145736 | tf_op jit(solution)/shard_map/ppermute | solution.py:246
  207.5 21.6 %copy-start.6 = (bf16[512,1024]{1,0:T(8,128)(2,1)S(1)}, bf16[512,1024]{1,0:T(8,128)(2,1)}, u32[]{:S(2)}) copy-start(bf16[512,1024]{1,0:T(8,128)(2,1)} %param.18) | copy-start | bytes 3145732
  207.5 21.6 %copy-start.29 = (f32[1024]{0:T(1024)S(1)}, f32[1024]{0:T(1024)}, u32[]{:S(2)}) copy-start(f32[1024]{0:T(1024)} %param.33) | copy-start | bytes 12292
  232.1 1.2 collective-permute-start.29
  233.3 3.7 collective-permute-start.30
  236.2 25.3 %collective-permute-start.19 = (bf16[512,1024]{1,0:T(8,128)(2,1)}, bf16[512,1024]{1,0:T(8,128)(2,1)}, u32[]{:S(2)}, u32[]{:S(2)}) collective-permute-start(bf16[512,1024]{1,0:T(8,128)(2,1)} %convert_element_type.399), channel_id=1, source_target_pairs={{0,2},{1,3},{2,0},{3,1},{4,6},{5,7},{6,4},{7,5},{8,10},{9,11},{10,... | collective-permute-start | bytes 3145736 | tf_op jit(solution)/shard_map/ppermute | solution.py:246
  237.1 24.4 %copy-start.45 = (bf16[512,1024]{1,0:T(8,128)(2,1)S(1)}, bf16[512,1024]{1,0:T(8,128)(2,1)}, u32[]{:S(2)}) copy-start(bf16[512,1024]{1,0:T(8,128)(2,1)} %get-tuple-element.63) | copy-start | bytes 3145732
  237.1 24.4 %copy-start.49 = (bf16[512,1024]{1,0:T(8,128)(2,1)S(1)}, bf16[512,1024]{1,0:T(8,128)(2,1)}, u32[]{:S(2)}) copy-start(bf16[512,1024]{1,0:T(8,128)(2,1)} %get-tuple-element.87) | copy-start | bytes 3145732
  237.1 7.9 %collective-permute-start.31 = (f32[5120]{0:T(1024)S(1)}, f32[5120]{0:T(1024)S(1)}, u32[]{:S(2)}, u32[]{:S(2)}) collective-permute-start(f32[5120]{0:T(1024)S(1)} %pad_maximum_fusion), channel_id=1, source_target_pairs={{0,4},{4,0},{8,12},{12,8},{16,20},{20,16},{24,28},{28,24},{1,5},{5... | collective-permute-start | bytes 61448 | tf_op jit(solution)/shard_map/ppermute | solution.py:246
  245.0 32.7 %collective-permute-start.18 = (bf16[512,1024]{1,0:T(8,128)(2,1)}, bf16[512,1024]{1,0:T(8,128)(2,1)}, u32[]{:S(2)}, u32[]{:S(2)}) collective-permute-start(bf16[512,1024]{1,0:T(8,128)(2,1)} %convert_element_type.399), channel_id=1, source_target_pairs={{0,1},{1,0},{2,3},{3,2},{4,5},{5,4},{6,7},{7,6},{8,9},{9,8},{10,11... | collective-permute-start | bytes 3145736 | tf_op jit(solution)/shard_map/ppermute | solution.py:246
  245.0 24.2 %collective-permute-start.32 = (f32[5120]{0:T(1024)S(1)}, f32[5120]{0:T(1024)S(1)}, u32[]{:S(2)}, u32[]{:S(2)}) collective-permute-start(f32[5120]{0:T(1024)S(1)} %fusion.136), channel_id=1, source_target_pairs={{0,8},{4,12},{8,0},{12,4},{16,24},{20,28},{24,16},{28,20},{1,9},{5... | collective-permute-start | bytes 61448 | tf_op jit(solution)/shard_map/ppermute | solution.py:246
  261.5 18.7 %collective-permute-start.20 = (bf16[512,1024]{1,0:T(8,128)(2,1)}, bf16[512,1024]{1,0:T(8,128)(2,1)}, u32[]{:S(2)}, u32[]{:S(2)}) collective-permute-start(bf16[512,1024]{1,0:T(8,128)(2,1)} %collective-permute-done.19), channel_id=1, source_target_pairs={{0,1},{1,0},{2,3},{3,2},{4,5},{5,4},{6,7},{7,6},{8,9},{9,8},{10,11... | collective-permute-start | bytes 3145736 | tf_op jit(solution)/shard_map/ppermute | solution.py:246
  268.9 263.1 %all-reduce.5.cloned.1.call-start = ((), (), s32[]{:S(2)}) async-start(), calls=%async_computation | async-start | bytes 4194304 | tf_op jit(solution)/shard_map/psum | solution.py:362
  269.2 8.6 %copy-start.5 = (bf16[256,1024]{1,0:T(8,128)(2,1)S(1)}, bf16[256,1024]{1,0:T(8,128)(2,1)}, u32[]{:S(2)}) copy-start(bf16[256,1024]{1,0:T(8,128)(2,1)} %param.26) | copy-start | bytes 1572868
  269.2 5.2 collective-permute-start.33
  320.5 9.7 %collective-permute-start.22 = (bf16[512,1024]{1,0:T(8,128)(2,1)}, bf16[512,1024]{1,0:T(8,128)(2,1)}, u32[]{:S(2)}, u32[]{:S(2)}) collective-permute-start(bf16[512,1024]{1,0:T(8,128)(2,1)} %convolution_convert_fusion), channel_id=1, source_target_pairs={{0,1},{1,0},{2,3},{3,2},{4,5},{5,4},{6,7},{7,6},{8,9},{9,8},{10,11... | collective-permute-start | bytes 3145736 | tf_op jit(solution)/shard_map/ppermute | solution.py:246
  325.6 100.5 %collective-permute-start.21 = (bf16[512,1024]{1,0:T(8,128)(2,1)}, bf16[512,1024]{1,0:T(8,128)(2,1)}, u32[]{:S(2)}, u32[]{:S(2)}) collective-permute-start(bf16[512,1024]{1,0:T(8,128)(2,1)} %convolution_convert_fusion.2), channel_id=1, source_target_pairs={{0,1},{1,0},{2,3},{3,2},{4,5},{5,4},{6,7},{7,6},{8,9},{9,8},{10,11... | collective-permute-start | bytes 3145736 | tf_op jit(solution)/shard_map/ppermute | solution.py:246
  333.7 92.5 %collective-permute-start.23 = (bf16[512,1024]{1,0:T(8,128)(2,1)}, bf16[512,1024]{1,0:T(8,128)(2,1)}, u32[]{:S(2)}, u32[]{:S(2)}) collective-permute-start(bf16[512,1024]{1,0:T(8,128)(2,1)} %add_convert_fusion), channel_id=1, source_target_pairs={{0,2},{1,3},{2,0},{3,1},{4,6},{5,7},{6,4},{7,5},{8,10},{9,11},{10,... | collective-permute-start | bytes 3145736 | tf_op jit(solution)/shard_map/ppermute | solution.py:246
  431.0 1.2 collective-permute-start.24
  432.2 8.7 %collective-permute-start.25 = (f32[2048]{0:T(1024)S(1)}, f32[2048]{0:T(1024)S(1)}, u32[]{:S(2)}, u32[]{:S(2)}) collective-permute-start(f32[2048]{0:T(1024)S(1)} %fusion.135), channel_id=1, source_target_pairs={{0,2},{1,3},{2,0},{3,1},{4,6},{5,7},{6,4},{7,5},{8,10},{9,11},{10,... | collective-permute-start | bytes 24584 | tf_op jit(solution)/shard_map/ppermute | solution.py:246
  438.5 11.6 %copy-start.9 = (bf16[512,1024]{1,0:T(8,128)(2,1)S(1)}, bf16[512,1024]{1,0:T(8,128)(2,1)}, u32[]{:S(2)}) copy-start(bf16[512,1024]{1,0:T(8,128)(2,1)} %get-tuple-element.97) | copy-start | bytes 3145732
  440.9 3.8 collective-permute-start.26
  444.7 4.3 collective-permute-start.27
  449.1 87.1 %collective-permute-start.28 = (f32[2560]{0:T(1024)S(1)}, f32[2560]{0:T(1024)S(1)}, u32[]{:S(2)}, u32[]{:S(2)}) collective-permute-start(f32[2560]{0:T(1024)S(1)} %add.348), channel_id=1, source_target_pairs={{0,16},{4,20},{8,24},{12,28},{16,0},{20,4},{24,8},{28,12},{1,17},{... | collective-permute-start | bytes 30728 | tf_op jit(solution)/shard_map/ppermute | solution.py:246
  (38 other events, 133.0 us)
Sparse Core Ops, SparseCore 0:
  269.0 157.0 all-reduce.6
  430.4 101.6 all-reduce.4

commit v3 on v2

--- a/solution.py
+++ b/solution.py
@@ -1,4 +1,5 @@
 import functools
+import math
 import jax
 import jax.numpy as jnp
 from jax import lax
@@ -11,6 +12,7 @@
 LANES = 128
 F32 = jnp.float32
 BF16 = jnp.bfloat16
+COST = pl.CostEstimate(flops=1000, transcendentals=0, bytes_accessed=1000)
 
 
 def split3(x):
@@ -123,10 +125,7 @@
         out_specs=(vm,) * (count + 3),
         scratch_shapes=[pltpu.VMEM((heads, span, LANES), BF16)],
         compiler_params=pltpu.CompilerParams(vmem_limit_bytes=60 << 20),
-        cost_estimate=pl.CostEstimate(
-            flops=4 * heads * span * span * LANES // 2, transcendentals=heads * span * span // 2,
-            bytes_accessed=heads * span * LANES * 10,
-        ),
+        cost_estimate=COST,
         name="attend_forward",
     )(place, length, slope_parts, *mixed)
     return res[:count], res[count:]
@@ -134,7 +133,7 @@
 
 def bwd_kernel(count, bk, bq, place_ref, qa_ref, ka_ref, va_ref, *refs):
     heads_refs, grad_refs, out_refs = refs[:count], refs[count : 2 * count], refs[2 * count : 3 * count]
-    da_ref, dqt_ref, dk_ref, dv_ref = refs[3 * count :]
+    sums_ref, da_ref, dqt_ref, dk_ref, dv_ref = refs[3 * count :]
     own = heads_refs[0].shape[0]
     heads, span, _ = qa_ref.shape
     lane = lax.broadcasted_iota(jnp.int32, (1, LANES), 1)
@@ -185,20 +184,29 @@
         pieces = []
         for h in range(heads):
             pieces += [dqt_ref[h, :, rows].T * (HD ** -0.5), dk_ref[h, rows, :HD], dv_ref[h, rows, :HD]]
-        out_refs[j][...] = jnp.concatenate(pieces, axis=1).astype(BF16)
-
-
-def attend_backward(saved, heads_b, grad_heads, place, bk=256, bq=2048):
+        rounded = jnp.concatenate(pieces, axis=1).astype(BF16)
+        out_refs[j][...] = rounded
+        sums = jnp.sum(rounded.astype(F32), axis=0, keepdims=True)
+        sums_ref[...] = sums if j == 0 else sums_ref[...] + sums
+
+
+def attend_backward(saved, heads_b, grad_heads, place, part, parts, bk=256, bq=2048):
     heads, span, _ = saved[0].shape
+    heads = heads // parts
     count = len(heads_b)
     own = span // count
     vm = pl.BlockSpec(memory_space=pltpu.VMEM)
     sm = pl.BlockSpec(memory_space=pltpu.SMEM)
+    aug = pl.BlockSpec((heads, span, LANES), lambda i: (part, 0, 0))
+    flat = pl.BlockSpec((own, heads * HD), lambda i: (0, part))
+    out = pl.BlockSpec((own, heads * 3 * HD), lambda i: (0, 0))
     return pl.pallas_call(
         functools.partial(bwd_kernel, count, bk, bq),
-        out_shape=(jax.ShapeDtypeStruct((own, heads * 3 * HD), BF16),) * count,
-        in_specs=[sm] + [vm] * (3 + 2 * count),
-        out_specs=(vm,) * count,
+        grid=(1,),
+        out_shape=(jax.ShapeDtypeStruct((own, heads * 3 * HD), BF16),) * count
+        + (jax.ShapeDtypeStruct((1, heads * 3 * HD), F32),),
+        in_specs=[sm] + [aug] * 3 + [flat] * (2 * count),
+        out_specs=(out,) * count + (pl.BlockSpec((1, heads * 3 * HD), lambda i: (0, 0)),),
         scratch_shapes=[
             pltpu.VMEM((heads, span, LANES), BF16),
             pltpu.VMEM((heads, HD, span), F32),
@@ -206,10 +214,7 @@
             pltpu.VMEM((heads, span, LANES), F32),
         ],
         compiler_params=pltpu.CompilerParams(vmem_limit_bytes=60 << 20),
-        cost_estimate=pl.CostEstimate(
-            flops=10 * heads * span * span * LANES // 2, transcendentals=heads * span * span // 2,
-            bytes_accessed=heads * span * LANES * 12,
-        ),
+        cost_estimate=COST,
         name="attend_backward",
     )(place, *saved, *heads_b, *grad_heads)
 
@@ -223,23 +228,160 @@
 eps = 1e-05
 
 
-def layer_norm(values, gain, bias):
+def whole_call(kernel, outs, ins, name, smem=0):
+    vm = pl.BlockSpec(memory_space=pltpu.VMEM)
+    sm = pl.BlockSpec(memory_space=pltpu.SMEM)
+    return pl.pallas_call(
+        kernel,
+        out_shape=tuple(jax.ShapeDtypeStruct(shape, kind) for shape, kind in outs),
+        in_specs=[sm] * smem + [vm] * (len(ins) - smem),
+        out_specs=(vm,) * len(outs),
+        compiler_params=pltpu.CompilerParams(vmem_limit_bytes=60 << 20),
+        cost_estimate=COST,
+        name=name,
+    )(*ins)
+
+
+def tn(a, b):
+    return lax.dot_general(a, b, (((0,), (0,)), ((), ())), preferred_element_type=F32)
+
+
+def weight_kernel(count, spots, based, *refs):
+    out_ref = refs[-1]
+    for n, (row, column) in enumerate(spots):
+        lefts, rights = [refs[m * count : (m + 1) * count] for m in (2 * n, 2 * n + 1)]
+        rows, width = lefts[0].shape[1], rights[0].shape[1]
+        for top in range(0, rows, 256):
+            size = min(256, rows - top)
+            total = tn(lefts[0][:, top : top + size], rights[0][...])
+            for left, right in zip(lefts[1:], rights[1:]):
+                total = total + tn(left[:, top : top + size], right[...])
+            spot = (slice(row + top, row + top + size), slice(column, column + width))
+            if based:
+                total = total + refs[-2][spot]
+            out_ref[spot] = total.astype(out_ref.dtype)
+
+
+def weight_grads(*groups, base=None, kind=BF16, stack=False):
+    count = len(groups[0][0])
+    ins = [x for lefts, rights in groups for x in list(lefts) + list(rights)]
+    spots, row, column = [], 0, 0
+    for lefts, rights in groups:
+        spots.append((row, column))
+        row, column = (row + lefts[0].shape[1], 0) if stack else (0, column + rights[0].shape[1])
+    last = groups[-1]
+    shape = (spots[-1][0] + last[0][0].shape[1], spots[-1][1] + last[1][0].shape[1])
+    if base is not None:
+        ins.append(base)
+    kernel = functools.partial(weight_kernel, count, spots, base is not None)
+    return whole_call(kernel, [(shape, kind)], ins, "weight_grads")[0]
+
+
+def through_kernel(count, parts, w_ref, *refs):
+    outs = refs[count * parts :]
+    width = w_ref.shape[1] // parts
+    for j in range(count):
+        total = nt(refs[j * parts][...], w_ref[:, :width])
+        for p in range(1, parts):
+            total = total + nt(refs[j * parts + p][...], w_ref[:, p * width : (p + 1) * width])
+        outs[j][...] = total.astype(BF16)
+
+
+def through(blocks, w):
+    count, parts = len(blocks), len(blocks[0])
+    shape = (blocks[0][0].shape[0], w.shape[0])
+    ins = [w] + [x for block in blocks for x in block]
+    return list(whole_call(functools.partial(through_kernel, count, parts), [(shape, BF16)] * count, ins, "through"))
+
+
+def unit_of(values):
     centre = jnp.mean(values, axis=-1, keepdims=True)
     shifted = values - centre
-    spread = jnp.mean(shifted * shifted, axis=-1, keepdims=True)
-    factor = lax.rsqrt(spread + eps)
-    unit_rows = shifted * factor
-    return (unit_rows * gain + bias, unit_rows, factor)
-
-
-def norm_back(grad_rows, unit_rows, factor, gain):
-    scaled = grad_rows * gain
-    inner = jnp.mean(scaled * unit_rows, axis=-1, keepdims=True)
-    return factor * (scaled - jnp.mean(scaled, axis=-1, keepdims=True) - unit_rows * inner)
-
-
-def tn(a, b):
-    return lax.dot_general(a, b, (((0,), (0,)), ((), ())), preferred_element_type=F32)
+    factor = lax.rsqrt(jnp.mean(shifted * shifted, axis=-1, keepdims=True) + eps)
+    return shifted * factor, factor
+
+
+def norm_in_kernel(x_ref, gain_ref, bias_ref, out_ref):
+    unit, _ = unit_of(x_ref[...].astype(F32))
+    out_ref[...] = (unit * gain_ref[...] + bias_ref[...]).astype(BF16)
+
+
+def norm_mid_kernel(x_ref, near_ref, far_ref, b_ref, gain_ref, bias_ref, mid_ref, out_ref):
+    mid = x_ref[...].astype(F32) + (near_ref[...].astype(F32) + far_ref[...].astype(F32)) + b_ref[...]
+    mid_ref[...] = mid
+    unit, _ = unit_of(mid)
+    out_ref[...] = (unit * gain_ref[...] + bias_ref[...]).astype(BF16)
+
+
+def back_of(grad, values, gain):
+    unit, factor = unit_of(values)
+    d = grad * gain
+    inner = jnp.mean(d * unit, axis=-1, keepdims=True)
+    sums = [jnp.sum(grad * unit, axis=0, keepdims=True), jnp.sum(grad, axis=0, keepdims=True)]
+    return factor * (d - jnp.mean(d, axis=-1, keepdims=True) - unit * inner), sums
+
+
+def norm_mid_back_kernel(mid_ref, near_ref, far_ref, top_ref, live_ref, gain_ref, grad_ref, rounded_ref, sums_ref):
+    grad = near_ref[...].astype(F32) + far_ref[...].astype(F32)
+    back, sums = back_of(grad, mid_ref[...], gain_ref[...])
+    top = top_ref[...].astype(F32) * live_ref[...]
+    grad_mid = top + back
+    grad_ref[...] = grad_mid
+    rounded_ref[...] = grad_mid.astype(BF16)
+    rows = [jnp.sum(top, axis=0, keepdims=True), jnp.sum(grad_mid, axis=0, keepdims=True)] + sums
+    sums_ref[...] = jnp.concatenate(rows, axis=0)
+
+
+def norm_in_back_kernel(x_ref, near_ref, far_ref, mid_ref, gain_ref, grad_ref, sums_ref):
+    grad = near_ref[...].astype(F32) + far_ref[...].astype(F32)
+    back, sums = back_of(grad, x_ref[...].astype(F32), gain_ref[...])
+    grad_ref[...] = (mid_ref[...] + back).astype(BF16)
+    sums_ref[...] = jnp.concatenate(sums, axis=0)
+
+
+def mlp_kernel(count, tile, w_up_ref, w_down_ref, b_up_ref, *refs):
+    n2_refs, top_refs, act_refs, pre_refs, back_refs = [refs[n * count : (n + 1) * count] for n in range(5)]
+    sums_ref = refs[-1]
+    sums_ref[...] = jnp.zeros_like(sums_ref)
+    root = (2.0 / math.pi) ** 0.5
+
+    for j in range(count):
+
+        def step(i, carry):
+            rows = pl.ds(pl.multiple_of(i * tile, tile), tile)
+            pre = nn(n2_refs[j][rows, :], w_up_ref[...]) + b_up_ref[...]
+            grad = nt(top_refs[j][rows, :], w_down_ref[...])
+            square = pre * pre
+            tanh = jnp.tanh(pre * (root + (root * 0.044715) * square))
+            half = 0.5 + 0.5 * tanh
+            act_refs[j][rows, :] = (pre * half).astype(BF16)
+            slope = half + (0.5 * pre) * (1.0 - tanh * tanh) * (root + (root * 0.134145) * square)
+            inner = (grad * slope).astype(BF16)
+            pre_refs[j][rows, :] = inner
+            sums_ref[...] += jnp.sum(inner.astype(F32), axis=0, keepdims=True)
+            back_refs[j][rows, :] = nt(inner, w_up_ref[...]).astype(BF16)
+            return carry
+
+        lax.fori_loop(0, n2_refs[j].shape[0] // tile, step, 0)
+
+
+def mlp_both(n2, top, w_up, w_down, b_up):
+    count = len(n2)
+    own, width = n2[0].shape
+    hidden = w_up.shape[1]
+    vm = pl.BlockSpec(memory_space=pltpu.VMEM)
+    inner = jax.ShapeDtypeStruct((own, hidden), BF16)
+    outer = jax.ShapeDtypeStruct((own, width), BF16)
+    res = pl.pallas_call(
+        functools.partial(mlp_kernel, count, min(own, 256)),
+        out_shape=(inner,) * (2 * count) + (outer,) * count + (jax.ShapeDtypeStruct((1, hidden), F32),),
+        in_specs=[vm] * (3 + 2 * count),
+        out_specs=(vm,) * (3 * count + 1),
+        compiler_params=pltpu.CompilerParams(vmem_limit_bytes=60 << 20),
+        cost_estimate=COST,
+        name="mlp_both",
+    )(w_up, w_down, b_up.reshape(1, -1), *n2, *top)
+    return list(res[:count]), list(res[count : 2 * count]), list(res[2 * count : -1]), res[-1][0]
 
 
 def swap(x, axis, bit):
@@ -250,21 +392,31 @@
     return [1 << n for n in range(lax.axis_size(axis).bit_length() - 1)]
 
 
-def gather_blocks(x, axis):
+def gather_ring(x, axis):
     blocks = {0: x}
     for bit in bits_of(axis)[1:]:
         blocks.update({j ^ bit: swap(b, axis, bit) for j, b in list(blocks.items())})
-    blocks.update({j ^ 1: swap(b, axis, 1) for j, b in list(blocks.items())})
-    return [blocks[j] for j in range(len(blocks))]
-
-
-def sum_blocks(parts, axis):
-    parts = dict(enumerate(parts))
-    for bit in bits_of(axis):
+    return [blocks[j] for j in sorted(blocks) if j]
+
+
+def gather_chip(blocks, axis):
+    return [x for b in blocks for x in (b, swap(b, axis, 1))]
+
+
+def sum_chip(parts, axis):
+    return [
+        (parts[j].astype(F32) + swap(parts[j + 1], axis, 1).astype(F32)).astype(BF16)
+        for j in range(0, len(parts), 2)
+    ]
+
+
+def sum_ring(parts, axis):
+    parts = {2 * (n + 1): x for n, x in enumerate(parts)}
+    for bit in bits_of(axis)[1:]:
         kept = {}
-        for j in sorted(parts, reverse=True):
-            if not j & bit:
-                kept[j] = parts[j].astype(F32) + swap(parts[j | bit].astype(BF16), axis, bit).astype(F32)
+        for j in sorted({j & ~bit for j in parts}):
+            got = swap(parts[j | bit].astype(BF16), axis, bit).astype(F32)
+            kept[j] = got + parts[j].astype(F32) if j in parts else got
         parts = kept
     return parts[0]
 
@@ -273,6 +425,43 @@
     for bit in bits_of(axis):
         x = x + swap(x, axis, bit)
     return x
+
+
+def gate(*values):
+    return lax.optimization_barrier(values)
+
+
+def half_of(x, upper):
+    rows = x.shape[0] // 2
+    return lax.dynamic_slice_in_dim(x, jnp.where(upper, rows, 0), rows, 0)
+
+
+class DpSum:
+    def __init__(self, x, order, place):
+        self.value, self.got, self.later = x, None, [(True, b) for b in order] + [(False, b) for b in order[::-1]]
+        self.advance(place)
+
+    def advance(self, place):
+        if self.got is not None:
+            halving, bit = self.later.pop(0)
+            upper = (place & bit) != 0
+            x, got = self.value, self.got
+            if halving:
+                x = half_of(x, upper) + got.astype(F32)
+                if not self.later[0][0]:
+                    x = x.astype(BF16)
+            else:
+                x = jnp.concatenate([jnp.where(upper, got, x), jnp.where(upper, x, got)], axis=0)
+            self.value, self.got = x, None
+        if self.later:
+            halving, bit = self.later[0]
+            send = half_of(self.value, (place & bit) == 0).astype(BF16) if halving else self.value
+            self.got = swap(send, "dp", bit)
+
+    def result(self, place):
+        while self.later:
+            self.advance(place)
+        return self.value.astype(F32)
 
 
 def body(
@@ -299,89 +488,177 @@
     place_one = place.astype(jnp.int32).reshape(1)
     own_rows = layer_in.shape[0]
     local_heads = w_out.shape[0] // HD
-
-    in_float = layer_in.astype(F32)
-    normed1, unit1, factor1 = layer_norm(in_float, ln1_gain, ln1_bias)
-    n1 = gather_blocks(normed1.astype(BF16), "tensor")
+    dp_place = lax.axis_index("dp")
+    order_a = bits_of("dp")
+    order_b = order_a[1:] + order_a[:1]
+
+    width = layer_in.shape[1]
+
+    def row(x):
+        return x.reshape(1, -1)
+
+    def tokens_of(kernel, kinds, ins, name, sums=0):
+        outs = [((own_rows, width), kind) for kind in kinds] + [((n, width), F32) for n in ([sums] if sums else [])]
+        return whole_call(kernel, outs, ins, name)
+
+    (n1_own,) = tokens_of(norm_in_kernel, [BF16], (layer_in, row(ln1_gain), row(ln1_bias)), "norm_in")
+    n1_far = gather_ring(n1_own, "tensor")
+    n1 = gather_chip([n1_own], "tensor")
+    near = len(n1)
 
     positions = place * own_rows + jnp.arange(own_rows, dtype=jnp.int32)
     weight = jnp.sum(jnp.where(jnp.arange(lang_weight.shape[0]) == languages[0], lang_weight, 0.0))
-    live = jnp.where(positions < lengths[0], weight, 0.0)
-    grad_top = cotangent.astype(F32) * live[:, None]
-    g_b_down = jnp.sum(grad_top, axis=0)
+    live = jnp.where(positions < lengths[0], weight, 0.0)[:, None]
+    top_own = (cotangent.astype(F32) * live).astype(BF16)
 
     pairs = b_qv.reshape(local_heads, 2, HD)
     bias_three = jnp.stack([pairs[:, 0], jnp.zeros_like(pairs[:, 0]), pairs[:, 1]], axis=1).reshape(1, -1)
-    mixed = [(nn(x, w_qkv) + bias_three).astype(BF16) for x in n1]
+
+    def project(x):
+        return (nn(x, w_qkv) + bias_three).astype(BF16)
+
+    mixed = [project(x) for x in n1]
+    top_own, *rest = gate(top_own, *mixed, *n1_far)
+    mixed, n1_far = rest[:near], rest[near:]
+    top_far = gather_ring(top_own, "tensor")
+    n1 += gather_chip(n1_far, "tensor")
+    mixed += [project(x) for x in n1[near:]]
     slope_parts = slope_table(place * local_heads, local_heads, HEADS)
     heads_b, saved = attend_forward(mixed, place_one, lengths, slope_parts)
-
-    top_gate, mixed_gate = lax.optimization_barrier((grad_top.astype(BF16), mixed[-1]))
-    top = gather_blocks(top_gate, "tensor")
-
-    attn_sum = sum_blocks([nn(x, w_out).astype(BF16) for x in heads_b], "tensor")
-    middle = in_float + attn_sum + b_out
-    normed2, unit2, factor2 = layer_norm(middle, ln2_gain, ln2_bias)
-    n2 = gather_blocks(normed2.astype(BF16), "tensor")
-
-    active, grad_pre = [], []
-    for j in range(groups):
-        pre = nn(n2[j], w_up) + b_up
-        out, pull = jax.vjp(lambda v: jax.nn.gelu(v, approximate=True), pre)
-        active.append(out.astype(BF16))
-        grad_pre.append(pull(nt(top[j], w_down))[0].astype(BF16))
-    grad_norm2 = sum_blocks([nt(x, w_up).astype(BF16) for x in grad_pre], "tensor")
-    mlp_sum = sum_blocks([nn(x, w_down).astype(BF16) for x in active], "tensor")
-    output = middle + mlp_sum + b_down
-
-    def weight_grad(lefts, rights):
-        return tn(jnp.concatenate(lefts, axis=0), jnp.concatenate(rights, axis=0))
-
-    g_w_down = weight_grad(active, top)
-    g_w_up = weight_grad(n2, grad_pre)
-    g_b_up = sum(jnp.sum(x.astype(F32), axis=0) for x in grad_pre)
-
-    g_ln2_gain = jnp.sum(grad_norm2 * unit2, axis=0)
-    g_ln2_bias = jnp.sum(grad_norm2, axis=0)
-    grad_middle = grad_top + norm_back(grad_norm2, unit2, factor2, ln2_gain)
-    g_b_out = jnp.sum(grad_middle, axis=0)
-    gm = gather_blocks(grad_middle.astype(BF16), "tensor")
-    grad_heads = [nt(x, w_out).astype(BF16) for x in gm]
-    grad_mixed = attend_backward(saved, heads_b, grad_heads, place_one)
-    g_w_out = weight_grad(heads_b, gm)
-    column_sums = sum(jnp.sum(x.astype(F32), axis=0) for x in grad_mixed).reshape(local_heads, 3, HD)
+    rest = gate(*heads_b, *top_far)
+    heads_b, top_far = list(rest[:groups]), list(rest[groups:])
+
+    parts = [nn(x, w_out).astype(BF16) for x in heads_b[near:]]
+    far_sum = sum_chip(parts, "tensor")
+    rest = gate(*heads_b[:near], *far_sum)
+    heads_b[:near], far_sum = rest[:near], rest[near:]
+    attn_far = sum_ring(far_sum, "tensor")
+    parts = [nn(x, w_out).astype(BF16) for x in heads_b[:near]]
+    attn_near = sum_chip(parts, "tensor")[0]
+    top = gather_chip([top_own] + top_far, "tensor")
+    middle, n2_own = tokens_of(
+        norm_mid_kernel, [F32, BF16], (layer_in, attn_near, attn_far, row(b_out), row(ln2_gain), row(ln2_bias)), "norm_mid"
+    )
+    n2_far = gather_ring(n2_own, "tensor")
+    n2 = gather_chip([n2_own], "tensor")
+
+    active, grad_pre, back, up_sums = mlp_both(n2, top[:near], w_up, w_down, b_up)
+    square = w_up.shape[0] == w_up.shape[1]
+
+    def mlp_weight_grads(lows, highs, **more):
+        if square:
+            return [weight_grads(lows, highs, stack=True, **more)]
+        return [weight_grads(lows, **more), weight_grads(highs, **more)]
+
+    near_sums = mlp_weight_grads((active, top[:near]), (n2, grad_pre), kind=F32)
+    rest = gate(*back, *n2_far, *near_sums)
+    back, n2_far, near_sums = list(rest[:near]), list(rest[near : -len(near_sums)]), rest[-len(near_sums) :]
+    n2 += gather_chip(n2_far, "tensor")
+    far_active, far_pre, far_back, far_sums = mlp_both(n2[near:], top[near:], w_up, w_down, b_up)
+    g_b_up = up_sums + far_sums
+    far_sum = sum_chip(far_back, "tensor")
+    rest = gate(*far_sum, *far_active, *far_pre, *back, *active)
+    far_sum, rest = list(rest[: len(far_sum)]), list(rest[len(far_sum) :])
+    count = groups - near
+    far_active, far_pre, back, active = rest[:count], rest[count : 2 * count], rest[2 * count : -near], rest[-near:]
+    norm2_far = sum_ring(far_sum, "tensor")
+    groups_of_far = (far_active, top[near:]), (n2[near:], far_pre)
+    if square:
+        mlp_grads = [weight_grads(*groups_of_far, base=near_sums[0], stack=True)]
+    else:
+        mlp_grads = [weight_grads(g, base=base) for g, base in zip(groups_of_far, near_sums)]
+    *mlp_grads, back[0] = gate(*mlp_grads, back[0])
+    mlp_grads = [lax.psum_scatter(x, "dp", scatter_dimension=0, tiled=True) for x in mlp_grads]
+    active += far_active
+    norm2_near = sum_chip(back, "tensor")[0]
+
+    grad_middle, gm_own, mid_sums = tokens_of(
+        norm_mid_back_kernel,
+        [F32, BF16],
+        (middle, norm2_near, norm2_far, cotangent, live, row(ln2_gain)),
+        "norm_mid_back",
+        4,
+    )
+    *active, gm_own, dp_place = gate(*active, gm_own, dp_place)
+    gm_far = gather_ring(gm_own, "tensor")
+    gm = gather_chip([gm_own], "tensor")
+
+    mlp_sums = sum_chip([nn(x, w_down).astype(BF16) for x in active], "tensor")
+    grad_heads = through([[x] for x in gm], w_out)
+    rest = gate(*gm_far, *grad_heads, *mlp_sums, dp_place)
+    dp_place = rest[-1]
+    count = len(gm_far)
+    gm_far, grad_heads, mlp_sums = list(rest[:count]), list(rest[count : count + near]), rest[count + near : -1]
+    gm += gather_chip(gm_far, "tensor")
+    grad_heads += through([[x] for x in gm[near:]], w_out)
+    mlp_far = sum_ring(mlp_sums[1:], "tensor")
+
+    parts = 2 if local_heads % 4 == 0 else 1
+    grad_mixed, w_sums, columns, w_cols = [], [], [], w_qkv.shape[1] // parts
+    for part in range(parts):
+        *piece, sums = attend_backward(saved, heads_b, grad_heads, place_one, part, parts)
+        *grad_heads, piece[0], dp_place = gate(*grad_heads, piece[0], dp_place)
+        columns.append(sums[0])
+        if w_sums:
+            w_sums[-1].advance(dp_place)
+            w_sums[-1].value, mlp_far, piece[near] = gate(w_sums[-1].value, mlp_far, piece[near])
+        grad_mixed.append(piece)
+        if part == 0:
+            dp_place, *mlp_grads = gate(dp_place, *mlp_grads)
+            mlp_grads = [lax.all_gather(x, "dp", axis=0, tiled=True) for x in mlp_grads]
+        if part < parts - 1:
+            w_part = weight_grads((n1, piece), (gm, heads_b))
+            *grad_heads, w_part, dp_place = gate(*grad_heads, w_part, dp_place)
+            w_sums.append(DpSum(w_part, order_a, dp_place))
+    blocks = [[piece[j] for piece in grad_mixed] for j in range(groups)]
+    far_sum = sum_chip(through(blocks[near:], w_qkv), "tensor")
+    *far_sum, n1[0], blocks[0][0], dp_place = gate(*far_sum, n1[0], blocks[0][0], dp_place)
+    norm1_far = sum_ring(far_sum, "tensor")
+    last = [(n1, grad_mixed[-1])] + ([(gm, heads_b)] if parts == 1 else [])
+    w_part = weight_grads(*last)
+    blocks[0][0], w_part = gate(blocks[0][0], w_part)
+    w_sums.append(DpSum(w_part, order_a, dp_place))
+    norm1_near = sum_chip(through(blocks[:near], w_qkv), "tensor")[0]
+    for _ in range(2):
+        norm1_near, dp_place = gate(norm1_near, dp_place)
+        for item in w_sums:
+            item.advance(dp_place)
+        rest = gate(norm1_near, *[item.value for item in w_sums])
+        norm1_near = rest[0]
+        for item, value in zip(w_sums, rest[1:]):
+            item.value = value
+    norm1_near, dp_place, *mlp_grads = gate(norm1_near, dp_place, *mlp_grads)
+    down, up = (mlp_grads[0][: w_down.shape[0]], mlp_grads[0][w_down.shape[0] :]) if square else mlp_grads
+    w_parts = [item.result(dp_place) for item in w_sums]
+    out = w_parts[0][:, w_cols:].T
+    qkv = jnp.concatenate([w_parts[0][:, :w_cols]] + w_parts[1:], axis=1)
+    column_sums = jnp.concatenate(columns).reshape(local_heads, 3, HD)
     g_b_qv = jnp.stack([column_sums[:, 0], column_sums[:, 2]], axis=1).reshape(-1)
-    g_w_qkv = weight_grad(n1, grad_mixed)
-    grad_norm1 = sum_blocks([nt(x, w_qkv).astype(BF16) for x in grad_mixed], "tensor")
-    g_ln1_gain = jnp.sum(grad_norm1 * unit1, axis=0)
-    g_ln1_bias = jnp.sum(grad_norm1, axis=0)
-    grad_input = grad_middle + norm_back(grad_norm1, unit1, factor1, ln1_gain)
-
-    up, down = lax.psum((g_w_up.astype(BF16), g_w_down.astype(BF16)), "dp")
-    w_rest, up, down = lax.optimization_barrier(((g_w_qkv.astype(BF16), g_w_out.astype(BF16)), up, down))
-    qkv, out = lax.psum(w_rest, "dp")
-
-    width = ln1_gain.shape[0]
-    early = total_of(jnp.concatenate([g_b_down, g_b_out, g_ln2_gain, g_ln2_bias]), "tensor")
-    early = total_of(jnp.concatenate([early, g_b_up]), "dp")
-    late = total_of(jnp.concatenate([g_ln1_gain, g_ln1_bias]), "tensor")
-    late = total_of(jnp.concatenate([late, g_b_qv]), "dp")
-    shared = [early[n * width : (n + 1) * width] for n in range(4)]
-    g_b_up = early[4 * width :]
+    grad_input, in_sums = tokens_of(
+        norm_in_back_kernel, [BF16], (layer_in, norm1_near, norm1_far, grad_middle, row(ln1_gain)), "norm_in_back", 2
+    )
+    down, up = down.astype(F32), up.astype(F32)
+    output = middle + (mlp_sums[0].astype(F32) + mlp_far) + b_down
+
+    total = total_of(jnp.concatenate([mid_sums.reshape(-1), in_sums.reshape(-1)]), "tensor")
+    total = total_of(jnp.concatenate([total, g_b_up, g_b_qv]), "dp")
+    shared = [total[n * width : (n + 1) * width] for n in range(6)]
+    hidden = b_up.shape[0]
+    g_b_up, g_b_qv = total[6 * width : 6 * width + hidden], total[6 * width + hidden :]
     return (
         output.astype(BF16),
-        grad_input.astype(BF16),
-        late[:width],
-        late[width : 2 * width],
-        qkv.astype(F32),
-        late[2 * width :],
-        out.astype(F32),
+        grad_input,
+        shared[4],
+        shared[5],
+        qkv,
+        g_b_qv,
+        out,
         shared[1],
         shared[2],
         shared[3],
-        up.astype(F32),
+        up,
         g_b_up,
-        down.astype(F32),
+        down,
         shared[0],
     )
 

time: 553 us -> 440 us (0.80)
  waiting for transfers between devices: 308 us -> 143 us
  Pallas kernels: 60.3 us -> 165 us
  matrix products: 103 us -> 29.5 us
  local copies, waits for them, and re-layouts: 3.2 us -> 11.8 us
  other arithmetic: 29.3 us -> 36.9 us
  starting transfers between devices: 24.6 us -> 31.3 us
    psum x2 -> x0, waiting for transfers between devices: 164 us -> none  [the longest x1 85.3 us: body(): up, down = lax.psum((g_w_up.astype(BF16), g_w_down.astype(BF16)), 'dp')]
    pallas_call x1 -> x16, Pallas kernels: 34.1 us -> 138 us  [the longest x12 75.1 us: whole_call(): pl.pallas_call(kernel, out_shape=tuple((jax.ShapeDtypeStruct(shape, kind)...]
    dot_general x20 -> x0, matrix products: 65.7 us -> none  [the longest x16 41.2 us: nt(): lax.dot_general(a, b, (((1,), (1,)), ((), ())), preferred_element_type=F32)]
    reduce_sum x9 -> x0, other arithmetic: 7.87 us -> none  [the longest x1 2.99 us: body(): g_b_out = jnp.sum(grad_middle, axis=0)]
    dot_general x16 -> x12, matrix products: 36.9 us -> 29.5 us  [nn(): return jnp.dot(a, b, preferred_element_type=F32)]
    ppermute x34 -> x41, starting transfers between devices: 24.3 us -> 30.8 us  [swap(): lax.ppermute(x, axis, [(i, i ^ bit) for i in range(lax.axis_size(axis))])]
    convert_element_type x9 -> x16, other arithmetic: 19.3 us -> 24.9 us  [the longest x5 8.97 us: sum_chip(): (parts[j].astype(F32) + swap(parts[j + 1], axis, 1).astype(F32)).astype(B...]
    ppermute x34 -> x41, waiting for transfers between devices: 145 us -> 143 us  [swap(): lax.ppermute(x, axis, [(i, i ^ bit) for i in range(lax.axis_size(axis))])]
  transfers between devices with their start and end apart: 36 -> 43, of which waited for: 14 -> 19; matrix products, arithmetic and copies ran while one was open for 20% -> 15% of each run, Pallas kernels for 6% -> 31%
where the time goes in v3:
time: 440 us; the launch traced here: 434 us
  Pallas kernels  165 us (38%)
  waiting for transfers between devices  143 us (32%)
  other arithmetic  36.9 us (8%)
  starting transfers between devices  31.3 us (7%)
  matrix products  29.5 us (7%)
  between operations  16.4 us (4%)
  local copies, waits for them, and re-layouts  11.8 us (3%)
    ppermute x41, waiting for transfers between devices, swap(): lax.ppermute(x, axis, [(i, i ^ bit) for i in range(lax.axis_size(axis))])  143 us
    pallas_call x12, Pallas kernels, whole_call(): pl.pallas_call(kernel, out_shape=tuple((jax.ShapeDtypeStruct(shape, kind)...  75.1 us
    pallas_call x2, Pallas kernels, attend_backward(): pl.pallas_call(functools.partial(bwd_kernel, count, bk, bq), grid=(1,), o...  37 us
    ppermute x41, starting transfers between devices, swap(): lax.ppermute(x, axis, [(i, i ^ bit) for i in range(lax.axis_size(axis))])  30.8 us
    dot_general x12, matrix products, nn(): return jnp.dot(a, b, preferred_element_type=F32)  29.5 us
    pallas_call x2, Pallas kernels, mlp_both(): pl.pallas_call(functools.partial(mlp_kernel, count, min(own, 256)), out_s...  26.4 us
    pallas_call x1, Pallas kernels, attend_forward(): pl.pallas_call(functools.partial(fwd_kernel, count, bq), out_shape=(jax.S...  26.1 us
    convert_element_type x5, other arithmetic, sum_chip(): (parts[j].astype(F32) + swap(parts[j + 1], axis, 1).astype(F32)).astype(B...  8.97 us
  transfers between devices with their start and end apart: 43, of which 19 were waited for; matrix products, arithmetic and copies ran while one was open for 15% of the time, Pallas kernels for 31%

profile of v3, /device:TPU:0, one launch (start us, length us, event | category | flops | bytes accessed | tf_op | source)
XLA Modules:
  0.0 433.9 jit_solution(10730785064319281302)
XLA Ops:
  7.3 3.0 norm_in.1.refs_0_
  10.8 2.5 collective-permute-start.1
  16.4 3.7 add_convert_fusion.12.refs_0_
  20.1 3.2 add_convert_fusion.11.refs_1_
  23.3 14.1 %collective-permute-done.1.refs_2_ = bf16[512,1024]{1,0:T(8,128)(2,1)} collective-permute-done((bf16[512,1024]{1,0:T(8,128)(2,1)}, bf16[512,1024]{1,0:T(8,128)(2,1)}, u32[]{:S(2)}, u32[]{:S(2)}) %collective-permute-start.1) | collective-permute-done | bytes 1048608 | tf_op jit(solution)/shard_map/ppermute | solution.py:388
  39.9 3.1 add_convert_fusion.10.refs_2_
  42.9 3.1 add_convert_fusion.9.refs_3_
  46.0 26.1 %attend_forward.1 = (bf16[512,256]{1,0:T(8,128)(2,1)}, bf16[512,256]{1,0:T(8,128)(2,1)}, bf16[512,256]{1,0:T(8,128)(2,1)}, bf16[512,256]{1,0:T(8,128)(2,1)}, bf1...) custom-call(s32[1]{0:T(128)} %bitcast.place_ref, s32[1]{0:T(128)} %copy.39.length_ref, ...), custom_call_target="tpu_custom_call" | custom-call | flops 1000 | bytes 1000 | tf_op jit(solution)/shard_map/attend_forward/pallas_call | solution.py:121
  78.1 24.0 %collective-permute-done.6 = bf16[512,1024]{1,0:T(8,128)(2,1)S(1)} collective-permute-done((bf16[512,1024]{1,0:T(8,128)(2,1)S(1)}, bf16[512,1024]{1,0:T(8,128)(2,1)S(1)}, u32[]{:S(2)}, u32[]{:S(2)}) %collective-permute-start.6) | collective-permute-done | bytes 1048608 | tf_op jit(solution)/shard_map/ppermute | solution.py:388
  105.1 4.3 norm_mid.1
  112.4 13.2 %mlp_both.2 = (bf16[512,1024]{1,0:T(8,128)(2,1)}, bf16[512,1024]{1,0:T(8,128)(2,1)}, bf16[512,1024]{1,0:T(8,128)(2,1)}, bf16[512,1024]{1,0:T(8,128)(2,1)}, bf16[...) custom-call(bf16[1024,1024]{1,0:T(8,128)(2,1)} %w_up_ref.3, bf16[1024,1024]{1,0:T(8,128)(2,1)} %w_down_ref.3, ...), custom_call_target="tpu_custom_call" | custom-call | flops 1000 | bytes 1000 | tf_op jit(solution)/shard_map/mlp_both/pallas_call | solution.py:375
  125.5 11.3 %weight_grads.4.refs_8_ = f32[2048,1024]{1,0:T(8,128)} custom-call(bf16[512,1024]{1,0:T(8,128)(2,1)} %get-tuple-element.185.refs_0_, bf16[512,1024]{1,0:T(8,128)(2,1)} %get-tuple-element.186.refs_1_, bf16[512,1024]{1,0:T(8,128)(2,1)} %copy-done.2, bf16[512,1024]{1,0:T(8,128)(2,1)} %collective-permute-done.8.refs_3_, ...), custom_call_target="tpu_custom_call" | custom-call | flops 1000 | bytes 1000 | tf_op jit(solution)/shard_map/weight_grads/pallas_call | solution.py:234
  140.5 13.2 %mlp_both.3 = (bf16[512,1024]{1,0:T(8,128)(2,1)}, bf16[512,1024]{1,0:T(8,128)(2,1)}, bf16[512,1024]{1,0:T(8,128)(2,1)}, bf16[512,1024]{1,0:T(8,128)(2,1)}, bf16[...) custom-call(bf16[1024,1024]{1,0:T(8,128)(2,1)} %w_up_ref.3, bf16[1024,1024]{1,0:T(8,128)(2,1)} %w_down_ref.3, ...), custom_call_target="tpu_custom_call" | custom-call | flops 1000 | bytes 1000 | tf_op jit(solution)/shard_map/mlp_both/pallas_call | solution.py:375
  153.9 2.7 collective-permute-done.12
  158.2 12.6 %weight_grads.5 = bf16[2048,1024]{1,0:T(8,128)(2,1)} custom-call(bf16[512,1024]{1,0:T(8,128)(2,1)} %get-tuple-element.187.refs_0_, bf16[512,1024]{1,0:T(8,128)(2,1)} %get-tuple-element.188.refs_1_, bf16[512,1024]{1,0:T(8,128)(2,1)} %collective-permute-done.3.refs_2_, bf16[512,1024]{1,0:T(8,128)(2,1)} %copy-done.14, bf16[512,1024]{1,0:T(8,128)(2,1)} %copy-done.13, ...), custom_call_target="tpu_custom_call" | custom-call | flops 1000 | bytes 1000 | tf_op jit(solution)/shard_map/weight_grads/pallas_call | solution.py:234
  173.1 23.6 %collective-permute-done.14 = bf16[512,1024]{1,0:T(8,128)(2,1)} collective-permute-done((bf16[512,1024]{1,0:T(8,128)(2,1)S(1)}, bf16[512,1024]{1,0:T(8,128)(2,1)}, u32[]{:S(2)}, u32[]{:S(2)}) %collective-permute-start.14) | collective-permute-done | bytes 1048608 | tf_op jit(solution)/shard_map/ppermute | solution.py:388
  196.7 2.9 convert_element_type.320.far_ref
  201.0 6.8 %norm_mid_back.1 = (f32[512,1024]{1,0:T(8,128)}, bf16[512,1024]{1,0:T(8,128)(2,1)}, f32[4,1024]{1,0:T(4,128)}) custom-call(f32[512,1024]{1,0:T(8,128)} %get-tuple-element.152.mid_ref, bf16[512,1024]{1,0:T(8,128)(2,1)} %add_convert_fusion.5.near_ref, f32[512,1024]{1,0:T(8,128)} %convert_element_type.320.far_ref, bf16[512,1024]{1,0:T(8,128)(2,1)} %top_ref.1, ...), custom_call_target="tpu_custom_call" | custom-call | flops 1000 | bytes 1000 | tf_op jit(solution)/shard_map/norm_mid_back/pallas_call | solution.py:234
  213.0 3.3 through.4
  216.3 3.9 add_convert_fusion.4
  220.2 3.5 add_convert_fusion.3
  223.7 14.7 %collective-permute-done.15.refs_0_.refs_10_ = bf16[512,1024]{1,0:T(8,128)(2,1)} collective-permute-done((bf16[512,1024]{1,0:T(8,128)(2,1)S(1)}, bf16[512,1024]{1,0:T(8,128)(2,1)}, u32[]{:S(2)}, u32[]{:S(2)}) %collective-permute-start.15) | collective-permute-done | bytes 1048608 | tf_op jit(solution)/shard_map/ppermute | solution.py:388
  238.4 2.9 collective-permute-done.19.refs_1_.refs_11_
  242.3 3.2 through.5
  245.5 18.4 %attend_backward.2 = (bf16[512,384]{1,0:T(8,128)(2,1)}, bf16[512,384]{1,0:T(8,128)(2,1)}, bf16[512,384]{1,0:T(8,128)(2,1)}, bf16[512,384]{1,0:T(8,128)(2,1)}, f32[1,384]{1,0:T(1,128)}) custom-call(s32[1]{0:T(128)} %bitcast.place_ref, bf16[4,2048,128]{2,1,0:T(8,128)(2,1)} %get-tuple-element.196.qa_ref, bf16[4,2048,128]{2,1,0:T(8,128)(2,1)} %get-tuple-element.197.ka_ref, ...), custom_call_target="tpu_custom_call" | custom-call | flops 1000 | bytes 1000 | tf_op jit(solution)/shard_map/attend_backward/pallas_call | solution.py:203
  264.3 8.6 %weight_grads.6 = bf16[1024,640]{1,0:T(8,128)(2,1)} custom-call(bf16[512,1024]{1,0:T(8,128)(2,1)} %norm_in.1.refs_0_, bf16[512,1024]{1,0:T(8,128)(2,1)} %collective-permute-done.refs_1_, bf16[512,1024]{1,0:T(8,128)(2,1)} %collective-permute-done.1.refs_2_, bf16[512,1024]{1,0:T(8,128)(2,1)} %collective-permute-done.2.refs_3_, ...), custom_call_target="tpu_custom_call" | custom-call | flops 1000 | bytes 1000 | tf_op jit(solution)/shard_map/weight_grads/pallas_call | solution.py:234
  276.7 12.5 %collective-permute-done.21 = bf16[512,1024]{1,0:T(8,128)(2,1)S(1)} collective-permute-done((bf16[512,1024]{1,0:T(8,128)(2,1)S(1)}, bf16[512,1024]{1,0:T(8,128)(2,1)S(1)}, u32[]{:S(2)}, u32[]{:S(2)}) %collective-permute-start.21) | collective-permute-done | bytes 1048608 | tf_op jit(solution)/shard_map/ppermute | solution.py:388
  289.5 18.6 %attend_backward.3 = (bf16[512,384]{1,0:T(8,128)(2,1)}, bf16[512,384]{1,0:T(8,128)(2,1)}, bf16[512,384]{1,0:T(8,128)(2,1)}, bf16[512,384]{1,0:T(8,128)(2,1)}, f32[1,384]{1,0:T(1,128)}) custom-call(s32[1]{0:T(128)} %bitcast.place_ref, bf16[4,2048,128]{2,1,0:T(8,128)(2,1)} %get-tuple-element.196.qa_ref, bf16[4,2048,128]{2,1,0:T(8,128)(2,1)} %get-tuple-element.197.ka_ref, ...), custom_call_target="tpu_custom_call" | custom-call | flops 1000 | bytes 1000 | tf_op jit(solution)/shard_map/attend_backward/pallas_call | solution.py:203
  310.3 5.2 %through.6 = (bf16[512,1024]{1,0:T(8,128)(2,1)}, bf16[512,1024]{1,0:T(8,128)(2,1)}) custom-call(bf16[1024,768]{1,0:T(8,128)(2,1)} %w_ref.7, bf16[512,384]{1,0:T(8,128)(2,1)} %get-tuple-element.207.refs_6_.refs_0_, bf16[512,384]{1,0:T(8,128)(2,1)} %get-tuple-element.223.refs_1_.refs_6_, bf16[512,384]{1,0:T(8,128)(2,1)} %get-tuple-element.208.refs_7_.refs_2_, ...), custom_call_target="tpu_custom_call" | custom-call | flops 1000 | bytes 1000 | tf_op jit(solution)/shard_map/through/pallas_call | solution.py:234
  315.8 2.6 collective-permute-done.22
  318.4 2.6 add_convert_fusion.1
  321.0 5.9 %weight_grads.7 = bf16[1024,384]{1,0:T(8,128)(2,1)} custom-call(bf16[512,1024]{1,0:T(8,128)(2,1)} %norm_in.1.refs_0_, bf16[512,1024]{1,0:T(8,128)(2,1)} %collective-permute-done.refs_1_, bf16[512,1024]{1,0:T(8,128)(2,1)} %collective-permute-done.1.refs_2_, bf16[512,1024]{1,0:T(8,128)(2,1)} %collective-permute-done.2.refs_3_, ...), custom_call_target="tpu_custom_call" | custom-call | flops 1000 | bytes 1000 | tf_op jit(solution)/shard_map/weight_grads/pallas_call | solution.py:234
  326.9 5.3 %through.7 = (bf16[512,1024]{1,0:T(8,128)(2,1)}, bf16[512,1024]{1,0:T(8,128)(2,1)}) custom-call(bf16[1024,768]{1,0:T(8,128)(2,1)} %w_ref.7, bf16[512,384]{1,0:T(8,128)(2,1)} %get-tuple-element.231.refs_4_.refs_0_, bf16[512,384]{1,0:T(8,128)(2,1)} %get-tuple-element.229.refs_4_.refs_1_, bf16[512,384]{1,0:T(8,128)(2,1)} %get-tuple-element.206.refs_5_.refs_2_, ...), custom_call_target="tpu_custom_call" | custom-call | flops 1000 | bytes 1000 | tf_op jit(solution)/shard_map/through/pallas_call | solution.py:234
  334.9 3.4 add_convert_fusion.2
  342.0 3.0 add_convert_fusion.near_ref
  346.1 2.7 collective-permute-start.26
  348.8 2.7 collective-permute-done.25
  352.1 11.7 %collective-permute-done.28 = bf16[512,1024]{1,0:T(8,128)(2,1)} collective-permute-done((bf16[512,1024]{1,0:T(8,128)(2,1)}, bf16[512,1024]{1,0:T(8,128)(2,1)}, u32[]{:S(2)}, u32[]{:S(2)}) %collective-permute-start.28) | collective-permute-done | bytes 1048608 | tf_op jit(solution)/shard_map/ppermute | solution.py:388
  363.7 2.8 convert_element_type.351.far_ref
  366.6 2.6 collective-permute-start.34
  369.7 5.5 %norm_in_back.1 = (bf16[512,1024]{1,0:T(8,128)(2,1)}, f32[2,1024]{1,0:T(2,128)}) custom-call(bf16[512,1024]{1,0:T(8,128)(2,1)} %x_ref.5, bf16[512,1024]{1,0:T(8,128)(2,1)} %add_convert_fusion.near_ref, f32[512,1024]{1,0:T(8,128)} %convert_element_type.351.far_ref, f32[512,1024]{1,0:T(8,128)} %get-tuple-element.248.mid_ref, f32[1,1024]{1,0:T(1,128)} %bitcast.54), custom_call_target="tpu_custom_call" | custom-call | flops 1000 | bytes 1000 | tf_op jit(solution)/shard_map/norm_in_back/pallas_call | solution.py:234
  376.0 4.5 %collective-permute-done.37 = bf16[128,384]{1,0:T(8,128)(2,1)S(1)} collective-permute-done((bf16[128,384]{1,0:T(8,128)(2,1)S(1)}, bf16[128,384]{1,0:T(8,128)(2,1)S(1)}, u32[]{:S(2)}, u32[]{:S(2)}) %collective-permute-start.37) | collective-permute-done | bytes 98336 | tf_op jit(solution)/shard_map/ppermute | solution.py:388
  381.2 3.3 collective-permute-done.30
  392.1 3.9 collective-permute-done.32
  399.0 3.0 collective-permute-done.35
  403.8 4.4 %slice_convert_fusion = (f32[1024,1024]{1,0:T(8,128)}, f32[1024,1024]{1,0:T(8,128)}) fusion(bf16[2048,1024]{1,0:T(8,128)(2,1)S(1)} %copy-done.7), kind=kLoop, calls=%fused_computation.1 | loop fusion | flops 2097152 | bytes 12582912 | tf_op jit(solution)/shard_map/convert_element_type | solution.py:640
  410.5 10.0 %collective-permute-done.36 = bf16[512,640]{1,0:T(8,128)(2,1)S(1)} collective-permute-done((bf16[512,640]{1,0:T(8,128)(2,1)S(1)}, bf16[512,640]{1,0:T(8,128)(2,1)S(1)}, u32[]{:S(2)}, u32[]{:S(2)}) %collective-permute-start.36) | collective-permute-done | bytes 655392 | tf_op jit(solution)/shard_map/ppermute | solution.py:388
  422.0 2.5 copy.32
  (206 shorter events, 66.8 us)
Async XLA Ops:
  7.2 256.7 %reduce-scatter.2.cloned.1.call-start = ((), (), s32[]{:S(2)}) async-start(), calls=%async_computation.1 | async-start | bytes 4718592 | tf_op jit(solution)/shard_map/reduce_scatter | solution.py:571
  10.3 9.8 %collective-permute-start = (bf16[512,1024]{1,0:T(8,128)(2,1)}, bf16[512,1024]{1,0:T(8,128)(2,1)}, u32[]{:S(2)}, u32[]{:S(2)}) collective-permute-start(bf16[512,1024]{1,0:T(8,128)(2,1)} %norm_in.1.refs_0_), channel_id=1, source_target_pairs={{0,1},{1,0},{2,3},{3,2},{4,5},{5,4},{6,7},{7,6},{8,9},{9,8},{10,11... | collective-permute-start | bytes 3145736 | tf_op jit(solution)/shard_map/ppermute | solution.py:388
  10.8 26.7 %collective-permute-start.1 = (bf16[512,1024]{1,0:T(8,128)(2,1)}, bf16[512,1024]{1,0:T(8,128)(2,1)}, u32[]{:S(2)}, u32[]{:S(2)}) collective-permute-start(bf16[512,1024]{1,0:T(8,128)(2,1)} %norm_in.1.refs_0_), channel_id=1, source_target_pairs={{0,2},{1,3},{2,0},{3,1},{4,6},{5,7},{6,4},{7,5},{8,10},{9,11},{10,... | collective-permute-start | bytes 3145736 | tf_op jit(solution)/shard_map/ppermute | solution.py:388
  16.4 61.2 %copy-start.2 = (bf16[512,1024]{1,0:T(8,128)(2,1)}, bf16[512,1024]{1,0:T(8,128)(2,1)S(1)}, u32[]{:S(2)}) copy-start(bf16[512,1024]{1,0:T(8,128)(2,1)S(1)} %multiply_convert_fusion.refs_2_) | copy-start | bytes 3145732
  20.1 19.7 %copy-start.5 = (bf16[1024,768]{1,0:T(8,128)(2,1)S(1)}, bf16[1024,768]{1,0:T(8,128)(2,1)}, u32[]{:S(2)}) copy-start(bf16[1024,768]{1,0:T(8,128)(2,1)} %w_ref.7) | copy-start | bytes 4718596
  37.4 5.5 %collective-permute-start.2 = (bf16[512,1024]{1,0:T(8,128)(2,1)}, bf16[512,1024]{1,0:T(8,128)(2,1)}, u32[]{:S(2)}, u32[]{:S(2)}) collective-permute-start(bf16[512,1024]{1,0:T(8,128)(2,1)} %collective-permute-done.1.refs_2_), channel_id=1, source_target_pairs={{0,1},{1,0},{2,3},{3,2},{4,5},{5,4},{6,7},{7,6},{8,9},{9,8},{10,11... | collective-permute-start | bytes 3145736 | tf_op jit(solution)/shard_map/ppermute | solution.py:388
  37.4 34.7 %collective-permute-start.3 = (bf16[512,1024]{1,0:T(8,128)(2,1)S(1)}, bf16[512,1024]{1,0:T(8,128)(2,1)}, u32[]{:S(2)}, u32[]{:S(2)}) collective-permute-start(bf16[512,1024]{1,0:T(8,128)(2,1)S(1)} %multiply_convert_fusion.refs_2_), channel_id=1, source_target_pairs={{0,2},{1,3},{2,0},{3,1},{4,6},{5,7},{6,4},{7,5},{8,10},{9,11},{10,... | collective-permute-start | bytes 3145736 | tf_op jit(solution)/shard_map/ppermute | solution.py:388
  46.0 26.1 %copy-start = (bf16[256,1024]{1,0:T(8,128)(2,1)S(1)}, bf16[256,1024]{1,0:T(8,128)(2,1)}, u32[]{:S(2)}) copy-start(bf16[256,1024]{1,0:T(8,128)(2,1)} %w_ref.5) | copy-start | bytes 1572868
  73.6 2.7 collective-permute-start.4
  76.7 26.9 %copy-start.11 = (bf16[512,256]{1,0:T(8,128)(2,1)S(1)}, bf16[512,256]{1,0:T(8,128)(2,1)}, u32[]{:S(2)}) copy-start(bf16[512,256]{1,0:T(8,128)(2,1)} %get-tuple-element.149.refs_0_.refs_12_) | copy-start | bytes 786436
  76.7 25.4 %collective-permute-start.6 = (bf16[512,1024]{1,0:T(8,128)(2,1)S(1)}, bf16[512,1024]{1,0:T(8,128)(2,1)S(1)}, u32[]{:S(2)}, u32[]{:S(2)}) collective-permute-start(bf16[512,1024]{1,0:T(8,128)(2,1)S(1)} %add_convert_fusion.8), channel_id=1, source_target_pairs={{0,2},{1,3},{2,0},{3,1},{4,6},{5,7},{6,4},{7,5},{8,10},{9,11},{10,... | collective-permute-start | bytes 3145736 | tf_op jit(solution)/shard_map/ppermute | solution.py:388
  77.5 26.1 %collective-permute-start.5 = (bf16[512,1024]{1,0:T(8,128)(2,1)S(1)}, bf16[512,1024]{1,0:T(8,128)(2,1)S(1)}, u32[]{:S(2)}, u32[]{:S(2)}) collective-permute-start(bf16[512,1024]{1,0:T(8,128)(2,1)S(1)} %convolution_convert_fusion.4), channel_id=1, source_target_pairs={{0,1},{1,0},{2,3},{3,2},{4,5},{5,4},{6,7},{7,6},{8,9},{9,8},{10,11... | collective-permute-start | bytes 3145736 | tf_op jit(solution)/shard_map/ppermute | solution.py:388
  77.6 32.3 %collective-permute-start.8 = (bf16[512,1024]{1,0:T(8,128)(2,1)S(1)}, bf16[512,1024]{1,0:T(8,128)(2,1)}, u32[]{:S(2)}, u32[]{:S(2)}) collective-permute-start(bf16[512,1024]{1,0:T(8,128)(2,1)S(1)} %multiply_convert_fusion.refs_2_), channel_id=1, source_target_pairs={{0,1},{1,0},{2,3},{3,2},{4,5},{5,4},{6,7},{7,6},{8,9},{9,8},{10,11... | collective-permute-start | bytes 3145736 | tf_op jit(solution)/shard_map/ppermute | solution.py:388
  109.4 3.0 collective-permute-start.7
  109.4 27.5 %collective-permute-start.9 = (bf16[512,1024]{1,0:T(8,128)(2,1)}, bf16[512,1024]{1,0:T(8,128)(2,1)S(1)}, u32[]{:S(2)}, u32[]{:S(2)}) collective-permute-start(bf16[512,1024]{1,0:T(8,128)(2,1)} %get-tuple-element.153.refs_0_.refs_4_), channel_id=1, source_target_pairs={{0,2},{1,3},{2,0},{3,1},{4,6},{5,7},{6,4},{7,5},{8,10},{9,11},{10,... | collective-permute-start | bytes 3145736 | tf_op jit(solution)/shard_map/ppermute | solution.py:388
  109.7 27.4 %collective-permute-start.11 = (bf16[512,1024]{1,0:T(8,128)(2,1)}, bf16[512,1024]{1,0:T(8,128)(2,1)S(1)}, u32[]{:S(2)}, u32[]{:S(2)}) collective-permute-start(bf16[512,1024]{1,0:T(8,128)(2,1)} %collective-permute-done.3.refs_2_), channel_id=1, source_target_pairs={{0,1},{1,0},{2,3},{3,2},{4,5},{5,4},{6,7},{7,6},{8,9},{9,8},{10,11... | collective-permute-start | bytes 3145736 | tf_op jit(solution)/shard_map/ppermute | solution.py:388
  136.8 2.7 collective-permute-start.10
  153.7 2.9 collective-permute-start.12
  170.9 28.7 %copy-start.22 = (bf16[512,1024]{1,0:T(8,128)(2,1)S(1)}, bf16[512,1024]{1,0:T(8,128)(2,1)}, u32[]{:S(2)}) copy-start(bf16[512,1024]{1,0:T(8,128)(2,1)} %get-tuple-element.178) | copy-start | bytes 3145732
  170.9 198.8 %all-gather.2.cloned.1.call-start = ((), (), s32[]{:S(2)}) async-start(), calls=%async_computation.2 | async-start | bytes 4718592 | tf_op jit(solution)/shard_map/all_gather | solution.py:608
  171.3 25.4 %collective-permute-start.14 = (bf16[512,1024]{1,0:T(8,128)(2,1)S(1)}, bf16[512,1024]{1,0:T(8,128)(2,1)}, u32[]{:S(2)}, u32[]{:S(2)}) collective-permute-start(bf16[512,1024]{1,0:T(8,128)(2,1)S(1)} %add_convert_fusion.6), channel_id=1, source_target_pairs={{0,2},{1,3},{2,0},{3,1},{4,6},{5,7},{6,4},{7,5},{8,10},{9,11},{10,... | collective-permute-start | bytes 3145736 | tf_op jit(solution)/shard_map/ppermute | solution.py:388
  171.7 27.9 %collective-permute-start.13 = (bf16[512,1024]{1,0:T(8,128)(2,1)}, bf16[512,1024]{1,0:T(8,128)(2,1)S(1)}, u32[]{:S(2)}, u32[]{:S(2)}) collective-permute-start(bf16[512,1024]{1,0:T(8,128)(2,1)} %get-tuple-element.179), channel_id=1, source_target_pairs={{0,1},{1,0},{2,3},{3,2},{4,5},{5,4},{6,7},{7,6},{8,9},{9,8},{10,11... | collective-permute-start | bytes 3145736 | tf_op jit(solution)/shard_map/ppermute | solution.py:388
  207.8 5.3 %collective-permute-start.16 = (bf16[512,1024]{1,0:T(8,128)(2,1)}, bf16[512,1024]{1,0:T(8,128)(2,1)}, u32[]{:S(2)}, u32[]{:S(2)}) collective-permute-start(bf16[512,1024]{1,0:T(8,128)(2,1)} %get-tuple-element.182.refs_0_.refs_8_), channel_id=1, source_target_pairs={{0,1},{1,0},{2,3},{3,2},{4,5},{5,4},{6,7},{7,6},{8,9},{9,8},{10,11... | collective-permute-start | bytes 3145736 | tf_op jit(solution)/shard_map/ppermute | solution.py:388
  210.0 6.3 %collective-permute-start.17 = (bf16[512,1024]{1,0:T(8,128)(2,1)}, bf16[512,1024]{1,0:T(8,128)(2,1)}, u32[]{:S(2)}, u32[]{:S(2)}) collective-permute-start(bf16[512,1024]{1,0:T(8,128)(2,1)} %convolution_convert_fusion.2), channel_id=1, source_target_pairs={{0,1},{1,0},{2,3},{3,2},{4,5},{5,4},{6,7},{7,6},{8,9},{9,8},{10,11... | collective-permute-start | bytes 3145736 | tf_op jit(solution)/shard_map/ppermute | solution.py:388
  212.7 7.5 %collective-permute-start.18 = (bf16[512,1024]{1,0:T(8,128)(2,1)}, bf16[512,1024]{1,0:T(8,128)(2,1)}, u32[]{:S(2)}, u32[]{:S(2)}) collective-permute-start(bf16[512,1024]{1,0:T(8,128)(2,1)} %convolution_convert_fusion), channel_id=1, source_target_pairs={{0,1},{1,0},{2,3},{3,2},{4,5},{5,4},{6,7},{7,6},{8,9},{9,8},{10,11... | collective-permute-start | bytes 3145736 | tf_op jit(solution)/shard_map/ppermute | solution.py:388
  212.8 25.7 %collective-permute-start.15 = (bf16[512,1024]{1,0:T(8,128)(2,1)S(1)}, bf16[512,1024]{1,0:T(8,128)(2,1)}, u32[]{:S(2)}, u32[]{:S(2)}) collective-permute-start(bf16[512,1024]{1,0:T(8,128)(2,1)S(1)} %copy-done.9), channel_id=1, source_target_pairs={{0,2},{1,3},{2,0},{3,1},{4,6},{5,7},{6,4},{7,5},{8,10},{9,11},{10,... | collective-permute-start | bytes 3145736 | tf_op jit(solution)/shard_map/ppermute | solution.py:388
  238.4 2.9 collective-permute-start.19
  263.9 25.2 %collective-permute-start.21 = (bf16[512,1024]{1,0:T(8,128)(2,1)S(1)}, bf16[512,1024]{1,0:T(8,128)(2,1)S(1)}, u32[]{:S(2)}, u32[]{:S(2)}) collective-permute-start(bf16[512,1024]{1,0:T(8,128)(2,1)S(1)} %copy-done.31), channel_id=1, source_target_pairs={{0,2},{1,3},{2,0},{3,1},{4,6},{5,7},{6,4},{7,5},{8,10},{9,11},{10,... | collective-permute-start | bytes 3145736 | tf_op jit(solution)/shard_map/ppermute | solution.py:388
  275.0 33.0 %collective-permute-start.20 = (bf16[512,640]{1,0:T(8,128)(2,1)}, bf16[512,640]{1,0:T(8,128)(2,1)}, u32[]{:S(2)}, u32[]{:S(2)}) collective-permute-start(bf16[512,640]{1,0:T(8,128)(2,1)} %constant_dynamic-slice_fusion.1), channel_id=1, source_target_pairs={{0,4},{4,0},{8,12},{12,8},{16,20},{20,16},{24,28},{28,24},{1,5},{5... | collective-permute-start | bytes 1966088 | tf_op jit(solution)/shard_map/ppermute | solution.py:388
  315.6 2.9 collective-permute-start.22
  332.2 9.9 %collective-permute-start.23 = (bf16[512,1024]{1,0:T(8,128)(2,1)}, bf16[512,1024]{1,0:T(8,128)(2,1)}, u32[]{:S(2)}, u32[]{:S(2)}) collective-permute-start(bf16[512,1024]{1,0:T(8,128)(2,1)} %get-tuple-element.233), channel_id=1, source_target_pairs={{0,1},{1,0},{2,3},{3,2},{4,5},{5,4},{6,7},{7,6},{8,9},{9,8},{10,11... | collective-permute-start | bytes 3145736 | tf_op jit(solution)/shard_map/ppermute | solution.py:388
  333.2 11.8 %collective-permute-start.24 = (bf16[256,640]{1,0:T(8,128)(2,1)}, bf16[256,640]{1,0:T(8,128)(2,1)}, u32[]{:S(2)}, u32[]{:S(2)}) collective-permute-start(bf16[256,640]{1,0:T(8,128)(2,1)} %dynamic-slice_convert_fusion), channel_id=1, source_target_pairs={{0,8},{4,12},{8,0},{12,4},{16,24},{20,28},{24,16},{28,20},{1,9},{5... | collective-permute-start | bytes 983048 | tf_op jit(solution)/shard_map/ppermute | solution.py:388
  338.3 25.4 %collective-permute-start.28 = (bf16[512,1024]{1,0:T(8,128)(2,1)}, bf16[512,1024]{1,0:T(8,128)(2,1)}, u32[]{:S(2)}, u32[]{:S(2)}) collective-permute-start(bf16[512,1024]{1,0:T(8,128)(2,1)} %add_convert_fusion.1), channel_id=1, source_target_pairs={{0,2},{1,3},{2,0},{3,1},{4,6},{5,7},{6,4},{7,5},{8,10},{9,11},{10,... | collective-permute-start | bytes 3145736 | tf_op jit(solution)/shard_map/ppermute | solution.py:388
  340.6 11.0 %collective-permute-start.25 = (bf16[512,384]{1,0:T(8,128)(2,1)}, bf16[512,384]{1,0:T(8,128)(2,1)S(1)}, u32[]{:S(2)}, u32[]{:S(2)}) collective-permute-start(bf16[512,384]{1,0:T(8,128)(2,1)} %constant_dynamic-slice_fusion), channel_id=1, source_target_pairs={{0,4},{4,0},{8,12},{12,8},{16,20},{20,16},{24,28},{28,24},{1,5},{5... | collective-permute-start | bytes 1179656 | tf_op jit(solution)/shard_map/ppermute | solution.py:388
  346.1 20.4 %collective-permute-start.26 = (bf16[128,640]{1,0:T(8,128)(2,1)S(1)}, bf16[128,640]{1,0:T(8,128)(2,1)S(1)}, u32[]{:S(2)}, u32[]{:S(2)}) collective-permute-start(bf16[128,640]{1,0:T(8,128)(2,1)S(1)} %dynamic-slice_convert_fusion.2), channel_id=1, source_target_pairs={{0,16},{4,20},{8,24},{12,28},{16,0},{20,4},{24,8},{28,12},{1,17},{... | collective-permute-start | bytes 491528 | tf_op jit(solution)/shard_map/ppermute | solution.py:388
  351.7 17.4 %collective-permute-start.27 = (bf16[256,384]{1,0:T(8,128)(2,1)S(1)}, bf16[256,384]{1,0:T(8,128)(2,1)S(1)}, u32[]{:S(2)}, u32[]{:S(2)}) collective-permute-start(bf16[256,384]{1,0:T(8,128)(2,1)S(1)} %dynamic-slice_convert_fusion.1), channel_id=1, source_target_pairs={{0,8},{4,12},{8,0},{12,4},{16,24},{20,28},{24,16},{28,20},{1,9},{5... | collective-permute-start | bytes 589832 | tf_op jit(solution)/shard_map/ppermute | solution.py:388
  366.6 14.6 %collective-permute-start.34 = (bf16[128,640]{1,0:T(8,128)(2,1)S(1)}, bf16[128,640]{1,0:T(8,128)(2,1)S(1)}, u32[]{:S(2)}, u32[]{:S(2)}) collective-permute-start(bf16[128,640]{1,0:T(8,128)(2,1)S(1)} %add_convert_fusion.13), channel_id=1, source_target_pairs={{0,16},{4,20},{8,24},{12,28},{16,0},{20,4},{24,8},{28,12},{1,17},{... | collective-permute-start | bytes 491528 | tf_op jit(solution)/shard_map/ppermute | solution.py:388
  369.2 11.2 %collective-permute-start.37 = (bf16[128,384]{1,0:T(8,128)(2,1)S(1)}, bf16[128,384]{1,0:T(8,128)(2,1)S(1)}, u32[]{:S(2)}, u32[]{:S(2)}) collective-permute-start(bf16[128,384]{1,0:T(8,128)(2,1)S(1)} %dynamic-slice_convert_fusion.3), channel_id=1, source_target_pairs={{0,16},{4,20},{8,24},{12,28},{16,0},{20,4},{24,8},{28,12},{1,17},{... | collective-permute-start | bytes 294920 | tf_op jit(solution)/shard_map/ppermute | solution.py:388
  376.0 4.6 %collective-permute-start.29 = (f32[6144]{0:T(1024)S(1)}, f32[6144]{0:T(1024)S(1)}, u32[]{:S(2)}, u32[]{:S(2)}) collective-permute-start(f32[6144]{0:T(1024)S(1)} %bitcast_dynamic-update-slice_fusion.1), channel_id=1, source_target_pairs={{0,1},{1,0},{2,3},{3,2},{4,5},{5,4},{6,7},{7,6},{8,9},{9,8},{10,11... | collective-permute-start | bytes 73736 | tf_op jit(solution)/shard_map/ppermute | solution.py:388
  380.5 6.8 %collective-permute-start.38 = (bf16[128,384]{1,0:T(8,128)(2,1)S(1)}, bf16[128,384]{1,0:T(8,128)(2,1)S(1)}, u32[]{:S(2)}, u32[]{:S(2)}) collective-permute-start(bf16[128,384]{1,0:T(8,128)(2,1)S(1)} %add_convert_fusion.14), channel_id=1, source_target_pairs={{0,16},{4,20},{8,24},{12,28},{16,0},{20,4},{24,8},{28,12},{1,17},{... | collective-permute-start | bytes 294920 | tf_op jit(solution)/shard_map/ppermute | solution.py:388
  380.6 3.9 collective-permute-start.30
  384.5 5.0 %collective-permute-start.31 = (f32[7680]{0:T(1024)S(1)}, f32[7680]{0:T(1024)S(1)}, u32[]{:S(2)}, u32[]{:S(2)}) collective-permute-start(f32[7680]{0:T(1024)S(1)} %pad_maximum_fusion.5), channel_id=1, source_target_pairs={{0,4},{4,0},{8,12},{12,8},{16,20},{20,16},{24,28},{28,24},{1,5},{5... | collective-permute-start | bytes 92168 | tf_op jit(solution)/shard_map/ppermute | solution.py:388
  387.3 11.0 %collective-permute-start.39 = (bf16[256,384]{1,0:T(8,128)(2,1)S(1)}, bf16[256,384]{1,0:T(8,128)(2,1)S(1)}, u32[]{:S(2)}, u32[]{:S(2)}) collective-permute-start(bf16[256,384]{1,0:T(8,128)(2,1)S(1)} %pad_maximum_fusion.4), channel_id=1, source_target_pairs={{0,8},{4,12},{8,0},{12,4},{16,24},{20,28},{24,16},{28,20},{1,9},{5... | collective-permute-start | bytes 589832 | tf_op jit(solution)/shard_map/ppermute | solution.py:388
  389.5 6.5 %collective-permute-start.32 = (f32[7680]{0:T(1024)S(1)}, f32[7680]{0:T(1024)S(1)}, u32[]{:S(2)}, u32[]{:S(2)}) collective-permute-start(f32[7680]{0:T(1024)S(1)} %fusion.7), channel_id=1, source_target_pairs={{0,8},{4,12},{8,0},{12,4},{16,24},{20,28},{24,16},{28,20},{1,9},{5... | collective-permute-start | bytes 92168 | tf_op jit(solution)/shard_map/ppermute | solution.py:388
  392.0 10.0 %collective-permute-start.35 = (bf16[256,640]{1,0:T(8,128)(2,1)S(1)}, bf16[256,640]{1,0:T(8,128)(2,1)S(1)}, u32[]{:S(2)}, u32[]{:S(2)}) collective-permute-start(bf16[256,640]{1,0:T(8,128)(2,1)S(1)} %pad_maximum_fusion.3), channel_id=1, source_target_pairs={{0,8},{4,12},{8,0},{12,4},{16,24},{20,28},{24,16},{28,20},{1,9},{5... | collective-permute-start | bytes 983048 | tf_op jit(solution)/shard_map/ppermute | solution.py:388
  396.6 11.6 %collective-permute-start.33 = (f32[7680]{0:T(1024)}, f32[7680]{0:T(1024)}, u32[]{:S(2)}, u32[]{:S(2)}) collective-permute-start(f32[7680]{0:T(1024)} %add.211), channel_id=1, source_target_pairs={{0,16},{4,20},{8,24},{12,28},{16,0},{20,4},{24,8},{28,12},{1,17},{... | collective-permute-start | bytes 92168 | tf_op jit(solution)/shard_map/ppermute | solution.py:388
  398.5 11.7 %collective-permute-start.40 = (bf16[512,384]{1,0:T(8,128)(2,1)S(1)}, bf16[512,384]{1,0:T(8,128)(2,1)S(1)}, u32[]{:S(2)}, u32[]{:S(2)}) collective-permute-start(bf16[512,384]{1,0:T(8,128)(2,1)S(1)} %pad_maximum_fusion.2), channel_id=1, source_target_pairs={{0,4},{4,0},{8,12},{12,8},{16,20},{20,16},{24,28},{28,24},{1,5},{5... | collective-permute-start | bytes 1179656 | tf_op jit(solution)/shard_map/ppermute | solution.py:388
  402.2 18.2 %collective-permute-start.36 = (bf16[512,640]{1,0:T(8,128)(2,1)S(1)}, bf16[512,640]{1,0:T(8,128)(2,1)S(1)}, u32[]{:S(2)}, u32[]{:S(2)}) collective-permute-start(bf16[512,640]{1,0:T(8,128)(2,1)S(1)} %pad_maximum_fusion.1), channel_id=1, source_target_pairs={{0,4},{4,0},{8,12},{12,8},{16,20},{20,16},{24,28},{28,24},{1,5},{5... | collective-permute-start | bytes 1966088 | tf_op jit(solution)/shard_map/ppermute | solution.py:388
  (28 other events, 177.3 us)
Sparse Core Ops, SparseCore 0:
  171.0 88.2 reduce-scatter.1
  264.1 73.7 all-gather.1
